TPU v7x, 512 devices: a whole 4x8x8 slice. The times are simulated.
512 devices in a mesh: rep: 16 (over x, z_lo), shard: 32 (over y, z_hi, core).
Axes of the slice: x: 4, y: 8, z: 8 (z_hi: 2, z_lo: 4; z = z_hi * 4 + z_lo), core: 2. Of those that a mesh axis runs over, the one named last changes fastest.
Arguments:
- queries: bfloat16 [16, 4096, 2048], P('rep', 'shard'), may hold values from -6 to 6
- keys: bfloat16 [16, 4096, 256], P('rep', 'shard'), may hold values from -6 to 6
- values: bfloat16 [16, 4096, 256], P('rep', 'shard'), may hold values from -6 to 6
- segments: int32 [16, 4096], P('rep', 'shard'), may hold values from 0 to 63, never falling along the last dimension, each value on 1 to 512 neighbouring positions
- grad_output: bfloat16 [16, 4096, 1024], P('rep', 'shard'), may hold values from -0.125 to 0.125
Outputs:
- attention: bfloat16 [16, 4096, 2048], P('rep', 'shard')
- grad_weight: float32 [1024, 2048], P('shard')
Inputs may be any that keep to these rules, and one draw needn't show every extreme that they name: `segments`: document numbers never fall along a packed row; every document holds 1 to 512 positions and some document holds exactly 512.
All inputs are finite; a program needn't handle non-finite values.
Results may differ from a plain program's by a relative error of at most 0.015.
Values may be sent and summed in bfloat16 or wider, within the bound.
No kernel may reach another device: no remote copies, remote signals or barrier semaphores. Data moves between devices by JAX's collectives and lax.ppermute only.
A program may use at most 64 MiB of HBM per device.

v0:
```python
import jax
import jax.numpy as jnp
from jax import lax
from jax.sharding import PartitionSpec as P

HEADS = 16
KVH = 2
HD = 128
SPAN = 4


def shifted(value, axis, steps):
    count = lax.axis_size(axis)
    first, last = (max(0, -steps), min(count, count - steps))
    return lax.ppermute(value, axis, [(source, source + steps) for source in range(first, last)])


def absorb(state_now, block_data, first_row, q_heads, q_seg, q_pos):
    running_max, weight_sum, accumulated = state_now
    key_part, value_part, seg_part = block_data
    row_count = key_part.shape[1]
    key_heads = key_part[0].reshape(row_count, KVH, HD)
    value_heads = value_part[0].reshape(row_count, KVH, HD).astype(jnp.float32)
    k_pos = first_row + jnp.arange(row_count, dtype=jnp.int32)
    allowed = (
        (q_seg[:, None] == seg_part[0][None, :])
        & (k_pos[None, :] <= q_pos[:, None])
        & (k_pos[None, :] >= 0)
    )
    scores = jnp.einsum(
        "qhgd,khd->hgqk", q_heads, key_heads, preferred_element_type=jnp.float32
    ) * HD ** (-0.5)
    scores = jnp.where(allowed, scores, -1e30)
    new_max = jnp.maximum(running_max, jnp.max(scores, axis=-1))
    weights = jnp.where(allowed, jnp.exp(scores - new_max[..., None]), 0.0)
    rescale = jnp.exp(running_max - new_max)
    weight_sum = weight_sum * rescale + jnp.sum(weights, axis=-1)
    product = jnp.einsum("hgqk,khd->hgqd", weights, value_heads, precision=lax.Precision.HIGHEST)
    accumulated = accumulated * rescale[..., None] + product
    return (new_max, weight_sum, accumulated)


def maybe_absorb(state_now, block_data, first_row, q_heads, q_seg, q_pos):
    return absorb(state_now, block_data, first_row, q_heads, q_seg, q_pos)


def local(queries, keys, values, segments, grad_output):
    tok_rows = queries.shape[1]
    shard_index = lax.axis_index("shard")
    group_size = HEADS // KVH
    q_heads = queries[0].reshape(tok_rows, KVH, group_size, HD)
    q_seg = segments[0]
    q_pos = shard_index * tok_rows + jnp.arange(tok_rows, dtype=jnp.int32)
    state_now = (
        jnp.full((KVH, group_size, tok_rows), -1e30, jnp.float32),
        jnp.zeros((KVH, group_size, tok_rows), jnp.float32),
        jnp.zeros((KVH, group_size, tok_rows, HD), jnp.float32),
    )
    own_block = (keys, values, segments)
    state_now = maybe_absorb(state_now, own_block, shard_index * tok_rows, q_heads, q_seg, q_pos)
    for distance in range(1, SPAN + 1):
        moved = shifted((keys, values, segments), "shard", distance)
        state_now = maybe_absorb(
            state_now, moved, (shard_index - distance) * tok_rows, q_heads, q_seg, q_pos
        )
    running_max, weight_sum, accumulated = state_now
    mixed = accumulated / weight_sum[..., None]
    attn_rows = (
        jnp.transpose(mixed, (2, 0, 1, 3)).reshape(tok_rows, HEADS * HD).astype(jnp.bfloat16)
    )
    grad_rows_local = grad_output[0]
    partial_value = lax.dot_general(
        grad_rows_local, attn_rows, (((0,), (0,)), ((), ())), preferred_element_type=jnp.float32
    )
    row_share = lax.psum_scatter(
        partial_value.astype(jnp.bfloat16), "shard", scatter_dimension=0, tiled=True
    ).astype(jnp.float32)
    grad_weight = lax.psum(row_share, "rep")
    return (attn_rows[None], grad_weight)


def solution(mesh):
    placed = (
        P("rep", "shard", None),
        P("rep", "shard", None),
        P("rep", "shard", None),
        P("rep", "shard"),
        P("rep", "shard", None),
    )
    return jax.shard_map(
        local,
        mesh=mesh,
        in_specs=placed,
        out_specs=(P("rep", "shard", None), P("shard", None)),
        check_vma=False,
    )
```

profile of v0, /device:TPU:16, one launch (start us, length us, event | category | flops | bytes accessed | tf_op | source)
XLA Modules:
  0.0 354.2 jit_solution(11450698336824940740)
XLA Ops:
  7.2 0.0 copy-start
  7.2 0.0 reduce-scatter.4.cloned.1.call-start
  7.2 11.1 %collective-permute-start.3 = (s32[1,128]{1,0:T(1,128)}, s32[1,128]{1,0:T(1,128)S(1)}, u32[]{:S(2)}, u32[]{:S(2)}) collective-permute-start(s32[1,128]{1,0:T(1,128)} %param.8), channel_id=1, source_target_pairs={{0,2},{1,3},{2,4},{3,5},{4,6},{5,7},{6,8},{7,9},{8,10},{9,11},{10,... | collective-permute-start | bytes 1544 | tf_op jit(solution)/shard_map/ppermute | solution.py:15
  18.3 1.9 collective-permute-start
  20.2 3.5 collective-permute-start.9
  23.7 9.5 %collective-permute-start.6 = (s32[1,128]{1,0:T(1,128)}, s32[1,128]{1,0:T(1,128)S(1)}, u32[]{:S(2)}, u32[]{:S(2)}) collective-permute-start(s32[1,128]{1,0:T(1,128)} %param.8), channel_id=1, source_target_pairs={{0,3},{1,4},{2,5},{3,6},{4,7},{5,8},{6,9},{7,10},{8,11},{9,12},{10... | collective-permute-start | bytes 1544 | tf_op jit(solution)/shard_map/ppermute | solution.py:15
  33.2 1.6 copy.55
  34.8 2.6 collective-permute-start.10
  37.5 0.9 reshape_squeeze.33
  38.4 1.0 copy.94
  39.3 1.2 copy.105
  40.5 0.0 collective-permute-done.3
  40.5 1.9 collective-permute-start.7
  42.4 0.0 collective-permute-done
  42.4 2.6 collective-permute-start.4
  45.0 0.0 collective-permute-done.9
  45.0 2.0 collective-permute-start.1
  47.1 0.0 collective-permute-done.6
  47.1 7.7 %collective-permute-start.5 = (bf16[1,128,256]{2,1,0:T(8,128)(2,1)}, bf16[1,128,256]{2,1,0:T(8,128)(2,1)}, u32[]{:S(2)}, u32[]{:S(2)}) collective-permute-start(bf16[1,128,256]{2,1,0:T(8,128)(2,1)} %param.7), channel_id=1, source_target_pairs={{0,2},{1,3},{2,4},{3,5},{4,6},{5,7},{6,8},{7,9},{8,10},{9,11},{10,... | collective-permute-start | bytes 196616 | tf_op jit(solution)/shard_map/ppermute | solution.py:15
  54.8 1.1 and_and_fusion.2
  55.8 0.3 fusion.69
  56.2 0.8 collective-permute-done.1
  56.9 1.9 collective-permute-start.2
  58.9 0.4 fusion.68
  59.2 0.0 collective-permute-done.4
  59.2 2.6 collective-permute-start.11
  61.8 0.4 fusion.67
  62.2 0.0 collective-permute-done.7
  62.2 8.2 %collective-permute-start.8 = (bf16[1,128,256]{2,1,0:T(8,128)(2,1)}, bf16[1,128,256]{2,1,0:T(8,128)(2,1)}, u32[]{:S(2)}, u32[]{:S(2)}) collective-permute-start(bf16[1,128,256]{2,1,0:T(8,128)(2,1)} %param.7), channel_id=1, source_target_pairs={{0,3},{1,4},{2,5},{3,6},{4,7},{5,8},{6,9},{7,10},{8,11},{9,12},{10... | collective-permute-start | bytes 196616 | tf_op jit(solution)/shard_map/ppermute | solution.py:15
  70.5 0.4 fusion.66
  70.8 0.0 collective-permute-done.10
  70.8 1.2 fusion.65
  72.1 0.0 copy-start.1
  72.1 0.0 copy-start.3
  72.1 0.0 copy-start.2
  72.1 0.9 copy-done.1
  73.0 0.2 fusion.25
  73.2 0.0 copy-done.3
  73.3 0.4 fusion.23
  73.7 0.4 fusion.21
  74.1 0.6 bitcast_add_fusion
  74.7 1.9 fusion.9
  76.6 0.0 copy-done.2
  76.6 0.0 collective-permute-done.2
  76.6 0.9 copy.58
  77.5 3.1 fusion.7
  80.7 0.0 collective-permute-done.5
  80.7 1.0 copy.63
  81.6 2.1 fusion.5
  83.7 0.0 collective-permute-done.8
  83.7 0.9 copy.68
  84.7 1.5 fusion.3
  86.2 0.0 collective-permute-done.11
  86.2 0.9 copy.73
  87.2 0.0 copy-done.4
  87.2 2.1 fusion.20
  89.3 3.2 convert_bitcast_fusion
  92.5 6.5 %copy.103 = bf16[1024,2048]{1,0:T(8,128)(2,1)} copy(bf16[1024,2048]{0,1:T(8,128)(2,1)} %convert_bitcast_fusion) | data formatting | bytes 8388608
  99.0 0.0 reduce-scatter.4.cloned.1.call-update
  99.0 1.0 copy.75
  100.0 146.4 %reduce-scatter.4.cloned.1.call-done = bf16[32,2048]{1,0:T(8,128)(2,1)} async-done(((bf16[1024,2048]{1,0:T(8,128)(2,1)}), bf16[32,2048]{1,0:T(8,128)(2,1)}) %reduce-scatter.4.cloned.1.call-update) | async-done | bytes 131088
  246.5 1.2 copy.104
  247.6 98.7 %all-reduce.1 = f32[32,2048]{0,1:T(8,128)S(1)} all-reduce(bf16[32,2048]{0,1:T(8,128)(2,1)S(1)} %copy.104), channel_id=1, replica_groups=mesh['rep'=16,'shard'=32] {'rep'}, use_global_device_ids=true, to_apply=%region_11.12 | all-reduce | flops 65536 | bytes 393216 | tf_op jit(solution)/shard_map/psum | solution.py:78
  346.3 1.0 copy.76
  (15 shorter events, 0.1 us)
Async XLA Ops:
  7.2 82.1 %copy-start = (bf16[1,128,1024]{2,1,0:T(8,128)(2,1)S(1)}, bf16[1,128,1024]{2,1,0:T(8,128)(2,1)}, u32[]{:S(2)}) copy-start(bf16[1,128,1024]{2,1,0:T(8,128)(2,1)} %param.9) | copy-start | bytes 786436
  7.2 239.3 %reduce-scatter.4.cloned.1.call-start = ((), (), s32[]{:S(2)}) async-start(), calls=%async_computation.1 | async-start | bytes 4325376
  7.2 33.3 %collective-permute-start.3 = (s32[1,128]{1,0:T(1,128)}, s32[1,128]{1,0:T(1,128)S(1)}, u32[]{:S(2)}, u32[]{:S(2)}) collective-permute-start(s32[1,128]{1,0:T(1,128)} %param.8), channel_id=1, source_target_pairs={{0,2},{1,3},{2,4},{3,5},{4,6},{5,7},{6,8},{7,9},{8,10},{9,11},{10,... | collective-permute-start | bytes 1544 | tf_op jit(solution)/shard_map/ppermute | solution.py:15
  18.3 24.2 %collective-permute-start = (s32[1,128]{1,0:T(1,128)}, s32[1,128]{1,0:T(1,128)S(1)}, u32[]{:S(2)}, u32[]{:S(2)}) collective-permute-start(s32[1,128]{1,0:T(1,128)} %param.8), channel_id=1, source_target_pairs={{0,1},{1,2},{2,3},{3,4},{4,5},{5,6},{6,7},{7,8},{8,9},{9,10},{10,1... | collective-permute-start | bytes 1544 | tf_op jit(solution)/shard_map/ppermute | solution.py:15
  20.2 24.8 %collective-permute-start.9 = (s32[1,128]{1,0:T(1,128)}, s32[1,128]{1,0:T(1,128)S(1)}, u32[]{:S(2)}, u32[]{:S(2)}) collective-permute-start(s32[1,128]{1,0:T(1,128)} %param.8), channel_id=1, source_target_pairs={{0,4},{1,5},{2,6},{3,7},{4,8},{5,9},{6,10},{7,11},{8,12},{9,13},{1... | collective-permute-start | bytes 1544 | tf_op jit(solution)/shard_map/ppermute | solution.py:15
  23.7 23.4 %collective-permute-start.6 = (s32[1,128]{1,0:T(1,128)}, s32[1,128]{1,0:T(1,128)S(1)}, u32[]{:S(2)}, u32[]{:S(2)}) collective-permute-start(s32[1,128]{1,0:T(1,128)} %param.8), channel_id=1, source_target_pairs={{0,3},{1,4},{2,5},{3,6},{4,7},{5,8},{6,9},{7,10},{8,11},{9,12},{10... | collective-permute-start | bytes 1544 | tf_op jit(solution)/shard_map/ppermute | solution.py:15
  34.8 36.0 %collective-permute-start.10 = (bf16[1,128,256]{1,2,0:T(8,128)(2,1)}, bf16[1,128,256]{1,2,0:T(8,128)(2,1)}, u32[]{:S(2)}, u32[]{:S(2)}) collective-permute-start(bf16[1,128,256]{1,2,0:T(8,128)(2,1)} %copy.55), channel_id=1, source_target_pairs={{0,4},{1,5},{2,6},{3,7},{4,8},{5,9},{6,10},{7,11},{8,12},{9,13},{1... | collective-permute-start | bytes 196616 | tf_op jit(solution)/shard_map/ppermute | solution.py:15
  40.5 21.7 %collective-permute-start.7 = (bf16[1,128,256]{1,2,0:T(8,128)(2,1)}, bf16[1,128,256]{1,2,0:T(8,128)(2,1)S(1)}, u32[]{:S(2)}, u32[]{:S(2)}) collective-permute-start(bf16[1,128,256]{1,2,0:T(8,128)(2,1)} %copy.55), channel_id=1, source_target_pairs={{0,3},{1,4},{2,5},{3,6},{4,7},{5,8},{6,9},{7,10},{8,11},{9,12},{10... | collective-permute-start | bytes 196616 | tf_op jit(solution)/shard_map/ppermute | solution.py:15
  42.4 16.8 %collective-permute-start.4 = (bf16[1,128,256]{1,2,0:T(8,128)(2,1)}, bf16[1,128,256]{1,2,0:T(8,128)(2,1)S(1)}, u32[]{:S(2)}, u32[]{:S(2)}) collective-permute-start(bf16[1,128,256]{1,2,0:T(8,128)(2,1)} %copy.55), channel_id=1, source_target_pairs={{0,2},{1,3},{2,4},{3,5},{4,6},{5,7},{6,8},{7,9},{8,10},{9,11},{10,... | collective-permute-start | bytes 196616 | tf_op jit(solution)/shard_map/ppermute | solution.py:15
  45.0 11.9 %collective-permute-start.1 = (bf16[1,128,256]{1,2,0:T(8,128)(2,1)}, bf16[1,128,256]{1,2,0:T(8,128)(2,1)S(1)}, u32[]{:S(2)}, u32[]{:S(2)}) collective-permute-start(bf16[1,128,256]{1,2,0:T(8,128)(2,1)} %copy.55), channel_id=1, source_target_pairs={{0,1},{1,2},{2,3},{3,4},{4,5},{5,6},{6,7},{7,8},{8,9},{9,10},{10,1... | collective-permute-start | bytes 196616 | tf_op jit(solution)/shard_map/ppermute | solution.py:15
  47.1 33.6 %collective-permute-start.5 = (bf16[1,128,256]{2,1,0:T(8,128)(2,1)}, bf16[1,128,256]{2,1,0:T(8,128)(2,1)}, u32[]{:S(2)}, u32[]{:S(2)}) collective-permute-start(bf16[1,128,256]{2,1,0:T(8,128)(2,1)} %param.7), channel_id=1, source_target_pairs={{0,2},{1,3},{2,4},{3,5},{4,6},{5,7},{6,8},{7,9},{8,10},{9,11},{10,... | collective-permute-start | bytes 196616 | tf_op jit(solution)/shard_map/ppermute | solution.py:15
  56.9 19.6 %collective-permute-start.2 = (bf16[1,128,256]{2,1,0:T(8,128)(2,1)}, bf16[1,128,256]{2,1,0:T(8,128)(2,1)}, u32[]{:S(2)}, u32[]{:S(2)}) collective-permute-start(bf16[1,128,256]{2,1,0:T(8,128)(2,1)} %param.7), channel_id=1, source_target_pairs={{0,1},{1,2},{2,3},{3,4},{4,5},{5,6},{6,7},{7,8},{8,9},{9,10},{10,1... | collective-permute-start | bytes 196616 | tf_op jit(solution)/shard_map/ppermute | solution.py:15
  59.2 27.0 %collective-permute-start.11 = (bf16[1,128,256]{2,1,0:T(8,128)(2,1)}, bf16[1,128,256]{2,1,0:T(8,128)(2,1)}, u32[]{:S(2)}, u32[]{:S(2)}) collective-permute-start(bf16[1,128,256]{2,1,0:T(8,128)(2,1)} %param.7), channel_id=1, source_target_pairs={{0,4},{1,5},{2,6},{3,7},{4,8},{5,9},{6,10},{7,11},{8,12},{9,13},{1... | collective-permute-start | bytes 196616 | tf_op jit(solution)/shard_map/ppermute | solution.py:15
  62.2 21.5 %collective-permute-start.8 = (bf16[1,128,256]{2,1,0:T(8,128)(2,1)}, bf16[1,128,256]{2,1,0:T(8,128)(2,1)}, u32[]{:S(2)}, u32[]{:S(2)}) collective-permute-start(bf16[1,128,256]{2,1,0:T(8,128)(2,1)} %param.7), channel_id=1, source_target_pairs={{0,3},{1,4},{2,5},{3,6},{4,7},{5,8},{6,9},{7,10},{8,11},{9,12},{10... | collective-permute-start | bytes 196616 | tf_op jit(solution)/shard_map/ppermute | solution.py:15
  72.1 1.0 copy-start.1
  72.1 1.2 copy-start.3
  72.1 4.5 %copy-start.2 = (f32[2,8,128]{2,1,0:T(8,128)}, f32[2,8,128]{2,1,0:T(8,128)S(1)}, u32[]{:S(2)}) copy-start(f32[2,8,128]{2,1,0:T(8,128)S(1)} %get-tuple-element.15) | copy-start | bytes 24580
  80.6 6.5 %copy-start.4 = (f32[2,8,128]{2,1,0:T(8,128)S(1)}, f32[2,8,128]{2,1,0:T(8,128)}, u32[]{:S(2)}) copy-start(f32[2,8,128]{2,1,0:T(8,128)} %copy-done.3) | copy-start | bytes 24580
  80.6 6.5 %copy-start.5 = (f32[128,2,8]{0,2,1:T(8,128)S(1)}, f32[128,2,8]{0,2,1:T(8,128)}, u32[]{:S(2)}) copy-start(f32[128,2,8]{0,2,1:T(8,128)} %get-tuple-element.8) | copy-start | bytes 24580
Sparse Core Ops, SparseCore 0:
  99.1 147.2 reduce-scatter.3
where the time goes:
time: 355 us; the launch traced here: 354 us
  waiting for transfers between devices  147 us (41%)
  blocking collectives  98.7 us (28%)
  starting transfers between devices  55.5 us (16%)
  local copies, waits for them, and re-layouts  19 us (5%)
  matrix products  16.5 us (5%)
  between operations  14.5 us (4%)
    unnamed x2, waiting for transfers between devices  146 us
    psum x1, blocking collectives, local(): grad_weight = lax.psum(row_share, 'rep')  98.7 us
    ppermute x12, starting transfers between devices, shifted(): lax.ppermute(value, axis, [(source, source + steps) for source in range(f...  55.5 us
    unnamed x18, local copies, waits for them, and re-layouts  13.4 us
    dot_general x5, matrix products, absorb(): jnp.einsum('hgqk,khd->hgqd', weights, value_heads, precision=lax.Precisio...  10.6 us
  transfers between devices with their start and end apart: 13, of which 2 were waited for; matrix products, arithmetic and copies ran while one was open for 6% of the time, Pallas kernels for 0%

commit v1 on v0

v1 whole, which is shorter than its diff:
```python
import jax
import jax.numpy as jnp
import numpy as np
from jax import lax
from jax.experimental import pallas as pl
from jax.experimental.pallas import tpu as pltpu
from jax.sharding import Mesh
from jax.sharding import PartitionSpec as P

HEADS = 16
KVH = 2
HD = 128
TOK = 128
D_WIN = 1024
SPAN = 4
N_SHARD = 32
N_REP = 16
KV = KVH * HD
PAY_ROWS = TOK + 8
NEG = -1e30
EXP2_SCALE = (HD**-0.5) * 1.4426950408889634

AXES = ("x", "zlh", "zll", "shard")
REP = ("x", "zlh", "zll")
GROUP = ("x", "zll")
N_GROUP = 8
REST = ("shard", "zlh")
N_REST = 64
STACK = 4


def params(mib):
    return pltpu.CompilerParams(vmem_limit_bytes=mib << 20)


def vmem_specs(count):
    return [pl.BlockSpec(memory_space=pltpu.VMEM)] * count


def pack_kernel(key_ref, value_ref, seg_ref, grad_ref, pay_ref, grad_t_ref):
    pay_ref[:TOK, :KV] = key_ref[0]
    pay_ref[:TOK, KV:] = value_ref[0]
    seg = jnp.broadcast_to(seg_ref[...].astype(jnp.float32), (8, TOK))
    pay_ref[TOK:, :TOK] = seg.astype(jnp.bfloat16)
    pay_ref[TOK:, TOK:] = jnp.zeros((8, 2 * KV - TOK), jnp.bfloat16)
    grad_t_ref[...] = jnp.transpose(grad_ref[0].astype(jnp.float32)).astype(jnp.bfloat16)


def pack(keys, values, segments, grad_output):
    return pl.pallas_call(
        pack_kernel,
        out_shape=(
            jax.ShapeDtypeStruct((PAY_ROWS, 2 * KV), jnp.bfloat16),
            jax.ShapeDtypeStruct((D_WIN, TOK), jnp.bfloat16),
        ),
        in_specs=vmem_specs(4),
        out_specs=tuple(vmem_specs(2)),
        name="pack",
        compiler_params=params(8),
        cost_estimate=pl.CostEstimate(flops=0, bytes_accessed=1 << 20, transcendentals=0),
    )(keys, values, segments, grad_output)


def attend_kernel(index_ref, query_ref, *refs):
    pays, (out_ref, swap_ref, bias_ref) = refs[: SPAN + 1], refs[SPAN + 1 :]
    index = index_ref[0]
    own_row = jnp.broadcast_to(pays[0][TOK : TOK + 1, :TOK].astype(jnp.float32), (TOK, TOK))
    q_seg = jnp.transpose(own_row)
    q_at = lax.broadcasted_iota(jnp.int32, (TOK, TOK), 0)
    k_at = lax.broadcasted_iota(jnp.int32, (TOK, TOK), 1)
    for step in range(SPAN + 1):
        k_seg = jnp.broadcast_to(pays[step][TOK : TOK + 1, :TOK].astype(jnp.float32), (TOK, TOK))
        allowed = q_seg == k_seg
        if step == 0:
            allowed = allowed & (k_at <= q_at)
        else:
            allowed = allowed & (k_at + (index - step) * TOK >= 0)
        bias_ref[:, step * TOK : (step + 1) * TOK] = jnp.where(allowed, 0.0, NEG)
    ones = jnp.ones((TOK, HD), jnp.bfloat16)
    for first in range(0, HEADS, STACK):
        kv_head = first // (HEADS // KVH)
        k_cols = slice(kv_head * HD, (kv_head + 1) * HD)
        v_cols = slice(KV + kv_head * HD, KV + (kv_head + 1) * HD)
        query = jnp.concatenate(
            [query_ref[0, :, h * HD : (h + 1) * HD] for h in range(first, first + STACK)], axis=0
        )
        key = jnp.concatenate([pay[:TOK, k_cols] for pay in pays], axis=0)
        scores = lax.dot_general(
            query, key, (((1,), (1,)), ((), ())), preferred_element_type=jnp.float32
        )
        bias = bias_ref[...]
        scores = scores.reshape(STACK, TOK, (SPAN + 1) * TOK) + bias[None]
        largest = jnp.max(scores, axis=-1, keepdims=True)
        weights = jnp.exp2((scores - largest) * EXP2_SCALE).astype(jnp.bfloat16)
        weights = weights.reshape(STACK * TOK, (SPAN + 1) * TOK)
        value = jnp.concatenate(
            [jnp.concatenate([pay[:TOK, v_cols], ones], axis=1) for pay in pays], axis=0
        )
        mixed = jnp.dot(weights, value, preferred_element_type=jnp.float32)
        result = (mixed[:, :HD] / mixed[:, HD:]).astype(jnp.bfloat16)
        for h in range(STACK):
            head = first + h
            rows = result[h * TOK : (h + 1) * TOK]
            out_ref[0, :, head * HD : (head + 1) * HD] = rows
            swap_ref[head // 2, :, (head % 2) * HD : (head % 2 + 1) * HD] = rows


def attend(index, queries, pays):
    return pl.pallas_call(
        attend_kernel,
        out_shape=(
            jax.ShapeDtypeStruct((1, TOK, HEADS * HD), jnp.bfloat16),
            jax.ShapeDtypeStruct((N_GROUP, TOK, 2 * HD), jnp.bfloat16),
        ),
        in_specs=[pl.BlockSpec(memory_space=pltpu.SMEM)] + vmem_specs(SPAN + 2),
        out_specs=tuple(vmem_specs(2)),
        scratch_shapes=[pltpu.VMEM((TOK, (SPAN + 1) * TOK), jnp.float32)],
        name="attend",
        compiler_params=params(32),
        cost_estimate=pl.CostEstimate(
            flops=700_000_000, bytes_accessed=3 << 20, transcendentals=1_310_720
        ),
    )(index, queries, *pays)


def term_kernel(grad_t_ref, mixed_ref, out_ref):
    grad_t = jnp.concatenate([grad_t_ref[i] for i in range(N_GROUP)], axis=1)
    mixed = mixed_ref[...].reshape(N_GROUP * TOK, 2 * HD)
    term = jnp.dot(grad_t, mixed, preferred_element_type=jnp.float32).astype(jnp.bfloat16)
    term = term.reshape(N_SHARD, D_WIN // N_SHARD, 2 * HD)
    for half in range(2):
        out_ref[:, half] = term[:, :, half * HD : (half + 1) * HD]


def weight_term(grad_t, mixed):
    return pl.pallas_call(
        term_kernel,
        out_shape=jax.ShapeDtypeStruct((N_SHARD, 2, D_WIN // N_SHARD, HD), jnp.bfloat16),
        in_specs=vmem_specs(2),
        out_specs=vmem_specs(1)[0],
        name="weight_term",
        compiler_params=params(24),
        cost_estimate=pl.CostEstimate(
            flops=2 * D_WIN * N_GROUP * TOK * 2 * HD, bytes_accessed=3 << 20, transcendentals=0
        ),
    )(grad_t, mixed)


def total_kernel(terms_ref, out_ref):
    total = jnp.sum(terms_ref[...].astype(jnp.float32), axis=0).astype(jnp.bfloat16)
    out_ref[...] = jnp.broadcast_to(total[None], out_ref.shape)


def total(terms):
    return pl.pallas_call(
        total_kernel,
        out_shape=jax.ShapeDtypeStruct((N_REP, D_WIN // N_SHARD, HD), jnp.bfloat16),
        in_specs=vmem_specs(1),
        out_specs=vmem_specs(1)[0],
        name="total",
        compiler_params=params(8),
    )(terms)


def assemble_kernel(parts_ref, out_ref):
    for x in range(4):
        for zlh in range(2):
            for zll in range(2):
                head = (x * 2 + zll) * 2 + zlh
                part = parts_ref[x * 4 + zlh * 2 + zll]
                out_ref[:, head * HD : (head + 1) * HD] = part.astype(jnp.float32)


def assemble(parts):
    return pl.pallas_call(
        assemble_kernel,
        out_shape=jax.ShapeDtypeStruct((D_WIN // N_SHARD, HEADS * HD), jnp.float32),
        in_specs=vmem_specs(1),
        out_specs=vmem_specs(1)[0],
        name="assemble",
        compiler_params=params(8),
    )(parts)


def shifted(value, steps):
    count = lax.axis_size("shard")
    return lax.ppermute(value, "shard", [(s, s + steps) for s in range(count - steps)])


def local(queries, keys, values, segments, grad_output):
    pay, grad_t = pack(keys, values, segments, grad_output)
    grads = lax.all_gather(grad_t, GROUP, axis=0, tiled=False)
    pays = [pay] + [shifted(pay, step) for step in range(1, SPAN + 1)]
    index = lax.axis_index("shard").reshape(1).astype(jnp.int32)
    attention, swap = attend(index, queries, pays)
    mixed = lax.all_to_all(swap, GROUP, 0, 0, tiled=True)
    term = weight_term(grads.reshape(N_GROUP, D_WIN, TOK), mixed)
    terms = lax.all_to_all(
        term.reshape(N_REST, D_WIN // N_SHARD, HD), REST, 0, 0, tiled=True
    )
    parts = lax.all_to_all(total(terms), REP, 0, 0, tiled=True)
    return attention, assemble(parts)


def solution(mesh):
    fine = Mesh(np.asarray(mesh.devices).reshape(4, 2, 2, N_SHARD), AXES)
    row = P(REP, "shard", None)
    return jax.shard_map(
        local,
        mesh=fine,
        in_specs=(row, row, row, P(REP, "shard"), row),
        out_specs=(row, P("shard", None)),
        check_vma=False,
    )
```

time: 355 us -> 140 us (0.39)
  the two profiles are of different devices: /device:TPU:16 before, /device:TPU:1 now
where the time goes in v1:
time: 140 us; the launch traced here: 139 us
  blocking collectives  63.3 us (45%)
  waiting for transfers between devices  29.5 us (21%)
  starting transfers between devices  20.7 us (15%)
  between operations  14.1 us (10%)
  local copies, waits for them, and re-layouts  5.91 us (4%)
  Pallas kernels  5.65 us (4%)
    all_to_all x1, blocking collectives, local(): lax.all_to_all(term.reshape(N_REST, D_WIN // N_SHARD, HD), REST, 0, 0, ti...  32 us
    all_gather x1, waiting for transfers between devices, local(): grads = lax.all_gather(grad_t, GROUP, axis=0, tiled=False)  27.5 us
    ppermute x4, starting transfers between devices, shifted(): lax.ppermute(value, 'shard', [(s, s + steps) for s in range(count - steps)])  20.6 us
    all_to_all x1, blocking collectives, local(): mixed = lax.all_to_all(swap, GROUP, 0, 0, tiled=True)  18.8 us
    all_to_all x1, blocking collectives, local(): parts = lax.all_to_all(total(terms), REP, 0, 0, tiled=True)  12.5 us
    unnamed x12, local copies, waits for them, and re-layouts  5.91 us
    pallas_call x1, Pallas kernels, attend(): pl.pallas_call(attend_kernel, out_shape=(jax.ShapeDtypeStruct((1, TOK, HE...  3.29 us
  transfers between devices with their start and end apart: 5, of which 2 were waited for; matrix products, arithmetic and copies ran while one was open for 0% of the time, Pallas kernels for 2%

profile of v1, /device:TPU:1, one launch (start us, length us, event | category | flops | bytes accessed | tf_op | source)
XLA Modules:
  0.0 139.1 jit_solution(16076870739179162854)
XLA Ops:
  7.2 0.0 all-gather.3.cloned.1.call-start
  7.2 0.0 copy-start.1
  7.2 0.9 copy-done.1
  8.2 0.0 copy-start.2
  8.2 0.8 copy-done.2
  9.0 0.0 copy-start.3
  9.0 0.8 copy-done.3
  9.8 0.0 copy-start.4
  9.8 0.7 copy-done.4
  10.5 0.8 pack.1
  11.3 0.0 all-gather.3.cloned.1.call-update
  11.4 12.0 %collective-permute-start = (bf16[136,512]{1,0:T(8,128)(2,1)S(1)}, bf16[136,512]{1,0:T(8,128)(2,1)S(1)}, u32[]{:S(2)}, u32[]{:S(2)}) collective-permute-start(bf16[136,512]{1,0:T(8,128)(2,1)S(1)} %get-tuple-element.6.refs_0_), channel_id=1, source_target_pairs={{0,1},{1,2},{2,3},{3,4},{4,5},{5,6},{6,7},{7,8},{8,9},{9,10},{10,1... | collective-permute-start | bytes 417800 | tf_op jit(solution)/shard_map/ppermute | solution.py:187
  23.4 1.4 collective-permute-start.1
  24.8 4.0 %collective-permute-start.2 = (bf16[136,512]{1,0:T(8,128)(2,1)S(1)}, bf16[136,512]{1,0:T(8,128)(2,1)S(1)}, u32[]{:S(2)}, u32[]{:S(2)}) collective-permute-start(bf16[136,512]{1,0:T(8,128)(2,1)S(1)} %get-tuple-element.6.refs_0_), channel_id=1, source_target_pairs={{0,3},{1,4},{2,5},{3,6},{4,7},{5,8},{6,9},{7,10},{8,11},{9,12},{10... | collective-permute-start | bytes 417800 | tf_op jit(solution)/shard_map/ppermute | solution.py:187
  28.8 3.2 %collective-permute-start.3 = (bf16[136,512]{1,0:T(8,128)(2,1)S(1)}, bf16[136,512]{1,0:T(8,128)(2,1)S(1)}, u32[]{:S(2)}, u32[]{:S(2)}) collective-permute-start(bf16[136,512]{1,0:T(8,128)(2,1)S(1)} %get-tuple-element.6.refs_0_), channel_id=1, source_target_pairs={{0,4},{1,5},{2,6},{3,7},{4,8},{5,9},{6,10},{7,11},{8,12},{9,13},{1... | collective-permute-start | bytes 417800 | tf_op jit(solution)/shard_map/ppermute | solution.py:187
  32.0 0.0 collective-permute-done.refs_1_
  32.0 0.0 collective-permute-done.1.refs_2_
  32.0 0.0 collective-permute-done.2.refs_3_
  32.1 2.0 %collective-permute-done.3.refs_4_ = bf16[136,512]{1,0:T(8,128)(2,1)S(1)} collective-permute-done((bf16[136,512]{1,0:T(8,128)(2,1)S(1)}, bf16[136,512]{1,0:T(8,128)(2,1)S(1)}, u32[]{:S(2)}, u32[]{:S(2)}) %collective-permute-start.3) | collective-permute-done | bytes 139296 | tf_op jit(solution)/shard_map/ppermute | solution.py:187
  34.0 0.0 copy-start.5
  34.0 1.0 copy-done.5
  35.1 3.3 %attend.1 = (bf16[1,128,2048]{2,1,0:T(8,128)(2,1)}, bf16[8,128,256]{2,1,0:T(8,128)(2,1)S(1)}) custom-call(s32[1]{0:T(128)} %bitcast.index_ref, bf16[1,128,2048]{2,1,0:T(8,128)(2,1)S(1)} %copy-done.5, bf16[136,512]{1,0:T(8,128)(2,1)S(1)} %get-tuple-element.6.refs_0_, bf16[136,512]{1,0:T(8,128)(2,1)S(1)} %collective-permute-done.refs_1_, ...), custom_call_target="tpu_custom_call" | custom-call | flops 700000000 | bytes 3145728 | tf_op jit(solution)/shard_map/attend/pallas_call | solution.py:109
  38.4 18.8 %all_to_all.15.mixed_ref = bf16[8,128,256]{2,1,0:T(8,128)(2,1)S(1)} all-to-all(bf16[8,128,256]{2,1,0:T(8,128)(2,1)S(1)} %get-tuple-element.9), channel_id=1, replica_groups=mesh['x'=4,'zlh'=2,'zll'=2,'shard'=32] {'x','zll'}, dimensions={0} | all-to-all | bytes 1048576 | tf_op jit(solution)/shard_map/all_to_all | solution.py:196
  57.1 27.5 %all-gather.3.cloned.1.call-done = bf16[8192,128]{1,0:T(8,128)(2,1)} async-done(((bf16[1024,128]{1,0:T(8,128)(2,1)}), bf16[8192,128]{1,0:T(8,128)(2,1)}) %all-gather.3.cloned.1.call-update) | async-done | bytes 2097168 | tf_op jit(solution)/shard_map/all_gather | solution.py:192
  84.6 0.0 copy-start
  84.6 1.6 %copy-done = bf16[8192,128]{1,0:T(8,128)(2,1)S(1)} copy-done((bf16[8192,128]{1,0:T(8,128)(2,1)S(1)}, bf16[8192,128]{1,0:T(8,128)(2,1)}, u32[]{:S(2)}) %copy-start) | copy-done | bytes 2097176
  86.2 0.7 weight_term.1
  86.9 32.0 %all_to_all.16.terms_ref = bf16[64,32,128]{2,1,0:T(8,128)(2,1)S(1)} all-to-all(bf16[64,32,128]{2,1,0:T(8,128)(2,1)S(1)} %bitcast.4), channel_id=1, replica_groups=mesh['x'=4,'zlh'=2,'zll'=2,'shard'=32] {'shard','zlh'}, dimensions={0} | all-to-all | bytes 1048576 | tf_op jit(solution)/shard_map/all_to_all | solution.py:198
  118.9 0.1 total.1
  119.0 12.5 %all_to_all.17.parts_ref = bf16[16,32,128]{2,1,0:T(8,128)(2,1)S(1)} all-to-all(bf16[16,32,128]{2,1,0:T(8,128)(2,1)S(1)} %total.1), channel_id=1, replica_groups=mesh['x'=4,'zlh'=2,'zll'=2,'shard'=32] {'x','zlh','zll'}, dimensions={0} | all-to-all | bytes 262144 | tf_op jit(solution)/shard_map/all_to_all | solution.py:201
  131.5 0.7 assemble.1
Async XLA Ops:
  7.2 77.4 %all-gather.3.cloned.1.call-start = ((), (), s32[]{:S(2)}) async-start(), calls=%async_computation.3 | async-start | bytes 2359296 | tf_op jit(solution)/shard_map/all_gather | solution.py:192
  7.2 1.0 copy-start.1
  8.2 0.8 copy-start.2
  9.0 0.8 copy-start.3
  9.8 0.7 copy-start.4
  11.4 20.7 %collective-permute-start = (bf16[136,512]{1,0:T(8,128)(2,1)S(1)}, bf16[136,512]{1,0:T(8,128)(2,1)S(1)}, u32[]{:S(2)}, u32[]{:S(2)}) collective-permute-start(bf16[136,512]{1,0:T(8,128)(2,1)S(1)} %get-tuple-element.6.refs_0_), channel_id=1, source_target_pairs={{0,1},{1,2},{2,3},{3,4},{4,5},{5,6},{6,7},{7,8},{8,9},{9,10},{10,1... | collective-permute-start | bytes 417800 | tf_op jit(solution)/shard_map/ppermute | solution.py:187
  23.4 8.7 %collective-permute-start.1 = (bf16[136,512]{1,0:T(8,128)(2,1)S(1)}, bf16[136,512]{1,0:T(8,128)(2,1)S(1)}, u32[]{:S(2)}, u32[]{:S(2)}) collective-permute-start(bf16[136,512]{1,0:T(8,128)(2,1)S(1)} %get-tuple-element.6.refs_0_), channel_id=1, source_target_pairs={{0,2},{1,3},{2,4},{3,5},{4,6},{5,7},{6,8},{7,9},{8,10},{9,11},{10,... | collective-permute-start | bytes 417800 | tf_op jit(solution)/shard_map/ppermute | solution.py:187
  24.8 7.3 %collective-permute-start.2 = (bf16[136,512]{1,0:T(8,128)(2,1)S(1)}, bf16[136,512]{1,0:T(8,128)(2,1)S(1)}, u32[]{:S(2)}, u32[]{:S(2)}) collective-permute-start(bf16[136,512]{1,0:T(8,128)(2,1)S(1)} %get-tuple-element.6.refs_0_), channel_id=1, source_target_pairs={{0,3},{1,4},{2,5},{3,6},{4,7},{5,8},{6,9},{7,10},{8,11},{9,12},{10... | collective-permute-start | bytes 417800 | tf_op jit(solution)/shard_map/ppermute | solution.py:187
  28.8 5.2 %collective-permute-start.3 = (bf16[136,512]{1,0:T(8,128)(2,1)S(1)}, bf16[136,512]{1,0:T(8,128)(2,1)S(1)}, u32[]{:S(2)}, u32[]{:S(2)}) collective-permute-start(bf16[136,512]{1,0:T(8,128)(2,1)S(1)} %get-tuple-element.6.refs_0_), channel_id=1, source_target_pairs={{0,4},{1,5},{2,6},{3,7},{4,8},{5,9},{6,10},{7,11},{8,12},{9,13},{1... | collective-permute-start | bytes 417800 | tf_op jit(solution)/shard_map/ppermute | solution.py:187
  34.0 1.0 copy-start.5
  84.6 1.6 %copy-start = (bf16[8192,128]{1,0:T(8,128)(2,1)S(1)}, bf16[8192,128]{1,0:T(8,128)(2,1)}, u32[]{:S(2)}) copy-start(bf16[8192,128]{1,0:T(8,128)(2,1)} %all-gather.3.cloned.1.call-done) | copy-start | bytes 6291460
Sparse Core Ops, SparseCore 0:
  11.5 73.0 all-gather.2

commit v2 on v1

--- a/solution.py
+++ b/solution.py
@@ -6,6 +6,7 @@
 from jax.experimental.pallas import tpu as pltpu
 from jax.sharding import Mesh
 from jax.sharding import PartitionSpec as P
+
 
 HEADS = 16
 KVH = 2
@@ -20,12 +21,18 @@
 NEG = -1e30
 EXP2_SCALE = (HD**-0.5) * 1.4426950408889634
 
-AXES = ("x", "zlh", "zll", "shard")
+AXES = ("x", "zlh", "zll", "yz", "core")
+SIZES = (4, 2, 2, 16, 2)
 REP = ("x", "zlh", "zll")
+SHARD = ("yz", "core")
 GROUP = ("x", "zll")
+N_X = 4
 N_GROUP = 8
-REST = ("shard", "zlh")
-N_REST = 64
+REST = ("yz", "zlh")
+N_YZ = 16
+N_REST = 32
+ROWS = D_WIN // N_SHARD
+HALF = D_WIN // 2
 STACK = 4
 
 
@@ -37,28 +44,33 @@
     return [pl.BlockSpec(memory_space=pltpu.VMEM)] * count
 
 
-def pack_kernel(key_ref, value_ref, seg_ref, grad_ref, pay_ref, grad_t_ref):
+def pack_kernel(core_ref, key_ref, value_ref, seg_ref, grad_ref, pay_ref, keep_ref, send_ref):
     pay_ref[:TOK, :KV] = key_ref[0]
     pay_ref[:TOK, KV:] = value_ref[0]
     seg = jnp.broadcast_to(seg_ref[...].astype(jnp.float32), (8, TOK))
     pay_ref[TOK:, :TOK] = seg.astype(jnp.bfloat16)
     pay_ref[TOK:, TOK:] = jnp.zeros((8, 2 * KV - TOK), jnp.bfloat16)
-    grad_t_ref[...] = jnp.transpose(grad_ref[0].astype(jnp.float32)).astype(jnp.bfloat16)
-
-
-def pack(keys, values, segments, grad_output):
+    grad_t = jnp.transpose(grad_ref[0].astype(jnp.float32)).reshape(N_YZ, 2, ROWS, TOK)
+    even = grad_t[:, 0].reshape(HALF, TOK)
+    odd = grad_t[:, 1].reshape(HALF, TOK)
+    first = core_ref[0] == 0
+    keep_ref[...] = jnp.where(first, even, odd).astype(jnp.bfloat16)
+    send_ref[...] = jnp.where(first, odd, even).astype(jnp.bfloat16)
+
+
+def pack(core, keys, values, segments, grad_output):
     return pl.pallas_call(
         pack_kernel,
         out_shape=(
             jax.ShapeDtypeStruct((PAY_ROWS, 2 * KV), jnp.bfloat16),
-            jax.ShapeDtypeStruct((D_WIN, TOK), jnp.bfloat16),
-        ),
-        in_specs=vmem_specs(4),
-        out_specs=tuple(vmem_specs(2)),
+            jax.ShapeDtypeStruct((HALF, TOK), jnp.bfloat16),
+            jax.ShapeDtypeStruct((HALF, TOK), jnp.bfloat16),
+        ),
+        in_specs=[pl.BlockSpec(memory_space=pltpu.SMEM)] + vmem_specs(4),
+        out_specs=tuple(vmem_specs(3)),
         name="pack",
-        compiler_params=params(8),
         cost_estimate=pl.CostEstimate(flops=0, bytes_accessed=1 << 20, transcendentals=0),
-    )(keys, values, segments, grad_output)
+    )(core, keys, values, segments, grad_output)
 
 
 def attend_kernel(index_ref, query_ref, *refs):
@@ -74,7 +86,9 @@
         if step == 0:
             allowed = allowed & (k_at <= q_at)
         else:
-            allowed = allowed & (k_at + (index - step) * TOK >= 0)
+            odd = lax.rem(index, 2)
+            back = (0, 2, 4, 3 - 2 * odd, 1 + 2 * odd)[step]
+            allowed = allowed & (k_at + (index - back) * TOK >= 0)
         bias_ref[:, step * TOK : (step + 1) * TOK] = jnp.where(allowed, 0.0, NEG)
     ones = jnp.ones((TOK, HD), jnp.bfloat16)
     for first in range(0, HEADS, STACK):
@@ -123,27 +137,34 @@
     )(index, queries, *pays)
 
 
-def term_kernel(grad_t_ref, mixed_ref, out_ref):
-    grad_t = jnp.concatenate([grad_t_ref[i] for i in range(N_GROUP)], axis=1)
-    mixed = mixed_ref[...].reshape(N_GROUP * TOK, 2 * HD)
-    term = jnp.dot(grad_t, mixed, preferred_element_type=jnp.float32).astype(jnp.bfloat16)
-    term = term.reshape(N_SHARD, D_WIN // N_SHARD, 2 * HD)
+def term_kernel(place_ref, *refs):
+    grads, (mine_ref, other_ref, out_ref) = refs[:N_X], refs[N_X:]
+    x, zll = place_ref[0], place_ref[1]
+    term = jnp.zeros((HALF, 2 * HD), jnp.float32)
+    for step in range(N_X):
+        source = lax.rem(x - step + N_X, N_X)
+        for flip in range(2):
+            block = source * 2 + (zll + flip) % 2
+            grad = jnp.concatenate([grads[step][2 * flip], grads[step][2 * flip + 1]], axis=1)
+            mixed = jnp.concatenate([mine_ref[block], other_ref[block]], axis=0)
+            term = term + jnp.dot(grad, mixed, preferred_element_type=jnp.float32)
+    term = term.astype(jnp.bfloat16).reshape(N_YZ, ROWS, 2 * HD)
     for half in range(2):
         out_ref[:, half] = term[:, :, half * HD : (half + 1) * HD]
 
 
-def weight_term(grad_t, mixed):
+def weight_term(place, grads, mine, other):
     return pl.pallas_call(
         term_kernel,
-        out_shape=jax.ShapeDtypeStruct((N_SHARD, 2, D_WIN // N_SHARD, HD), jnp.bfloat16),
-        in_specs=vmem_specs(2),
+        out_shape=jax.ShapeDtypeStruct((N_YZ, 2, ROWS, HD), jnp.bfloat16),
+        in_specs=[pl.BlockSpec(memory_space=pltpu.SMEM)] + vmem_specs(N_X + 2),
         out_specs=vmem_specs(1)[0],
         name="weight_term",
         compiler_params=params(24),
         cost_estimate=pl.CostEstimate(
-            flops=2 * D_WIN * N_GROUP * TOK * 2 * HD, bytes_accessed=3 << 20, transcendentals=0
-        ),
-    )(grad_t, mixed)
+            flops=2 * HALF * 2 * N_GROUP * TOK * 2 * HD, bytes_accessed=3 << 20, transcendentals=0
+        ),
+    )(place, *grads, mine, other)
 
 
 def total_kernel(terms_ref, out_ref):
@@ -182,33 +203,43 @@
     )(parts)
 
 
-def shifted(value, steps):
-    count = lax.axis_size("shard")
-    return lax.ppermute(value, "shard", [(s, s + steps) for s in range(count - steps)])
-
-
-def local(queries, keys, values, segments, grad_output):
-    pay, grad_t = pack(keys, values, segments, grad_output)
-    grads = lax.all_gather(grad_t, GROUP, axis=0, tiled=False)
-    pays = [pay] + [shifted(pay, step) for step in range(1, SPAN + 1)]
-    index = lax.axis_index("shard").reshape(1).astype(jnp.int32)
-    attention, swap = attend(index, queries, pays)
-    mixed = lax.all_to_all(swap, GROUP, 0, 0, tiled=True)
-    term = weight_term(grads.reshape(N_GROUP, D_WIN, TOK), mixed)
-    terms = lax.all_to_all(
-        term.reshape(N_REST, D_WIN // N_SHARD, HD), REST, 0, 0, tiled=True
-    )
+def step(queries, keys, values, segments, grad_output):
+    core = lax.axis_index("core").astype(jnp.int32)
+    index = lax.axis_index("yz").astype(jnp.int32) * 2 + core
+    place = jnp.stack([lax.axis_index("x"), lax.axis_index("zll")]).astype(jnp.int32)
+    pay, keep, send = pack(core.reshape(1), keys, values, segments, grad_output)
+
+    def back(steps):
+        return [(s, s + steps(s)) for s in range(N_SHARD) if s + steps(s) < N_SHARD]
+
+    def swap(value, axis):
+        return lax.ppermute(value, axis, [(0, 1), (1, 0)])
+
+    two = lax.ppermute(pay, SHARD, back(lambda s: 2))
+    four = lax.ppermute(pay, SHARD, back(lambda s: 4))
+    near = lax.ppermute(pay, SHARD, back(lambda s: 3 if s % 2 else 1))
+    pair = jnp.stack([keep, swap(send, "core")])
+    quad = jnp.concatenate([pair, swap(pair, "zll")])
+    cross = swap(two, "core")
+    grads = [quad]
+    for step in range(1, N_X):
+        around = [(s, (s + step) % N_X) for s in range(N_X)]
+        grads.append(lax.ppermute(quad, "x", around))
+    attention, heads = attend(index.reshape(1), queries, [pay, two, four, near, cross])
+    mine = lax.all_to_all(heads, GROUP, 0, 0, tiled=True)
+    term = weight_term(place, grads, mine, swap(mine, "core"))
+    terms = lax.all_to_all(term.reshape(N_REST, ROWS, HD), REST, 0, 0, tiled=True)
     parts = lax.all_to_all(total(terms), REP, 0, 0, tiled=True)
     return attention, assemble(parts)
 
 
 def solution(mesh):
-    fine = Mesh(np.asarray(mesh.devices).reshape(4, 2, 2, N_SHARD), AXES)
-    row = P(REP, "shard", None)
+    fine = Mesh(np.asarray(mesh.devices).reshape(SIZES), AXES)
+    row = P(REP, SHARD, None)
     return jax.shard_map(
-        local,
+        step,
         mesh=fine,
-        in_specs=(row, row, row, P(REP, "shard"), row),
-        out_specs=(row, P("shard", None)),
+        in_specs=(row, row, row, P(REP, SHARD), row),
+        out_specs=(row, P(SHARD, None)),
         check_vma=False,
     )

time: 140 us -> 122 us (0.87)
  the two profiles are of different devices: /device:TPU:1 before, /device:TPU:8 now
where the time goes in v2:
time: 122 us
  starting transfers between devices  42.4 us (35%)
  blocking collectives  38.8 us (32%)
  waiting for transfers between devices  30.1 us (25%)
  Pallas kernels  7.37 us (6%)
  local copies, waits for them, and re-layouts  1.96 us (2%)
    all_to_all x1, blocking collectives, step(): lax.all_to_all(term.reshape(N_REST, ROWS, HD), REST, 0, 0, tiled=True)  27.5 us
    ppermute x3, waiting for transfers between devices, step(): grads.append(lax.ppermute(quad, 'x', around))  20.1 us
    all_to_all x1, blocking collectives, step(): parts = lax.all_to_all(total(terms), REP, 0, 0, tiled=True)  11.3 us
    ppermute x1, starting transfers between devices, step(): two = lax.ppermute(pay, SHARD, back(lambda s: 2))  10.9 us
    ppermute x4, starting transfers between devices, swap(): return lax.ppermute(value, axis, [(0, 1), (1, 0)])  10.6 us
    ppermute x3, starting transfers between devices, step(): grads.append(lax.ppermute(quad, 'x', around))  10.1 us
    ppermute x4, waiting for transfers between devices, swap(): return lax.ppermute(value, axis, [(0, 1), (1, 0)])  8.16 us
    all_to_all x1, starting transfers between devices, step(): mine = lax.all_to_all(heads, GROUP, 0, 0, tiled=True)  5.34 us
  transfers between devices with their start and end apart: 11, of which 6 were waited for; matrix products, arithmetic and copies ran while one was open for 0% of the time, Pallas kernels for 0%

profile of v2, /device:TPU:8, one launch (start us, length us, event | category | flops | bytes accessed | tf_op | source)
XLA Modules:
  0.0 121.5 jit_solution(5936435337302338009)
XLA Ops:
  0.6 1.9 %pack.1 = (bf16[136,512]{1,0:T(8,128)(2,1)}, bf16[512,128]{1,0:T(8,128)(2,1)}, bf16[512,128]{1,0:T(8,128)(2,1)}) custom-call(s32[1]{0:T(128)} %bitcast.1.core_ref, bf16[1,128,256]{2,1,0:T(8,128)(2,1)} %key_ref.1, bf16[1,128,256]{2,1,0:T(8,128)(2,1)} %value_ref.1, s32[1,128]{1,0:T(1,128)} %seg_ref.1, bf16[1,128,1024]{2,1,0:T(8,128)(2,1)} %grad_ref.1), custom_call_target="tpu_custom_call" | custom-call | bytes 1048576 | tf_op jit(solution)/shard_map/pack/pallas_call | solution.py:62
  2.5 10.9 %collective-permute-start = (bf16[136,512]{1,0:T(8,128)(2,1)}, bf16[136,512]{1,0:T(8,128)(2,1)S(1)}, u32[]{:S(2)}, u32[]{:S(2)}) collective-permute-start(bf16[136,512]{1,0:T(8,128)(2,1)} %get-tuple-element.7.refs_0_), channel_id=1, source_target_pairs={{0,2},{1,3},{2,4},{3,5},{4,6},{5,7},{6,8},{7,9},{8,10},{9,11},{10,... | collective-permute-start | bytes 417800 | tf_op jit(solution)/shard_map/ppermute | solution.py:218
  13.4 1.9 %collective-permute-start.2 = (bf16[136,512]{1,0:T(8,128)(2,1)}, bf16[136,512]{1,0:T(8,128)(2,1)S(1)}, u32[]{:S(2)}, u32[]{:S(2)}) collective-permute-start(bf16[136,512]{1,0:T(8,128)(2,1)} %get-tuple-element.7.refs_0_), channel_id=1, source_target_pairs={{0,1},{1,4},{2,3},{3,6},{4,5},{5,8},{6,7},{7,10},{8,9},{9,12},{10,... | collective-permute-start | bytes 417800 | tf_op jit(solution)/shard_map/ppermute | solution.py:220
  15.4 3.5 %collective-permute-start.1 = (bf16[136,512]{1,0:T(8,128)(2,1)}, bf16[136,512]{1,0:T(8,128)(2,1)S(1)}, u32[]{:S(2)}, u32[]{:S(2)}) collective-permute-start(bf16[136,512]{1,0:T(8,128)(2,1)} %get-tuple-element.7.refs_0_), channel_id=1, source_target_pairs={{0,4},{1,5},{2,6},{3,7},{4,8},{5,9},{6,10},{7,11},{8,12},{9,13},{1... | collective-permute-start | bytes 417800 | tf_op jit(solution)/shard_map/ppermute | solution.py:219
  18.8 0.7 collective-permute-done.refs_1_
  19.5 2.6 %collective-permute-start.3 = (bf16[136,512]{1,0:T(8,128)(2,1)S(1)}, bf16[136,512]{1,0:T(8,128)(2,1)S(1)}, u32[]{:S(2)}, u32[]{:S(2)}) collective-permute-start(bf16[136,512]{1,0:T(8,128)(2,1)S(1)} %collective-permute-done.refs_1_), channel_id=1, source_target_pairs={{0,1},{1,0},{2,3},{3,2},{4,5},{5,4},{6,7},{7,6},{8,9},{9,8},{10,11... | collective-permute-start | bytes 417800 | tf_op jit(solution)/shard_map/ppermute | solution.py:216
  22.2 0.0 collective-permute-done.2.refs_3_
  22.2 1.1 collective-permute-done.1.refs_2_
  23.3 0.0 collective-permute-done.3.refs_4_
  23.3 0.0 copy-start
  23.3 1.0 copy-done
  24.3 0.0 copy-start.1
  24.3 0.9 copy-done.1
  25.2 3.5 %attend.1 = (bf16[1,128,2048]{2,1,0:T(8,128)(2,1)}, bf16[8,128,256]{2,1,0:T(8,128)(2,1)}) custom-call(s32[1]{0:T(128)} %bitcast.index_ref, bf16[1,128,2048]{2,1,0:T(8,128)(2,1)S(1)} %copy-done, bf16[136,512]{1,0:T(8,128)(2,1)S(1)} %copy-done.1, bf16[136,512]{1,0:T(8,128)(2,1)S(1)} %collective-permute-done.refs_1_, ...), custom_call_target="tpu_custom_call" | custom-call | flops 700000000 | bytes 3145728 | tf_op jit(solution)/shard_map/attend/pallas_call | solution.py:123
  28.7 0.0 copy-start.3
  28.7 0.0 copy-start.2
  28.7 5.3 %all-to-all-start = ((bf16[8,128,256]{2,1,0:T(8,128)(2,1)}), bf16[8,128,256]{2,1,0:T(8,128)(2,1)S(1)}, u32[]{:S(2)}, u32[]{:S(2)}) async-start(bf16[8,128,256]{2,1,0:T(8,128)(2,1)} %get-tuple-element.11), calls=%async_computation | async-start | bytes 1048576 | tf_op jit(solution)/shard_map/all_to_all | solution.py:229
  34.1 0.0 copy-done.3
  34.1 2.2 %collective-permute-start.4 = (bf16[512,128]{1,0:T(8,128)(2,1)S(1)}, bf16[512,128]{1,0:T(8,128)(2,1)S(1)}, u32[]{:S(2)}, u32[]{:S(2)}) collective-permute-start(bf16[512,128]{1,0:T(8,128)(2,1)S(1)} %copy-done.3), channel_id=1, source_target_pairs={{0,1},{1,0},{2,3},{3,2},{4,5},{5,4},{6,7},{7,6},{8,9},{9,8},{10,11... | collective-permute-start | bytes 393224 | tf_op jit(solution)/shard_map/ppermute | solution.py:216
  36.2 1.1 collective-permute-done.4
  37.3 0.0 copy-done.2
  37.3 3.9 %collective-permute-start.5 = (bf16[2,512,128]{2,1,0:T(8,128)(2,1)S(1)}, bf16[2,512,128]{2,1,0:T(8,128)(2,1)S(1)}, u32[]{:S(2)}, u32[]{:S(2)}) collective-permute-start(bf16[2,512,128]{2,1,0:T(8,128)(2,1)S(1)} %pad_maximum_fusion.1), channel_id=1, source_target_pairs={{0,32},{32,0},{1,33},{33,1},{2,34},{34,2},{3,35},{35,3},{4,36},{36... | collective-permute-start | bytes 786440 | tf_op jit(solution)/shard_map/ppermute | solution.py:216
  41.3 7.1 %collective-permute-done.5 = bf16[2,512,128]{2,1,0:T(8,128)(2,1)S(1)} collective-permute-done((bf16[2,512,128]{2,1,0:T(8,128)(2,1)S(1)}, bf16[2,512,128]{2,1,0:T(8,128)(2,1)S(1)}, u32[]{:S(2)}, u32[]{:S(2)}) %collective-permute-start.5) | collective-permute-done | bytes 262176 | tf_op jit(solution)/shard_map/ppermute | solution.py:216
  48.3 0.1 pad_maximum_fusion.refs_0_
  48.4 4.6 %collective-permute-start.8 = (bf16[4,512,128]{2,1,0:T(8,128)(2,1)S(1)}, bf16[4,512,128]{2,1,0:T(8,128)(2,1)S(1)}, u32[]{:S(2)}, u32[]{:S(2)}) collective-permute-start(bf16[4,512,128]{2,1,0:T(8,128)(2,1)S(1)} %pad_maximum_fusion.refs_0_), channel_id=1, source_target_pairs={{0,384},{128,0},{256,128},{384,256},{1,385},{129,1},{257,129},{385... | collective-permute-start | bytes 1572872 | tf_op jit(solution)/shard_map/ppermute | solution.py:227
  53.0 2.8 %collective-permute-start.7 = (bf16[4,512,128]{2,1,0:T(8,128)(2,1)S(1)}, bf16[4,512,128]{2,1,0:T(8,128)(2,1)S(1)}, u32[]{:S(2)}, u32[]{:S(2)}) collective-permute-start(bf16[4,512,128]{2,1,0:T(8,128)(2,1)S(1)} %pad_maximum_fusion.refs_0_), channel_id=1, source_target_pairs={{0,256},{128,384},{256,0},{384,128},{1,257},{129,385},{257,1},{385... | collective-permute-start | bytes 1572872 | tf_op jit(solution)/shard_map/ppermute | solution.py:227
  55.8 2.8 %collective-permute-start.6 = (bf16[4,512,128]{2,1,0:T(8,128)(2,1)S(1)}, bf16[4,512,128]{2,1,0:T(8,128)(2,1)S(1)}, u32[]{:S(2)}, u32[]{:S(2)}) collective-permute-start(bf16[4,512,128]{2,1,0:T(8,128)(2,1)S(1)} %pad_maximum_fusion.refs_0_), channel_id=1, source_target_pairs={{0,128},{128,256},{256,384},{384,0},{1,129},{129,257},{257,385},{3... | collective-permute-start | bytes 1572872 | tf_op jit(solution)/shard_map/ppermute | solution.py:227
  58.5 0.0 all-to-all-done.refs_4_
  58.6 1.9 %collective-permute-start.9 = (bf16[8,128,256]{2,1,0:T(8,128)(2,1)S(1)}, bf16[8,128,256]{2,1,0:T(8,128)(2,1)S(1)}, u32[]{:S(2)}, u32[]{:S(2)}) collective-permute-start(bf16[8,128,256]{2,1,0:T(8,128)(2,1)S(1)} %all-to-all-done.refs_4_), channel_id=1, source_target_pairs={{0,1},{1,0},{2,3},{3,2},{4,5},{5,4},{6,7},{7,6},{8,9},{9,8},{10,11... | collective-permute-start | bytes 1572872 | tf_op jit(solution)/shard_map/ppermute | solution.py:216
  60.5 0.1 pad_add_fusion.place_ref
  60.6 14.5 %collective-permute-done.8.refs_3_ = bf16[4,512,128]{2,1,0:T(8,128)(2,1)S(1)} collective-permute-done((bf16[4,512,128]{2,1,0:T(8,128)(2,1)S(1)}, bf16[4,512,128]{2,1,0:T(8,128)(2,1)S(1)}, u32[]{:S(2)}, u32[]{:S(2)}) %collective-permute-start.8) | collective-permute-done | bytes 524320 | tf_op jit(solution)/shard_map/ppermute | solution.py:227
  75.1 0.0 collective-permute-done.7.refs_2_
  75.1 5.6 %collective-permute-done.6.refs_1_ = bf16[4,512,128]{2,1,0:T(8,128)(2,1)S(1)} collective-permute-done((bf16[4,512,128]{2,1,0:T(8,128)(2,1)S(1)}, bf16[4,512,128]{2,1,0:T(8,128)(2,1)S(1)}, u32[]{:S(2)}, u32[]{:S(2)}) %collective-permute-start.6) | collective-permute-done | bytes 524320 | tf_op jit(solution)/shard_map/ppermute | solution.py:227
  80.7 0.0 collective-permute-done.9.refs_5_
  80.7 1.3 %weight_term.1 = bf16[16,2,32,128]{3,2,1,0:T(8,128)(2,1)S(1)} custom-call(s32[2]{0:T(128)S(1)} %pad_add_fusion.place_ref, bf16[4,512,128]{2,1,0:T(8,128)(2,1)S(1)} %pad_maximum_fusion.refs_0_, bf16[4,512,128]{2,1,0:T(8,128)(2,1)S(1)} %collective-permute-done.6.refs_1_, bf16[4,512,128]{2,1,0:T(8,128)(2,1)S(1)} %collective-permute-done.7.refs_2_, ...), custom_call_target="tpu_custom_call" | custom-call | flops 536870912 | bytes 3145728 | tf_op jit(solution)/shard_map/weight_term/pallas_call | solution.py:157
  81.9 27.5 %all_to_all.15.terms_ref = bf16[32,32,128]{2,1,0:T(8,128)(2,1)S(1)} all-to-all(bf16[32,32,128]{2,1,0:T(8,128)(2,1)S(1)} %bitcast.7), channel_id=1, replica_groups=mesh['x'=4,'zlh'=2,'zll'=2,'yz'=16,'core'=2] {'yz','zlh'}, dimensions={0} | all-to-all | bytes 524288 | tf_op jit(solution)/shard_map/all_to_all | solution.py:231
  109.5 11.3 %all_to_all.16.parts_ref = bf16[16,32,128]{2,1,0:T(8,128)(2,1)S(1)} all-to-all(bf16[16,32,128]{2,1,0:T(8,128)(2,1)S(1)} %total.1), channel_id=1, replica_groups=mesh['x'=4,'zlh'=2,'zll'=2,'yz'=16,'core'=2] {'x','zlh','zll'}, dimensions={0} | all-to-all | bytes 262144 | tf_op jit(solution)/shard_map/all_to_all | solution.py:232
  120.8 0.7 assemble.1
  (2 shorter events, 0.1 us)
Async XLA Ops:
  2.5 17.0 %collective-permute-start = (bf16[136,512]{1,0:T(8,128)(2,1)}, bf16[136,512]{1,0:T(8,128)(2,1)S(1)}, u32[]{:S(2)}, u32[]{:S(2)}) collective-permute-start(bf16[136,512]{1,0:T(8,128)(2,1)} %get-tuple-element.7.refs_0_), channel_id=1, source_target_pairs={{0,2},{1,3},{2,4},{3,5},{4,6},{5,7},{6,8},{7,9},{8,10},{9,11},{10,... | collective-permute-start | bytes 417800 | tf_op jit(solution)/shard_map/ppermute | solution.py:218
  13.4 8.8 %collective-permute-start.2 = (bf16[136,512]{1,0:T(8,128)(2,1)}, bf16[136,512]{1,0:T(8,128)(2,1)S(1)}, u32[]{:S(2)}, u32[]{:S(2)}) collective-permute-start(bf16[136,512]{1,0:T(8,128)(2,1)} %get-tuple-element.7.refs_0_), channel_id=1, source_target_pairs={{0,1},{1,4},{2,3},{3,6},{4,5},{5,8},{6,7},{7,10},{8,9},{9,12},{10,... | collective-permute-start | bytes 417800 | tf_op jit(solution)/shard_map/ppermute | solution.py:220
  15.4 7.9 %collective-permute-start.1 = (bf16[136,512]{1,0:T(8,128)(2,1)}, bf16[136,512]{1,0:T(8,128)(2,1)S(1)}, u32[]{:S(2)}, u32[]{:S(2)}) collective-permute-start(bf16[136,512]{1,0:T(8,128)(2,1)} %get-tuple-element.7.refs_0_), channel_id=1, source_target_pairs={{0,4},{1,5},{2,6},{3,7},{4,8},{5,9},{6,10},{7,11},{8,12},{9,13},{1... | collective-permute-start | bytes 417800 | tf_op jit(solution)/shard_map/ppermute | solution.py:219
  19.5 3.8 %collective-permute-start.3 = (bf16[136,512]{1,0:T(8,128)(2,1)S(1)}, bf16[136,512]{1,0:T(8,128)(2,1)S(1)}, u32[]{:S(2)}, u32[]{:S(2)}) collective-permute-start(bf16[136,512]{1,0:T(8,128)(2,1)S(1)} %collective-permute-done.refs_1_), channel_id=1, source_target_pairs={{0,1},{1,0},{2,3},{3,2},{4,5},{5,4},{6,7},{7,6},{8,9},{9,8},{10,11... | collective-permute-start | bytes 417800 | tf_op jit(solution)/shard_map/ppermute | solution.py:216
  23.3 1.0 copy-start
  24.3 0.9 copy-start.1
  28.7 5.3 %copy-start.3 = (bf16[512,128]{1,0:T(8,128)(2,1)S(1)}, bf16[512,128]{1,0:T(8,128)(2,1)}, u32[]{:S(2)}) copy-start(bf16[512,128]{1,0:T(8,128)(2,1)} %get-tuple-element.10) | copy-start | bytes 393220
  28.7 8.6 %copy-start.2 = (bf16[512,128]{1,0:T(8,128)(2,1)S(1)}, bf16[512,128]{1,0:T(8,128)(2,1)}, u32[]{:S(2)}) copy-start(bf16[512,128]{1,0:T(8,128)(2,1)} %get-tuple-element.9) | copy-start | bytes 393220
  28.7 29.8 %all-to-all-start = ((bf16[8,128,256]{2,1,0:T(8,128)(2,1)}), bf16[8,128,256]{2,1,0:T(8,128)(2,1)S(1)}, u32[]{:S(2)}, u32[]{:S(2)}) async-start(bf16[8,128,256]{2,1,0:T(8,128)(2,1)} %get-tuple-element.11), calls=%async_computation | async-start | bytes 1048576 | tf_op jit(solution)/shard_map/all_to_all | solution.py:229
  34.1 3.2 %collective-permute-start.4 = (bf16[512,128]{1,0:T(8,128)(2,1)S(1)}, bf16[512,128]{1,0:T(8,128)(2,1)S(1)}, u32[]{:S(2)}, u32[]{:S(2)}) collective-permute-start(bf16[512,128]{1,0:T(8,128)(2,1)S(1)} %copy-done.3), channel_id=1, source_target_pairs={{0,1},{1,0},{2,3},{3,2},{4,5},{5,4},{6,7},{7,6},{8,9},{9,8},{10,11... | collective-permute-start | bytes 393224 | tf_op jit(solution)/shard_map/ppermute | solution.py:216
  37.3 11.0 %collective-permute-start.5 = (bf16[2,512,128]{2,1,0:T(8,128)(2,1)S(1)}, bf16[2,512,128]{2,1,0:T(8,128)(2,1)S(1)}, u32[]{:S(2)}, u32[]{:S(2)}) collective-permute-start(bf16[2,512,128]{2,1,0:T(8,128)(2,1)S(1)} %pad_maximum_fusion.1), channel_id=1, source_target_pairs={{0,32},{32,0},{1,33},{33,1},{2,34},{34,2},{3,35},{35,3},{4,36},{36... | collective-permute-start | bytes 786440 | tf_op jit(solution)/shard_map/ppermute | solution.py:216
  48.4 26.7 %collective-permute-start.8 = (bf16[4,512,128]{2,1,0:T(8,128)(2,1)S(1)}, bf16[4,512,128]{2,1,0:T(8,128)(2,1)S(1)}, u32[]{:S(2)}, u32[]{:S(2)}) collective-permute-start(bf16[4,512,128]{2,1,0:T(8,128)(2,1)S(1)} %pad_maximum_fusion.refs_0_), channel_id=1, source_target_pairs={{0,384},{128,0},{256,128},{384,256},{1,385},{129,1},{257,129},{385... | collective-permute-start | bytes 1572872 | tf_op jit(solution)/shard_map/ppermute | solution.py:227
  53.0 22.1 %collective-permute-start.7 = (bf16[4,512,128]{2,1,0:T(8,128)(2,1)S(1)}, bf16[4,512,128]{2,1,0:T(8,128)(2,1)S(1)}, u32[]{:S(2)}, u32[]{:S(2)}) collective-permute-start(bf16[4,512,128]{2,1,0:T(8,128)(2,1)S(1)} %pad_maximum_fusion.refs_0_), channel_id=1, source_target_pairs={{0,256},{128,384},{256,0},{384,128},{1,257},{129,385},{257,1},{385... | collective-permute-start | bytes 1572872 | tf_op jit(solution)/shard_map/ppermute | solution.py:227
  55.8 24.9 %collective-permute-start.6 = (bf16[4,512,128]{2,1,0:T(8,128)(2,1)S(1)}, bf16[4,512,128]{2,1,0:T(8,128)(2,1)S(1)}, u32[]{:S(2)}, u32[]{:S(2)}) collective-permute-start(bf16[4,512,128]{2,1,0:T(8,128)(2,1)S(1)} %pad_maximum_fusion.refs_0_), channel_id=1, source_target_pairs={{0,128},{128,256},{256,384},{384,0},{1,129},{129,257},{257,385},{3... | collective-permute-start | bytes 1572872 | tf_op jit(solution)/shard_map/ppermute | solution.py:227
  58.6 22.1 %collective-permute-start.9 = (bf16[8,128,256]{2,1,0:T(8,128)(2,1)S(1)}, bf16[8,128,256]{2,1,0:T(8,128)(2,1)S(1)}, u32[]{:S(2)}, u32[]{:S(2)}) collective-permute-start(bf16[8,128,256]{2,1,0:T(8,128)(2,1)S(1)} %all-to-all-done.refs_4_), channel_id=1, source_target_pairs={{0,1},{1,0},{2,3},{3,2},{4,5},{5,4},{6,7},{7,6},{8,9},{9,8},{10,11... | collective-permute-start | bytes 1572872 | tf_op jit(solution)/shard_map/ppermute | solution.py:216

commit v3 on v2

--- a/solution.py
+++ b/solution.py
@@ -21,18 +21,18 @@
 NEG = -1e30
 EXP2_SCALE = (HD**-0.5) * 1.4426950408889634
 
-AXES = ("x", "zlh", "zll", "yz", "core")
-SIZES = (4, 2, 2, 16, 2)
-REP = ("x", "zlh", "zll")
+AXES = ("x", "zl", "yz", "core")
+SIZES = (4, 4, 16, 2)
+REP = ("x", "zl")
 SHARD = ("yz", "core")
-GROUP = ("x", "zll")
+REST = ("yz", "zl")
 N_X = 4
-N_GROUP = 8
-REST = ("yz", "zlh")
+N_ZL = 4
 N_YZ = 16
-N_REST = 32
+N_REST = 64
 ROWS = D_WIN // N_SHARD
 HALF = D_WIN // 2
+WIDE = HEADS * HD // N_X
 STACK = 4
 
 
@@ -44,33 +44,47 @@
     return [pl.BlockSpec(memory_space=pltpu.VMEM)] * count
 
 
-def pack_kernel(core_ref, key_ref, value_ref, seg_ref, grad_ref, pay_ref, keep_ref, send_ref):
+def pack_kernel(key_ref, value_ref, seg_ref, grad_ref, pay_ref, grad_t_ref):
     pay_ref[:TOK, :KV] = key_ref[0]
     pay_ref[:TOK, KV:] = value_ref[0]
     seg = jnp.broadcast_to(seg_ref[...].astype(jnp.float32), (8, TOK))
     pay_ref[TOK:, :TOK] = seg.astype(jnp.bfloat16)
     pay_ref[TOK:, TOK:] = jnp.zeros((8, 2 * KV - TOK), jnp.bfloat16)
     grad_t = jnp.transpose(grad_ref[0].astype(jnp.float32)).reshape(N_YZ, 2, ROWS, TOK)
-    even = grad_t[:, 0].reshape(HALF, TOK)
-    odd = grad_t[:, 1].reshape(HALF, TOK)
-    first = core_ref[0] == 0
-    keep_ref[...] = jnp.where(first, even, odd).astype(jnp.bfloat16)
-    send_ref[...] = jnp.where(first, odd, even).astype(jnp.bfloat16)
-
-
-def pack(core, keys, values, segments, grad_output):
+    for core in range(2):
+        grad_t_ref[core] = grad_t[:, core].reshape(HALF, TOK).astype(jnp.bfloat16)
+
+
+def pack(keys, values, segments, grad_output):
     return pl.pallas_call(
         pack_kernel,
         out_shape=(
             jax.ShapeDtypeStruct((PAY_ROWS, 2 * KV), jnp.bfloat16),
-            jax.ShapeDtypeStruct((HALF, TOK), jnp.bfloat16),
-            jax.ShapeDtypeStruct((HALF, TOK), jnp.bfloat16),
-        ),
-        in_specs=[pl.BlockSpec(memory_space=pltpu.SMEM)] + vmem_specs(4),
-        out_specs=tuple(vmem_specs(3)),
+            jax.ShapeDtypeStruct((2, HALF, TOK), jnp.bfloat16),
+        ),
+        in_specs=vmem_specs(4),
+        out_specs=tuple(vmem_specs(2)),
         name="pack",
         cost_estimate=pl.CostEstimate(flops=0, bytes_accessed=1 << 20, transcendentals=0),
-    )(core, keys, values, segments, grad_output)
+    )(keys, values, segments, grad_output)
+
+
+def pick_kernel(place_ref, *refs):
+    other = 1 - place_ref[1]
+    for step in range(N_X):
+        refs[N_X][step] = refs[step][other]
+
+
+def pick(place, grads):
+    return pl.pallas_call(
+        pick_kernel,
+        out_shape=jax.ShapeDtypeStruct((N_X, HALF, TOK), jnp.bfloat16),
+        in_specs=[pl.BlockSpec(memory_space=pltpu.SMEM)] + vmem_specs(N_X),
+        out_specs=vmem_specs(1)[0],
+        name="pick",
+        compiler_params=params(8),
+        cost_estimate=pl.CostEstimate(flops=0, bytes_accessed=1 << 20, transcendentals=0),
+    )(place, *grads)
 
 
 def attend_kernel(index_ref, query_ref, *refs):
@@ -116,7 +130,7 @@
             head = first + h
             rows = result[h * TOK : (h + 1) * TOK]
             out_ref[0, :, head * HD : (head + 1) * HD] = rows
-            swap_ref[head // 2, :, (head % 2) * HD : (head % 2 + 1) * HD] = rows
+            swap_ref[first // STACK, :, h * HD : (h + 1) * HD] = rows
 
 
 def attend(index, queries, pays):
@@ -124,7 +138,7 @@
         attend_kernel,
         out_shape=(
             jax.ShapeDtypeStruct((1, TOK, HEADS * HD), jnp.bfloat16),
-            jax.ShapeDtypeStruct((N_GROUP, TOK, 2 * HD), jnp.bfloat16),
+            jax.ShapeDtypeStruct((N_X, TOK, WIDE), jnp.bfloat16),
         ),
         in_specs=[pl.BlockSpec(memory_space=pltpu.SMEM)] + vmem_specs(SPAN + 2),
         out_specs=tuple(vmem_specs(2)),
@@ -138,33 +152,31 @@
 
 
 def term_kernel(place_ref, *refs):
-    grads, (mine_ref, other_ref, out_ref) = refs[:N_X], refs[N_X:]
-    x, zll = place_ref[0], place_ref[1]
-    term = jnp.zeros((HALF, 2 * HD), jnp.float32)
+    grads, (far_ref, mine_ref, other_ref, out_ref) = refs[:N_X], refs[N_X:]
+    x, core = place_ref[0], place_ref[1]
+    term = jnp.zeros((HALF, WIDE), jnp.float32)
     for step in range(N_X):
         source = lax.rem(x - step + N_X, N_X)
-        for flip in range(2):
-            block = source * 2 + (zll + flip) % 2
-            grad = jnp.concatenate([grads[step][2 * flip], grads[step][2 * flip + 1]], axis=1)
-            mixed = jnp.concatenate([mine_ref[block], other_ref[block]], axis=0)
-            term = term + jnp.dot(grad, mixed, preferred_element_type=jnp.float32)
-    term = term.astype(jnp.bfloat16).reshape(N_YZ, ROWS, 2 * HD)
-    for half in range(2):
-        out_ref[:, half] = term[:, :, half * HD : (half + 1) * HD]
-
-
-def weight_term(place, grads, mine, other):
+        grad = jnp.concatenate([grads[step][core], far_ref[step]], axis=1)
+        mixed = jnp.concatenate([mine_ref[source], other_ref[source]], axis=0)
+        term = term + jnp.dot(grad, mixed, preferred_element_type=jnp.float32)
+    term = term.astype(jnp.bfloat16).reshape(N_YZ, ROWS, WIDE)
+    for head in range(N_ZL):
+        out_ref[:, head] = term[:, :, head * HD : (head + 1) * HD]
+
+
+def weight_term(place, grads, far, mine, other):
     return pl.pallas_call(
         term_kernel,
-        out_shape=jax.ShapeDtypeStruct((N_YZ, 2, ROWS, HD), jnp.bfloat16),
-        in_specs=[pl.BlockSpec(memory_space=pltpu.SMEM)] + vmem_specs(N_X + 2),
+        out_shape=jax.ShapeDtypeStruct((N_YZ, N_ZL, ROWS, HD), jnp.bfloat16),
+        in_specs=[pl.BlockSpec(memory_space=pltpu.SMEM)] + vmem_specs(N_X + 3),
         out_specs=vmem_specs(1)[0],
         name="weight_term",
         compiler_params=params(24),
         cost_estimate=pl.CostEstimate(
-            flops=2 * HALF * 2 * N_GROUP * TOK * 2 * HD, bytes_accessed=3 << 20, transcendentals=0
-        ),
-    )(place, *grads, mine, other)
+            flops=2 * HALF * 2 * N_X * TOK * WIDE, bytes_accessed=3 << 20, transcendentals=0
+        ),
+    )(place, *grads, far, mine, other)
 
 
 def total_kernel(terms_ref, out_ref):
@@ -184,12 +196,8 @@
 
 
 def assemble_kernel(parts_ref, out_ref):
-    for x in range(4):
-        for zlh in range(2):
-            for zll in range(2):
-                head = (x * 2 + zll) * 2 + zlh
-                part = parts_ref[x * 4 + zlh * 2 + zll]
-                out_ref[:, head * HD : (head + 1) * HD] = part.astype(jnp.float32)
+    for head in range(HEADS):
+        out_ref[:, head * HD : (head + 1) * HD] = parts_ref[head].astype(jnp.float32)
 
 
 def assemble(parts):
@@ -206,28 +214,27 @@
 def step(queries, keys, values, segments, grad_output):
     core = lax.axis_index("core").astype(jnp.int32)
     index = lax.axis_index("yz").astype(jnp.int32) * 2 + core
-    place = jnp.stack([lax.axis_index("x"), lax.axis_index("zll")]).astype(jnp.int32)
-    pay, keep, send = pack(core.reshape(1), keys, values, segments, grad_output)
+    place = jnp.stack([lax.axis_index("x").astype(jnp.int32), core])
+    pay, grad_t = pack(keys, values, segments, grad_output)
 
     def back(steps):
         return [(s, s + steps(s)) for s in range(N_SHARD) if s + steps(s) < N_SHARD]
 
-    def swap(value, axis):
-        return lax.ppermute(value, axis, [(0, 1), (1, 0)])
+    def swap(value):
+        return lax.ppermute(value, "core", [(0, 1), (1, 0)])
 
     two = lax.ppermute(pay, SHARD, back(lambda s: 2))
     four = lax.ppermute(pay, SHARD, back(lambda s: 4))
     near = lax.ppermute(pay, SHARD, back(lambda s: 3 if s % 2 else 1))
-    pair = jnp.stack([keep, swap(send, "core")])
-    quad = jnp.concatenate([pair, swap(pair, "zll")])
-    cross = swap(two, "core")
-    grads = [quad]
+    grads = [grad_t]
     for step in range(1, N_X):
         around = [(s, (s + step) % N_X) for s in range(N_X)]
-        grads.append(lax.ppermute(quad, "x", around))
+        grads.append(lax.ppermute(grad_t, "x", around))
+    cross = swap(two)
+    far = swap(pick(place, grads))
     attention, heads = attend(index.reshape(1), queries, [pay, two, four, near, cross])
-    mine = lax.all_to_all(heads, GROUP, 0, 0, tiled=True)
-    term = weight_term(place, grads, mine, swap(mine, "core"))
+    mine = lax.all_to_all(heads, "x", 0, 0, tiled=True)
+    term = weight_term(place, grads, far, mine, swap(mine))
     terms = lax.all_to_all(term.reshape(N_REST, ROWS, HD), REST, 0, 0, tiled=True)
     parts = lax.all_to_all(total(terms), REP, 0, 0, tiled=True)
     return attention, assemble(parts)

time: 122 us -> 109 us (0.89)
  waiting for transfers between devices: 30.1 us -> 14.6 us
  blocking collectives: 38.8 us -> 44.6 us
  starting transfers between devices: 42.4 us -> 38.3 us
    ppermute x7 -> x6, waiting for transfers between devices: 28.3 us -> 12.8 us  [the longest x3 11.3 us: step(): grads.append(lax.ppermute(grad_t, 'x', around))]
    all_to_all x1, blocking collectives: 27.5 us -> 32 us  [step(): lax.all_to_all(term.reshape(N_REST, ROWS, HD), REST, 0, 0, tiled=True)]
    ppermute x7 -> x6, starting transfers between devices: 20.8 us -> 17.6 us  [the longest x3 10.7 us: step(): grads.append(lax.ppermute(grad_t, 'x', around))]
  transfers between devices with their start and end apart: 11 -> 10, of which waited for: 6 -> 6; matrix products, arithmetic and copies ran while one was open for 0% -> 0% of each run, Pallas kernels for 0% -> 1%
where the time goes in v3:
time: 109 us; the launch traced here: 108 us
  blocking collectives  44.6 us (41%)
  starting transfers between devices  38.3 us (35%)
  waiting for transfers between devices  14.6 us (13%)
  Pallas kernels  7.99 us (7%)
  local copies, waits for them, and re-layouts  1.95 us (2%)
    all_to_all x1, blocking collectives, step(): lax.all_to_all(term.reshape(N_REST, ROWS, HD), REST, 0, 0, tiled=True)  32 us
    all_to_all x1, blocking collectives, step(): parts = lax.all_to_all(total(terms), REP, 0, 0, tiled=True)  12.5 us
    ppermute x3, waiting for transfers between devices, step(): grads.append(lax.ppermute(grad_t, 'x', around))  11.3 us
    ppermute x1, starting transfers between devices, step(): two = lax.ppermute(pay, SHARD, back(lambda s: 2))  10.9 us
    ppermute x3, starting transfers between devices, step(): grads.append(lax.ppermute(grad_t, 'x', around))  10.7 us
    ppermute x3, starting transfers between devices, swap(): return lax.ppermute(value, 'core', [(0, 1), (1, 0)])  6.96 us
    all_to_all x1, starting transfers between devices, step(): mine = lax.all_to_all(heads, 'x', 0, 0, tiled=True)  4.41 us
    ppermute x1, starting transfers between devices, step(): four = lax.ppermute(pay, SHARD, back(lambda s: 4))  3.48 us
  transfers between devices with their start and end apart: 10, of which 6 were waited for; matrix products, arithmetic and copies ran while one was open for 0% of the time, Pallas kernels for 1%

profile of v3, /device:TPU:8, one launch (start us, length us, event | category | flops | bytes accessed | tf_op | source)
XLA Modules:
  0.0 108.3 jit_solution(16877194561853747813)
XLA Ops:
  0.6 1.9 %pack.1 = (bf16[136,512]{1,0:T(8,128)(2,1)}, bf16[2,512,128]{2,1,0:T(8,128)(2,1)}) custom-call(bf16[1,128,256]{2,1,0:T(8,128)(2,1)} %key_ref.1, bf16[1,128,256]{2,1,0:T(8,128)(2,1)} %value_ref.1, s32[1,128]{1,0:T(1,128)} %seg_ref.1, bf16[1,128,1024]{2,1,0:T(8,128)(2,1)} %grad_ref.1), custom_call_target="tpu_custom_call" | custom-call | bytes 1048576 | tf_op jit(solution)/shard_map/pack/pallas_call | solution.py:59
  2.5 10.9 %collective-permute-start = (bf16[136,512]{1,0:T(8,128)(2,1)}, bf16[136,512]{1,0:T(8,128)(2,1)S(1)}, u32[]{:S(2)}, u32[]{:S(2)}) collective-permute-start(bf16[136,512]{1,0:T(8,128)(2,1)} %get-tuple-element.6.refs_0_), channel_id=1, source_target_pairs={{0,2},{1,3},{2,4},{3,5},{4,6},{5,7},{6,8},{7,9},{8,10},{9,11},{10,... | collective-permute-start | bytes 417800 | tf_op jit(solution)/shard_map/ppermute | solution.py:226
  13.4 1.9 %collective-permute-start.2 = (bf16[136,512]{1,0:T(8,128)(2,1)}, bf16[136,512]{1,0:T(8,128)(2,1)S(1)}, u32[]{:S(2)}, u32[]{:S(2)}) collective-permute-start(bf16[136,512]{1,0:T(8,128)(2,1)} %get-tuple-element.6.refs_0_), channel_id=1, source_target_pairs={{0,1},{1,4},{2,3},{3,6},{4,5},{5,8},{6,7},{7,10},{8,9},{9,12},{10,... | collective-permute-start | bytes 417800 | tf_op jit(solution)/shard_map/ppermute | solution.py:228
  15.4 3.5 %collective-permute-start.1 = (bf16[136,512]{1,0:T(8,128)(2,1)}, bf16[136,512]{1,0:T(8,128)(2,1)S(1)}, u32[]{:S(2)}, u32[]{:S(2)}) collective-permute-start(bf16[136,512]{1,0:T(8,128)(2,1)} %get-tuple-element.6.refs_0_), channel_id=1, source_target_pairs={{0,4},{1,5},{2,6},{3,7},{4,8},{5,9},{6,10},{7,11},{8,12},{9,13},{1... | collective-permute-start | bytes 417800 | tf_op jit(solution)/shard_map/ppermute | solution.py:227
  18.9 0.7 collective-permute-done.refs_1_
  19.5 2.6 %collective-permute-start.3 = (bf16[136,512]{1,0:T(8,128)(2,1)S(1)}, bf16[136,512]{1,0:T(8,128)(2,1)S(1)}, u32[]{:S(2)}, u32[]{:S(2)}) collective-permute-start(bf16[136,512]{1,0:T(8,128)(2,1)S(1)} %collective-permute-done.refs_1_), channel_id=1, source_target_pairs={{0,1},{1,0},{2,3},{3,2},{4,5},{5,4},{6,7},{7,6},{8,9},{9,8},{10,11... | collective-permute-start | bytes 417800 | tf_op jit(solution)/shard_map/ppermute | solution.py:224
  22.2 0.0 collective-permute-done.2.refs_3_
  22.2 1.1 %collective-permute-done.1.refs_2_ = bf16[136,512]{1,0:T(8,128)(2,1)S(1)} collective-permute-done((bf16[136,512]{1,0:T(8,128)(2,1)}, bf16[136,512]{1,0:T(8,128)(2,1)S(1)}, u32[]{:S(2)}, u32[]{:S(2)}) %collective-permute-start.1) | collective-permute-done | bytes 139296 | tf_op jit(solution)/shard_map/ppermute | solution.py:227
  23.3 0.0 collective-permute-done.3.refs_4_
  23.3 0.0 copy-start.1
  23.3 1.0 copy-done.1
  24.3 0.0 copy-start.2
  24.3 0.9 copy-done.2
  25.3 3.5 %attend.1 = (bf16[1,128,2048]{2,1,0:T(8,128)(2,1)}, bf16[4,128,512]{2,1,0:T(8,128)(2,1)}) custom-call(s32[1]{0:T(128)} %bitcast.index_ref, bf16[1,128,2048]{2,1,0:T(8,128)(2,1)S(1)} %copy-done.1, bf16[136,512]{1,0:T(8,128)(2,1)S(1)} %copy-done.2, bf16[136,512]{1,0:T(8,128)(2,1)S(1)} %collective-permute-done.refs_1_, ...), custom_call_target="tpu_custom_call" | custom-call | flops 700000000 | bytes 3145728 | tf_op jit(solution)/shard_map/attend/pallas_call | solution.py:137
  28.7 0.0 copy-start
  28.7 4.4 %all-to-all-start = ((bf16[4,128,512]{2,1,0:T(8,128)(2,1)}), bf16[4,128,512]{2,1,0:T(8,128)(2,1)S(1)}, u32[]{:S(2)}, u32[]{:S(2)}) async-start(bf16[4,128,512]{2,1,0:T(8,128)(2,1)} %get-tuple-element.9), calls=%async_computation | async-start | bytes 1048576 | tf_op jit(solution)/shard_map/all_to_all | solution.py:236
  33.1 0.0 copy-done
  33.1 5.1 %collective-permute-start.6 = (bf16[2,512,128]{2,1,0:T(8,128)(2,1)S(1)}, bf16[2,512,128]{2,1,0:T(8,128)(2,1)S(1)}, u32[]{:S(2)}, u32[]{:S(2)}) collective-permute-start(bf16[2,512,128]{2,1,0:T(8,128)(2,1)S(1)} %copy-done), channel_id=1, source_target_pairs={{0,384},{128,0},{256,128},{384,256},{1,385},{129,1},{257,129},{385... | collective-permute-start | bytes 786440 | tf_op jit(solution)/shard_map/ppermute | solution.py:232
  38.3 2.8 %collective-permute-start.5 = (bf16[2,512,128]{2,1,0:T(8,128)(2,1)S(1)}, bf16[2,512,128]{2,1,0:T(8,128)(2,1)S(1)}, u32[]{:S(2)}, u32[]{:S(2)}) collective-permute-start(bf16[2,512,128]{2,1,0:T(8,128)(2,1)S(1)} %copy-done), channel_id=1, source_target_pairs={{0,256},{128,384},{256,0},{384,128},{1,257},{129,385},{257,1},{385... | collective-permute-start | bytes 786440 | tf_op jit(solution)/shard_map/ppermute | solution.py:232
  41.0 2.8 %collective-permute-start.4 = (bf16[2,512,128]{2,1,0:T(8,128)(2,1)S(1)}, bf16[2,512,128]{2,1,0:T(8,128)(2,1)S(1)}, u32[]{:S(2)}, u32[]{:S(2)}) collective-permute-start(bf16[2,512,128]{2,1,0:T(8,128)(2,1)S(1)} %copy-done), channel_id=1, source_target_pairs={{0,128},{128,256},{256,384},{384,0},{1,129},{129,257},{257,385},{3... | collective-permute-start | bytes 786440 | tf_op jit(solution)/shard_map/ppermute | solution.py:232
  43.8 0.1 pad_add_fusion.place_ref
  43.9 4.3 %collective-permute-done.6.refs_3_ = bf16[2,512,128]{2,1,0:T(8,128)(2,1)S(1)} collective-permute-done((bf16[2,512,128]{2,1,0:T(8,128)(2,1)S(1)}, bf16[2,512,128]{2,1,0:T(8,128)(2,1)S(1)}, u32[]{:S(2)}, u32[]{:S(2)}) %collective-permute-start.6) | collective-permute-done | bytes 262176 | tf_op jit(solution)/shard_map/ppermute | solution.py:232
  48.2 2.7 %collective-permute-done.5.refs_2_ = bf16[2,512,128]{2,1,0:T(8,128)(2,1)S(1)} collective-permute-done((bf16[2,512,128]{2,1,0:T(8,128)(2,1)S(1)}, bf16[2,512,128]{2,1,0:T(8,128)(2,1)S(1)}, u32[]{:S(2)}, u32[]{:S(2)}) %collective-permute-start.5) | collective-permute-done | bytes 262176 | tf_op jit(solution)/shard_map/ppermute | solution.py:232
  50.9 4.3 %collective-permute-done.4.refs_1_ = bf16[2,512,128]{2,1,0:T(8,128)(2,1)S(1)} collective-permute-done((bf16[2,512,128]{2,1,0:T(8,128)(2,1)S(1)}, bf16[2,512,128]{2,1,0:T(8,128)(2,1)S(1)}, u32[]{:S(2)}, u32[]{:S(2)}) %collective-permute-start.4) | collective-permute-done | bytes 262176 | tf_op jit(solution)/shard_map/ppermute | solution.py:232
  55.2 0.6 pick.1
  55.8 1.9 %collective-permute-start.7 = (bf16[4,512,128]{2,1,0:T(8,128)(2,1)S(1)}, bf16[4,512,128]{2,1,0:T(8,128)(2,1)S(1)}, u32[]{:S(2)}, u32[]{:S(2)}) collective-permute-start(bf16[4,512,128]{2,1,0:T(8,128)(2,1)S(1)} %pick.1), channel_id=1, source_target_pairs={{0,1},{1,0},{2,3},{3,2},{4,5},{5,4},{6,7},{7,6},{8,9},{9,8},{10,11... | collective-permute-start | bytes 1572872 | tf_op jit(solution)/shard_map/ppermute | solution.py:224
  57.7 0.0 all-to-all-done.refs_5_
  57.7 2.4 %collective-permute-start.8 = (bf16[4,128,512]{2,1,0:T(8,128)(2,1)S(1)}, bf16[4,128,512]{2,1,0:T(8,128)(2,1)S(1)}, u32[]{:S(2)}, u32[]{:S(2)}) collective-permute-start(bf16[4,128,512]{2,1,0:T(8,128)(2,1)S(1)} %all-to-all-done.refs_5_), channel_id=1, source_target_pairs={{0,1},{1,0},{2,3},{3,2},{4,5},{5,4},{6,7},{7,6},{8,9},{9,8},{10,11... | collective-permute-start | bytes 1572872 | tf_op jit(solution)/shard_map/ppermute | solution.py:224
  60.1 0.0 collective-permute-done.7.refs_4_
  60.1 1.5 %collective-permute-done.8.refs_6_ = bf16[4,128,512]{2,1,0:T(8,128)(2,1)S(1)} collective-permute-done((bf16[4,128,512]{2,1,0:T(8,128)(2,1)S(1)}, bf16[4,128,512]{2,1,0:T(8,128)(2,1)S(1)}, u32[]{:S(2)}, u32[]{:S(2)}) %collective-permute-start.8) | collective-permute-done | bytes 524320 | tf_op jit(solution)/shard_map/ppermute | solution.py:224
  61.6 1.2 %weight_term.1 = bf16[16,4,32,128]{3,2,1,0:T(8,128)(2,1)S(1)} custom-call(s32[2]{0:T(128)S(1)} %pad_add_fusion.place_ref, bf16[2,512,128]{2,1,0:T(8,128)(2,1)S(1)} %copy-done, bf16[2,512,128]{2,1,0:T(8,128)(2,1)S(1)} %collective-permute-done.4.refs_1_, bf16[2,512,128]{2,1,0:T(8,128)(2,1)S(1)} %collective-permute-done.5.refs_2_, ...), custom_call_target="tpu_custom_call" | custom-call | flops 536870912 | bytes 3145728 | tf_op jit(solution)/shard_map/weight_term/pallas_call | solution.py:169
  62.9 32.0 %all_to_all.15.terms_ref = bf16[64,32,128]{2,1,0:T(8,128)(2,1)S(1)} all-to-all(bf16[64,32,128]{2,1,0:T(8,128)(2,1)S(1)} %bitcast.4), channel_id=1, replica_groups=mesh['x'=4,'zl'=4,'yz'=16,'core'=2] {'yz','zl'}, dimensions={0} | all-to-all | bytes 1048576 | tf_op jit(solution)/shard_map/all_to_all | solution.py:238
  95.0 0.1 total.1
  95.0 12.5 %all_to_all.16.parts_ref = bf16[16,32,128]{2,1,0:T(8,128)(2,1)S(1)} all-to-all(bf16[16,32,128]{2,1,0:T(8,128)(2,1)S(1)} %total.1), channel_id=1, replica_groups=mesh['x'=4,'zl'=4,'yz'=16,'core'=2] {'x','zl'}, dimensions={0} | all-to-all | bytes 262144 | tf_op jit(solution)/shard_map/all_to_all | solution.py:239
  107.6 0.7 assemble.1
Async XLA Ops:
  2.5 17.0 %collective-permute-start = (bf16[136,512]{1,0:T(8,128)(2,1)}, bf16[136,512]{1,0:T(8,128)(2,1)S(1)}, u32[]{:S(2)}, u32[]{:S(2)}) collective-permute-start(bf16[136,512]{1,0:T(8,128)(2,1)} %get-tuple-element.6.refs_0_), channel_id=1, source_target_pairs={{0,2},{1,3},{2,4},{3,5},{4,6},{5,7},{6,8},{7,9},{8,10},{9,11},{10,... | collective-permute-start | bytes 417800 | tf_op jit(solution)/shard_map/ppermute | solution.py:226
  13.4 8.8 %collective-permute-start.2 = (bf16[136,512]{1,0:T(8,128)(2,1)}, bf16[136,512]{1,0:T(8,128)(2,1)S(1)}, u32[]{:S(2)}, u32[]{:S(2)}) collective-permute-start(bf16[136,512]{1,0:T(8,128)(2,1)} %get-tuple-element.6.refs_0_), channel_id=1, source_target_pairs={{0,1},{1,4},{2,3},{3,6},{4,5},{5,8},{6,7},{7,10},{8,9},{9,12},{10,... | collective-permute-start | bytes 417800 | tf_op jit(solution)/shard_map/ppermute | solution.py:228
  15.4 7.9 %collective-permute-start.1 = (bf16[136,512]{1,0:T(8,128)(2,1)}, bf16[136,512]{1,0:T(8,128)(2,1)S(1)}, u32[]{:S(2)}, u32[]{:S(2)}) collective-permute-start(bf16[136,512]{1,0:T(8,128)(2,1)} %get-tuple-element.6.refs_0_), channel_id=1, source_target_pairs={{0,4},{1,5},{2,6},{3,7},{4,8},{5,9},{6,10},{7,11},{8,12},{9,13},{1... | collective-permute-start | bytes 417800 | tf_op jit(solution)/shard_map/ppermute | solution.py:227
  19.5 3.8 %collective-permute-start.3 = (bf16[136,512]{1,0:T(8,128)(2,1)S(1)}, bf16[136,512]{1,0:T(8,128)(2,1)S(1)}, u32[]{:S(2)}, u32[]{:S(2)}) collective-permute-start(bf16[136,512]{1,0:T(8,128)(2,1)S(1)} %collective-permute-done.refs_1_), channel_id=1, source_target_pairs={{0,1},{1,0},{2,3},{3,2},{4,5},{5,4},{6,7},{7,6},{8,9},{9,8},{10,11... | collective-permute-start | bytes 417800 | tf_op jit(solution)/shard_map/ppermute | solution.py:224
  23.3 1.0 copy-start.1
  24.3 0.9 copy-start.2
  28.7 4.4 %copy-start = (bf16[2,512,128]{2,1,0:T(8,128)(2,1)S(1)}, bf16[2,512,128]{2,1,0:T(8,128)(2,1)}, u32[]{:S(2)}) copy-start(bf16[2,512,128]{2,1,0:T(8,128)(2,1)} %get-tuple-element.8.refs_0_) | copy-start | bytes 786436
  28.7 29.0 %all-to-all-start = ((bf16[4,128,512]{2,1,0:T(8,128)(2,1)}), bf16[4,128,512]{2,1,0:T(8,128)(2,1)S(1)}, u32[]{:S(2)}, u32[]{:S(2)}) async-start(bf16[4,128,512]{2,1,0:T(8,128)(2,1)} %get-tuple-element.9), calls=%async_computation | async-start | bytes 1048576 | tf_op jit(solution)/shard_map/all_to_all | solution.py:236
  33.1 15.0 %collective-permute-start.6 = (bf16[2,512,128]{2,1,0:T(8,128)(2,1)S(1)}, bf16[2,512,128]{2,1,0:T(8,128)(2,1)S(1)}, u32[]{:S(2)}, u32[]{:S(2)}) collective-permute-start(bf16[2,512,128]{2,1,0:T(8,128)(2,1)S(1)} %copy-done), channel_id=1, source_target_pairs={{0,384},{128,0},{256,128},{384,256},{1,385},{129,1},{257,129},{385... | collective-permute-start | bytes 786440 | tf_op jit(solution)/shard_map/ppermute | solution.py:232
  38.3 12.6 %collective-permute-start.5 = (bf16[2,512,128]{2,1,0:T(8,128)(2,1)S(1)}, bf16[2,512,128]{2,1,0:T(8,128)(2,1)S(1)}, u32[]{:S(2)}, u32[]{:S(2)}) collective-permute-start(bf16[2,512,128]{2,1,0:T(8,128)(2,1)S(1)} %copy-done), channel_id=1, source_target_pairs={{0,256},{128,384},{256,0},{384,128},{1,257},{129,385},{257,1},{385... | collective-permute-start | bytes 786440 | tf_op jit(solution)/shard_map/ppermute | solution.py:232
  41.0 14.1 %collective-permute-start.4 = (bf16[2,512,128]{2,1,0:T(8,128)(2,1)S(1)}, bf16[2,512,128]{2,1,0:T(8,128)(2,1)S(1)}, u32[]{:S(2)}, u32[]{:S(2)}) collective-permute-start(bf16[2,512,128]{2,1,0:T(8,128)(2,1)S(1)} %copy-done), channel_id=1, source_target_pairs={{0,128},{128,256},{256,384},{384,0},{1,129},{129,257},{257,385},{3... | collective-permute-start | bytes 786440 | tf_op jit(solution)/shard_map/ppermute | solution.py:232
  55.8 4.4 %collective-permute-start.7 = (bf16[4,512,128]{2,1,0:T(8,128)(2,1)S(1)}, bf16[4,512,128]{2,1,0:T(8,128)(2,1)S(1)}, u32[]{:S(2)}, u32[]{:S(2)}) collective-permute-start(bf16[4,512,128]{2,1,0:T(8,128)(2,1)S(1)} %pick.1), channel_id=1, source_target_pairs={{0,1},{1,0},{2,3},{3,2},{4,5},{5,4},{6,7},{7,6},{8,9},{9,8},{10,11... | collective-permute-start | bytes 1572872 | tf_op jit(solution)/shard_map/ppermute | solution.py:224
  57.7 3.9 %collective-permute-start.8 = (bf16[4,128,512]{2,1,0:T(8,128)(2,1)S(1)}, bf16[4,128,512]{2,1,0:T(8,128)(2,1)S(1)}, u32[]{:S(2)}, u32[]{:S(2)}) collective-permute-start(bf16[4,128,512]{2,1,0:T(8,128)(2,1)S(1)} %all-to-all-done.refs_5_), channel_id=1, source_target_pairs={{0,1},{1,0},{2,3},{3,2},{4,5},{5,4},{6,7},{7,6},{8,9},{9,8},{10,11... | collective-permute-start | bytes 1572872 | tf_op jit(solution)/shard_map/ppermute | solution.py:224

commit v4 on v3

--- a/solution.py
+++ b/solution.py
@@ -25,14 +25,15 @@
 SIZES = (4, 4, 16, 2)
 REP = ("x", "zl")
 SHARD = ("yz", "core")
-REST = ("yz", "zl")
+GROUP = ("x", "core")
+REST = ("yz", "core", "zl")
 N_X = 4
 N_ZL = 4
 N_YZ = 16
-N_REST = 64
+N_GROUP = 8
 ROWS = D_WIN // N_SHARD
-HALF = D_WIN // 2
-WIDE = HEADS * HD // N_X
+PART = ROWS // 2
+WIDE = HEADS * HD // N_GROUP
 STACK = 4
 
 
@@ -50,9 +51,9 @@
     seg = jnp.broadcast_to(seg_ref[...].astype(jnp.float32), (8, TOK))
     pay_ref[TOK:, :TOK] = seg.astype(jnp.bfloat16)
     pay_ref[TOK:, TOK:] = jnp.zeros((8, 2 * KV - TOK), jnp.bfloat16)
-    grad_t = jnp.transpose(grad_ref[0].astype(jnp.float32)).reshape(N_YZ, 2, ROWS, TOK)
-    for core in range(2):
-        grad_t_ref[core] = grad_t[:, core].reshape(HALF, TOK).astype(jnp.bfloat16)
+    grad_t = jnp.transpose(grad_ref[0].astype(jnp.float32)).astype(jnp.bfloat16)
+    for x in range(N_X):
+        grad_t_ref[x] = grad_t
 
 
 def pack(keys, values, segments, grad_output):
@@ -60,31 +61,13 @@
         pack_kernel,
         out_shape=(
             jax.ShapeDtypeStruct((PAY_ROWS, 2 * KV), jnp.bfloat16),
-            jax.ShapeDtypeStruct((2, HALF, TOK), jnp.bfloat16),
+            jax.ShapeDtypeStruct((N_X, D_WIN, TOK), jnp.bfloat16),
         ),
         in_specs=vmem_specs(4),
         out_specs=tuple(vmem_specs(2)),
         name="pack",
         cost_estimate=pl.CostEstimate(flops=0, bytes_accessed=1 << 20, transcendentals=0),
     )(keys, values, segments, grad_output)
-
-
-def pick_kernel(place_ref, *refs):
-    other = 1 - place_ref[1]
-    for step in range(N_X):
-        refs[N_X][step] = refs[step][other]
-
-
-def pick(place, grads):
-    return pl.pallas_call(
-        pick_kernel,
-        out_shape=jax.ShapeDtypeStruct((N_X, HALF, TOK), jnp.bfloat16),
-        in_specs=[pl.BlockSpec(memory_space=pltpu.SMEM)] + vmem_specs(N_X),
-        out_specs=vmem_specs(1)[0],
-        name="pick",
-        compiler_params=params(8),
-        cost_estimate=pl.CostEstimate(flops=0, bytes_accessed=1 << 20, transcendentals=0),
-    )(place, *grads)
 
 
 def attend_kernel(index_ref, query_ref, *refs):
@@ -130,7 +113,7 @@
             head = first + h
             rows = result[h * TOK : (h + 1) * TOK]
             out_ref[0, :, head * HD : (head + 1) * HD] = rows
-            swap_ref[first // STACK, :, h * HD : (h + 1) * HD] = rows
+            swap_ref[head // 2, :, (head % 2) * HD : (head % 2 + 1) * HD] = rows
 
 
 def attend(index, queries, pays):
@@ -138,7 +121,7 @@
         attend_kernel,
         out_shape=(
             jax.ShapeDtypeStruct((1, TOK, HEADS * HD), jnp.bfloat16),
-            jax.ShapeDtypeStruct((N_X, TOK, WIDE), jnp.bfloat16),
+            jax.ShapeDtypeStruct((N_GROUP, TOK, WIDE), jnp.bfloat16),
         ),
         in_specs=[pl.BlockSpec(memory_space=pltpu.SMEM)] + vmem_specs(SPAN + 2),
         out_specs=tuple(vmem_specs(2)),
@@ -151,43 +134,45 @@
     )(index, queries, *pays)
 
 
-def term_kernel(place_ref, *refs):
-    grads, (far_ref, mine_ref, other_ref, out_ref) = refs[:N_X], refs[N_X:]
-    x, core = place_ref[0], place_ref[1]
-    term = jnp.zeros((HALF, WIDE), jnp.float32)
-    for step in range(N_X):
-        source = lax.rem(x - step + N_X, N_X)
-        grad = jnp.concatenate([grads[step][core], far_ref[step]], axis=1)
-        mixed = jnp.concatenate([mine_ref[source], other_ref[source]], axis=0)
+def term_kernel(core_ref, near_ref, far_ref, mixed_ref, out_ref):
+    core = core_ref[0]
+    term = jnp.zeros((D_WIN, WIDE), jnp.float32)
+    for x in range(N_X):
+        grad = jnp.concatenate([near_ref[x], far_ref[x]], axis=1)
+        mixed = jnp.concatenate([mixed_ref[2 * x + core], mixed_ref[2 * x + 1 - core]], axis=0)
         term = term + jnp.dot(grad, mixed, preferred_element_type=jnp.float32)
-    term = term.astype(jnp.bfloat16).reshape(N_YZ, ROWS, WIDE)
-    for head in range(N_ZL):
-        out_ref[:, head] = term[:, :, head * HD : (head + 1) * HD]
-
-
-def weight_term(place, grads, far, mine, other):
+    term = term.astype(jnp.bfloat16).reshape(N_SHARD, 2, PART, WIDE)
+    for part in range(2):
+        for head in range(2):
+            out_ref[:, 2 * part + head] = term[:, part, :, head * HD : (head + 1) * HD]
+
+
+def weight_term(core, near, far, mixed):
     return pl.pallas_call(
         term_kernel,
-        out_shape=jax.ShapeDtypeStruct((N_YZ, N_ZL, ROWS, HD), jnp.bfloat16),
-        in_specs=[pl.BlockSpec(memory_space=pltpu.SMEM)] + vmem_specs(N_X + 3),
+        out_shape=jax.ShapeDtypeStruct((N_SHARD, N_ZL, PART, HD), jnp.bfloat16),
+        in_specs=[pl.BlockSpec(memory_space=pltpu.SMEM)] + vmem_specs(3),
         out_specs=vmem_specs(1)[0],
         name="weight_term",
         compiler_params=params(24),
         cost_estimate=pl.CostEstimate(
-            flops=2 * HALF * 2 * N_X * TOK * WIDE, bytes_accessed=3 << 20, transcendentals=0
-        ),
-    )(place, *grads, far, mine, other)
+            flops=2 * D_WIN * N_GROUP * TOK * WIDE, bytes_accessed=3 << 20, transcendentals=0
+        ),
+    )(core, near, far, mixed)
 
 
 def total_kernel(terms_ref, out_ref):
-    total = jnp.sum(terms_ref[...].astype(jnp.float32), axis=0).astype(jnp.bfloat16)
-    out_ref[...] = jnp.broadcast_to(total[None], out_ref.shape)
+    terms = terms_ref[...].reshape(N_YZ, 2, N_ZL, PART, HD)
+    for core in range(2):
+        own = terms[:, core].reshape(N_YZ * N_ZL, PART, HD).astype(jnp.float32)
+        total = jnp.sum(own, axis=0).astype(jnp.bfloat16)
+        out_ref[:, core] = jnp.broadcast_to(total[None], (N_REP, PART, HD))
 
 
 def total(terms):
     return pl.pallas_call(
         total_kernel,
-        out_shape=jax.ShapeDtypeStruct((N_REP, D_WIN // N_SHARD, HD), jnp.bfloat16),
+        out_shape=jax.ShapeDtypeStruct((N_REP, 2, PART, HD), jnp.bfloat16),
         in_specs=vmem_specs(1),
         out_specs=vmem_specs(1)[0],
         name="total",
@@ -196,8 +181,14 @@
 
 
 def assemble_kernel(parts_ref, out_ref):
-    for head in range(HEADS):
-        out_ref[:, head * HD : (head + 1) * HD] = parts_ref[head].astype(jnp.float32)
+    for x in range(N_X):
+        for part in range(2):
+            for half in range(2):
+                for core in range(2):
+                    head = 4 * x + 2 * core + half
+                    piece = parts_ref[4 * x + 2 * part + half, core].astype(jnp.float32)
+                    rows = slice(part * PART, (part + 1) * PART)
+                    out_ref[rows, head * HD : (head + 1) * HD] = piece
 
 
 def assemble(parts):
@@ -214,7 +205,6 @@
 def step(queries, keys, values, segments, grad_output):
     core = lax.axis_index("core").astype(jnp.int32)
     index = lax.axis_index("yz").astype(jnp.int32) * 2 + core
-    place = jnp.stack([lax.axis_index("x").astype(jnp.int32), core])
     pay, grad_t = pack(keys, values, segments, grad_output)
 
     def back(steps):
@@ -224,18 +214,17 @@
         return lax.ppermute(value, "core", [(0, 1), (1, 0)])
 
     two = lax.ppermute(pay, SHARD, back(lambda s: 2))
+    near_grads = lax.all_to_all(grad_t, "x", 0, 0, tiled=True)
+    near = lax.ppermute(pay, SHARD, back(lambda s: 3 if s % 2 else 1))
     four = lax.ppermute(pay, SHARD, back(lambda s: 4))
-    near = lax.ppermute(pay, SHARD, back(lambda s: 3 if s % 2 else 1))
-    grads = [grad_t]
-    for step in range(1, N_X):
-        around = [(s, (s + step) % N_X) for s in range(N_X)]
-        grads.append(lax.ppermute(grad_t, "x", around))
     cross = swap(two)
-    far = swap(pick(place, grads))
     attention, heads = attend(index.reshape(1), queries, [pay, two, four, near, cross])
-    mine = lax.all_to_all(heads, "x", 0, 0, tiled=True)
-    term = weight_term(place, grads, far, mine, swap(mine))
-    terms = lax.all_to_all(term.reshape(N_REST, ROWS, HD), REST, 0, 0, tiled=True)
+    far_grads = swap(near_grads)
+    mixed = lax.all_to_all(heads, GROUP, 0, 0, tiled=True)
+    term = weight_term(core.reshape(1), near_grads, far_grads, mixed)
+    terms = lax.all_to_all(
+        term.reshape(N_SHARD * N_ZL, PART, HD), REST, 0, 0, tiled=True
+    )
     parts = lax.all_to_all(total(terms), REP, 0, 0, tiled=True)
     return attention, assemble(parts)
 

time: 109 us -> 109 us (level)
  blocking collectives: 44.6 us -> 78 us
  starting transfers between devices: 38.3 us -> 20.6 us
  waiting for transfers between devices: 14.6 us -> 2.24 us
  local copies, waits for them, and re-layouts: 1.95 us -> 0.01 us
    all_to_all x1 -> x3, blocking collectives: 32 us -> 66.4 us  [the longest x1 34.1 us: step(): lax.all_to_all(term.reshape(N_SHARD * N_ZL, PART, HD), REST, 0, 0, tiled=...]
    ppermute x3 -> x0, waiting for transfers between devices: 11.3 us -> none  [step(): grads.append(lax.ppermute(grad_t, 'x', around))]
    ppermute x3 -> x0, starting transfers between devices: 10.7 us -> none  [step(): grads.append(lax.ppermute(grad_t, 'x', around))]
    all_to_all x1 -> x0, starting transfers between devices: 4.41 us -> none  [step(): mine = lax.all_to_all(heads, 'x', 0, 0, tiled=True)]
    ppermute x3 -> x2, starting transfers between devices: 6.96 us -> 4.09 us  [swap(): return lax.ppermute(value, 'core', [(0, 1), (1, 0)])]
    unnamed x6 -> x4, local copies, waits for them, and re-layouts: 1.95 us -> 0.01 us
    ppermute x3 -> x2, waiting for transfers between devices: 1.51 us -> 0.01 us  [swap(): return lax.ppermute(value, 'core', [(0, 1), (1, 0)])]
    pallas_call x3 -> x2, Pallas kernels: 1.92 us -> 0.8 us  [the longest x1 0.71 us: weight_term(): pl.pallas_call(term_kernel, out_shape=jax.ShapeDtypeStruct((N_SHARD, N_ZL...]
  transfers between devices with their start and end apart: 10 -> 5, of which waited for: 6 -> 2; matrix products, arithmetic and copies ran while one was open for 0% -> 0% of each run, Pallas kernels for 1% -> 3%
where the time goes in v4:
time: 109 us
  blocking collectives  78 us (72%)
  starting transfers between devices  20.6 us (19%)
  Pallas kernels  6.99 us (6%)
  waiting for transfers between devices  2.24 us (2%)
    all_to_all x1, blocking collectives, step(): lax.all_to_all(term.reshape(N_SHARD * N_ZL, PART, HD), REST, 0, 0, tiled=...  34.1 us
    all_to_all x1, blocking collectives, step(): near_grads = lax.all_to_all(grad_t, 'x', 0, 0, tiled=True)  19.5 us
    all_to_all x1, blocking collectives, step(): mixed = lax.all_to_all(heads, GROUP, 0, 0, tiled=True)  12.8 us
    all_to_all x1, blocking collectives, step(): parts = lax.all_to_all(total(terms), REP, 0, 0, tiled=True)  11.7 us
    ppermute x1, starting transfers between devices, step(): two = lax.ppermute(pay, SHARD, back(lambda s: 2))  10.9 us
    ppermute x2, starting transfers between devices, swap(): return lax.ppermute(value, 'core', [(0, 1), (1, 0)])  4.09 us
    ppermute x1, starting transfers between devices, step(): four = lax.ppermute(pay, SHARD, back(lambda s: 4))  3.48 us
    pallas_call x1, Pallas kernels, attend(): pl.pallas_call(attend_kernel, out_shape=(jax.ShapeDtypeStruct((1, TOK, HE...  3.28 us
  transfers between devices with their start and end apart: 5, of which 2 were waited for; matrix products, arithmetic and copies ran while one was open for 0% of the time, Pallas kernels for 3%

profile of v4, /device:TPU:8, one launch (start us, length us, event | category | flops | bytes accessed | tf_op | source)
XLA Modules:
  0.0 108.6 jit_solution(2865193595053583822)
XLA Ops:
  0.6 2.2 %pack.1 = (bf16[136,512]{1,0:T(8,128)(2,1)}, bf16[4,1024,128]{2,1,0:T(8,128)(2,1)}) custom-call(bf16[1,128,256]{2,1,0:T(8,128)(2,1)} %key_ref.1, bf16[1,128,256]{2,1,0:T(8,128)(2,1)} %value_ref.1, s32[1,128]{1,0:T(1,128)} %seg_ref.1, bf16[1,128,1024]{2,1,0:T(8,128)(2,1)} %grad_ref.1), custom_call_target="tpu_custom_call" | custom-call | bytes 1048576 | tf_op jit(solution)/shard_map/pack/pallas_call | solution.py:60
  2.8 0.0 copy-start.1
  2.8 0.0 copy-start
  2.8 19.5 %all_to_all.20.near_ref = bf16[4,1024,128]{2,1,0:T(8,128)(2,1)S(1)} all-to-all(bf16[4,1024,128]{2,1,0:T(8,128)(2,1)} %get-tuple-element.8), channel_id=1, replica_groups=mesh['x'=4,'zl'=4,'yz'=16,'core'=2] {'x'}, dimensions={0} | all-to-all | bytes 2097152 | tf_op jit(solution)/shard_map/all_to_all | solution.py:217
  22.3 1.9 %collective-permute-start.4 = (bf16[4,1024,128]{2,1,0:T(8,128)(2,1)S(1)}, bf16[4,1024,128]{2,1,0:T(8,128)(2,1)S(1)}, u32[]{:S(2)}, u32[]{:S(2)}) collective-permute-start(bf16[4,1024,128]{2,1,0:T(8,128)(2,1)S(1)} %all_to_all.20.near_ref), channel_id=1, source_target_pairs={{0,1},{1,0},{2,3},{3,2},{4,5},{5,4},{6,7},{7,6},{8,9},{9,8},{10,11... | collective-permute-start | bytes 3145736 | tf_op jit(solution)/shard_map/ppermute | solution.py:214
  24.3 0.0 copy-done.1
  24.3 10.9 %collective-permute-start = (bf16[136,512]{1,0:T(8,128)(2,1)S(1)}, bf16[136,512]{1,0:T(8,128)(2,1)S(1)}, u32[]{:S(2)}, u32[]{:S(2)}) collective-permute-start(bf16[136,512]{1,0:T(8,128)(2,1)S(1)} %copy-done.1), channel_id=1, source_target_pairs={{0,2},{1,3},{2,4},{3,5},{4,6},{5,7},{6,8},{7,9},{8,10},{9,11},{10,... | collective-permute-start | bytes 417800 | tf_op jit(solution)/shard_map/ppermute | solution.py:216
  35.2 2.1 %collective-permute-start.2 = (bf16[136,512]{1,0:T(8,128)(2,1)S(1)}, bf16[136,512]{1,0:T(8,128)(2,1)S(1)}, u32[]{:S(2)}, u32[]{:S(2)}) collective-permute-start(bf16[136,512]{1,0:T(8,128)(2,1)S(1)} %copy-done.1), channel_id=1, source_target_pairs={{0,1},{1,4},{2,3},{3,6},{4,5},{5,8},{6,7},{7,10},{8,9},{9,12},{10,... | collective-permute-start | bytes 417800 | tf_op jit(solution)/shard_map/ppermute | solution.py:218
  37.3 3.5 %collective-permute-start.1 = (bf16[136,512]{1,0:T(8,128)(2,1)S(1)}, bf16[136,512]{1,0:T(8,128)(2,1)S(1)}, u32[]{:S(2)}, u32[]{:S(2)}) collective-permute-start(bf16[136,512]{1,0:T(8,128)(2,1)S(1)} %copy-done.1), channel_id=1, source_target_pairs={{0,4},{1,5},{2,6},{3,7},{4,8},{5,9},{6,10},{7,11},{8,12},{9,13},{1... | collective-permute-start | bytes 417800 | tf_op jit(solution)/shard_map/ppermute | solution.py:219
  40.8 0.9 collective-permute-done.refs_1_
  41.7 2.2 %collective-permute-start.3 = (bf16[136,512]{1,0:T(8,128)(2,1)S(1)}, bf16[136,512]{1,0:T(8,128)(2,1)S(1)}, u32[]{:S(2)}, u32[]{:S(2)}) collective-permute-start(bf16[136,512]{1,0:T(8,128)(2,1)S(1)} %collective-permute-done.refs_1_), channel_id=1, source_target_pairs={{0,1},{1,0},{2,3},{3,2},{4,5},{5,4},{6,7},{7,6},{8,9},{9,8},{10,11... | collective-permute-start | bytes 417800 | tf_op jit(solution)/shard_map/ppermute | solution.py:214
  44.0 0.0 collective-permute-done.2.refs_3_
  44.0 1.3 %collective-permute-done.1.refs_2_ = bf16[136,512]{1,0:T(8,128)(2,1)S(1)} collective-permute-done((bf16[136,512]{1,0:T(8,128)(2,1)S(1)}, bf16[136,512]{1,0:T(8,128)(2,1)S(1)}, u32[]{:S(2)}, u32[]{:S(2)}) %collective-permute-start.1) | collective-permute-done | bytes 139296 | tf_op jit(solution)/shard_map/ppermute | solution.py:219
  45.3 0.0 collective-permute-done.3.refs_4_
  45.3 0.0 copy-done
  45.3 3.3 %attend.1 = (bf16[1,128,2048]{2,1,0:T(8,128)(2,1)}, bf16[8,128,256]{2,1,0:T(8,128)(2,1)S(1)}) custom-call(s32[1]{0:T(128)} %bitcast.index_ref, bf16[1,128,2048]{2,1,0:T(8,128)(2,1)S(1)} %copy-done, bf16[136,512]{1,0:T(8,128)(2,1)S(1)} %copy-done.1, bf16[136,512]{1,0:T(8,128)(2,1)S(1)} %collective-permute-done.refs_1_, ...), custom_call_target="tpu_custom_call" | custom-call | flops 700000000 | bytes 3145728 | tf_op jit(solution)/shard_map/attend/pallas_call | solution.py:120
  48.6 12.8 %all_to_all.21.mixed_ref = bf16[8,128,256]{2,1,0:T(8,128)(2,1)S(1)} all-to-all(bf16[8,128,256]{2,1,0:T(8,128)(2,1)S(1)} %get-tuple-element.9), channel_id=1, replica_groups=mesh['x'=4,'zl'=4,'yz'=16,'core'=2] {'x','core'}, dimensions={0} | all-to-all | bytes 1048576 | tf_op jit(solution)/shard_map/all_to_all | solution.py:223
  61.3 0.0 collective-permute-done.4.far_ref
  61.3 0.7 weight_term.1
  62.0 34.1 %all_to_all.22.terms_ref = bf16[128,16,128]{2,1,0:T(8,128)(2,1)S(1)} all-to-all(bf16[128,16,128]{2,1,0:T(8,128)(2,1)S(1)} %bitcast.3), channel_id=1, replica_groups=mesh['x'=4,'zl'=4,'yz'=16,'core'=2] {'yz','core','zl'}, dimensions={0} | all-to-all | bytes 1048576 | tf_op jit(solution)/shard_map/all_to_all | solution.py:225
  96.1 0.1 total.1
  96.2 11.7 %all_to_all.23.parts_ref = bf16[16,2,16,128]{3,2,1,0:T(8,128)(2,1)S(1)} all-to-all(bf16[16,2,16,128]{3,2,1,0:T(8,128)(2,1)S(1)} %total.1), channel_id=1, replica_groups=mesh['x'=4,'zl'=4,'yz'=16,'core'=2] {'x','zl'}, dimensions={0} | all-to-all | bytes 262144 | tf_op jit(solution)/shard_map/all_to_all | solution.py:228
  107.9 0.7 assemble.1
Async XLA Ops:
  2.8 21.4 %copy-start.1 = (bf16[136,512]{1,0:T(8,128)(2,1)S(1)}, bf16[136,512]{1,0:T(8,128)(2,1)}, u32[]{:S(2)}) copy-start(bf16[136,512]{1,0:T(8,128)(2,1)} %get-tuple-element.6.refs_0_) | copy-start | bytes 417796
  2.8 42.4 %copy-start = (bf16[1,128,2048]{2,1,0:T(8,128)(2,1)S(1)}, bf16[1,128,2048]{2,1,0:T(8,128)(2,1)}, u32[]{:S(2)}) copy-start(bf16[1,128,2048]{2,1,0:T(8,128)(2,1)} %query_ref.1) | copy-start | bytes 1572868
  22.3 39.0 %collective-permute-start.4 = (bf16[4,1024,128]{2,1,0:T(8,128)(2,1)S(1)}, bf16[4,1024,128]{2,1,0:T(8,128)(2,1)S(1)}, u32[]{:S(2)}, u32[]{:S(2)}) collective-permute-start(bf16[4,1024,128]{2,1,0:T(8,128)(2,1)S(1)} %all_to_all.20.near_ref), channel_id=1, source_target_pairs={{0,1},{1,0},{2,3},{3,2},{4,5},{5,4},{6,7},{7,6},{8,9},{9,8},{10,11... | collective-permute-start | bytes 3145736 | tf_op jit(solution)/shard_map/ppermute | solution.py:214
  24.3 17.5 %collective-permute-start = (bf16[136,512]{1,0:T(8,128)(2,1)S(1)}, bf16[136,512]{1,0:T(8,128)(2,1)S(1)}, u32[]{:S(2)}, u32[]{:S(2)}) collective-permute-start(bf16[136,512]{1,0:T(8,128)(2,1)S(1)} %copy-done.1), channel_id=1, source_target_pairs={{0,2},{1,3},{2,4},{3,5},{4,6},{5,7},{6,8},{7,9},{8,10},{9,11},{10,... | collective-permute-start | bytes 417800 | tf_op jit(solution)/shard_map/ppermute | solution.py:216
  35.2 8.8 %collective-permute-start.2 = (bf16[136,512]{1,0:T(8,128)(2,1)S(1)}, bf16[136,512]{1,0:T(8,128)(2,1)S(1)}, u32[]{:S(2)}, u32[]{:S(2)}) collective-permute-start(bf16[136,512]{1,0:T(8,128)(2,1)S(1)} %copy-done.1), channel_id=1, source_target_pairs={{0,1},{1,4},{2,3},{3,6},{4,5},{5,8},{6,7},{7,10},{8,9},{9,12},{10,... | collective-permute-start | bytes 417800 | tf_op jit(solution)/shard_map/ppermute | solution.py:218
  37.3 7.9 %collective-permute-start.1 = (bf16[136,512]{1,0:T(8,128)(2,1)S(1)}, bf16[136,512]{1,0:T(8,128)(2,1)S(1)}, u32[]{:S(2)}, u32[]{:S(2)}) collective-permute-start(bf16[136,512]{1,0:T(8,128)(2,1)S(1)} %copy-done.1), channel_id=1, source_target_pairs={{0,4},{1,5},{2,6},{3,7},{4,8},{5,9},{6,10},{7,11},{8,12},{9,13},{1... | collective-permute-start | bytes 417800 | tf_op jit(solution)/shard_map/ppermute | solution.py:219
  41.7 3.5 %collective-permute-start.3 = (bf16[136,512]{1,0:T(8,128)(2,1)S(1)}, bf16[136,512]{1,0:T(8,128)(2,1)S(1)}, u32[]{:S(2)}, u32[]{:S(2)}) collective-permute-start(bf16[136,512]{1,0:T(8,128)(2,1)S(1)} %collective-permute-done.refs_1_), channel_id=1, source_target_pairs={{0,1},{1,0},{2,3},{3,2},{4,5},{5,4},{6,7},{7,6},{8,9},{9,8},{10,11... | collective-permute-start | bytes 417800 | tf_op jit(solution)/shard_map/ppermute | solution.py:214

commit v5 on v3

--- a/solution.py
+++ b/solution.py
@@ -25,10 +25,12 @@
 SIZES = (4, 4, 16, 2)
 REP = ("x", "zl")
 SHARD = ("yz", "core")
+GROUP = ("x", "core")
 REST = ("yz", "zl")
 N_X = 4
 N_ZL = 4
 N_YZ = 16
+N_GROUP = 8
 N_REST = 64
 ROWS = D_WIN // N_SHARD
 HALF = D_WIN // 2
@@ -52,7 +54,9 @@
     pay_ref[TOK:, TOK:] = jnp.zeros((8, 2 * KV - TOK), jnp.bfloat16)
     grad_t = jnp.transpose(grad_ref[0].astype(jnp.float32)).reshape(N_YZ, 2, ROWS, TOK)
     for core in range(2):
-        grad_t_ref[core] = grad_t[:, core].reshape(HALF, TOK).astype(jnp.bfloat16)
+        rows = grad_t[:, core].reshape(HALF, TOK).astype(jnp.bfloat16)
+        for x in range(N_X):
+            grad_t_ref[2 * x + core] = rows
 
 
 def pack(keys, values, segments, grad_output):
@@ -60,31 +64,13 @@
         pack_kernel,
         out_shape=(
             jax.ShapeDtypeStruct((PAY_ROWS, 2 * KV), jnp.bfloat16),
-            jax.ShapeDtypeStruct((2, HALF, TOK), jnp.bfloat16),
+            jax.ShapeDtypeStruct((N_GROUP, HALF, TOK), jnp.bfloat16),
         ),
         in_specs=vmem_specs(4),
         out_specs=tuple(vmem_specs(2)),
         name="pack",
         cost_estimate=pl.CostEstimate(flops=0, bytes_accessed=1 << 20, transcendentals=0),
     )(keys, values, segments, grad_output)
-
-
-def pick_kernel(place_ref, *refs):
-    other = 1 - place_ref[1]
-    for step in range(N_X):
-        refs[N_X][step] = refs[step][other]
-
-
-def pick(place, grads):
-    return pl.pallas_call(
-        pick_kernel,
-        out_shape=jax.ShapeDtypeStruct((N_X, HALF, TOK), jnp.bfloat16),
-        in_specs=[pl.BlockSpec(memory_space=pltpu.SMEM)] + vmem_specs(N_X),
-        out_specs=vmem_specs(1)[0],
-        name="pick",
-        compiler_params=params(8),
-        cost_estimate=pl.CostEstimate(flops=0, bytes_accessed=1 << 20, transcendentals=0),
-    )(place, *grads)
 
 
 def attend_kernel(index_ref, query_ref, *refs):
@@ -151,32 +137,30 @@
     )(index, queries, *pays)
 
 
-def term_kernel(place_ref, *refs):
-    grads, (far_ref, mine_ref, other_ref, out_ref) = refs[:N_X], refs[N_X:]
-    x, core = place_ref[0], place_ref[1]
+def term_kernel(core_ref, grads_ref, mine_ref, other_ref, out_ref):
+    core = core_ref[0]
     term = jnp.zeros((HALF, WIDE), jnp.float32)
-    for step in range(N_X):
-        source = lax.rem(x - step + N_X, N_X)
-        grad = jnp.concatenate([grads[step][core], far_ref[step]], axis=1)
-        mixed = jnp.concatenate([mine_ref[source], other_ref[source]], axis=0)
+    for x in range(N_X):
+        grad = jnp.concatenate([grads_ref[2 * x + core], grads_ref[2 * x + 1 - core]], axis=1)
+        mixed = jnp.concatenate([mine_ref[x], other_ref[x]], axis=0)
         term = term + jnp.dot(grad, mixed, preferred_element_type=jnp.float32)
     term = term.astype(jnp.bfloat16).reshape(N_YZ, ROWS, WIDE)
     for head in range(N_ZL):
         out_ref[:, head] = term[:, :, head * HD : (head + 1) * HD]
 
 
-def weight_term(place, grads, far, mine, other):
+def weight_term(core, grads, mine, other):
     return pl.pallas_call(
         term_kernel,
         out_shape=jax.ShapeDtypeStruct((N_YZ, N_ZL, ROWS, HD), jnp.bfloat16),
-        in_specs=[pl.BlockSpec(memory_space=pltpu.SMEM)] + vmem_specs(N_X + 3),
+        in_specs=[pl.BlockSpec(memory_space=pltpu.SMEM)] + vmem_specs(3),
         out_specs=vmem_specs(1)[0],
         name="weight_term",
         compiler_params=params(24),
         cost_estimate=pl.CostEstimate(
-            flops=2 * HALF * 2 * N_X * TOK * WIDE, bytes_accessed=3 << 20, transcendentals=0
-        ),
-    )(place, *grads, far, mine, other)
+            flops=2 * HALF * N_GROUP * TOK * WIDE, bytes_accessed=3 << 20, transcendentals=0
+        ),
+    )(core, grads, mine, other)
 
 
 def total_kernel(terms_ref, out_ref):
@@ -214,7 +198,6 @@
 def step(queries, keys, values, segments, grad_output):
     core = lax.axis_index("core").astype(jnp.int32)
     index = lax.axis_index("yz").astype(jnp.int32) * 2 + core
-    place = jnp.stack([lax.axis_index("x").astype(jnp.int32), core])
     pay, grad_t = pack(keys, values, segments, grad_output)
 
     def back(steps):
@@ -224,17 +207,14 @@
         return lax.ppermute(value, "core", [(0, 1), (1, 0)])
 
     two = lax.ppermute(pay, SHARD, back(lambda s: 2))
+    grads = lax.all_to_all(grad_t, GROUP, 0, 0, tiled=True)
+    near = lax.ppermute(pay, SHARD, back(lambda s: 3 if s % 2 else 1))
     four = lax.ppermute(pay, SHARD, back(lambda s: 4))
-    near = lax.ppermute(pay, SHARD, back(lambda s: 3 if s % 2 else 1))
-    grads = [grad_t]
-    for step in range(1, N_X):
-        around = [(s, (s + step) % N_X) for s in range(N_X)]
-        grads.append(lax.ppermute(grad_t, "x", around))
     cross = swap(two)
-    far = swap(pick(place, grads))
     attention, heads = attend(index.reshape(1), queries, [pay, two, four, near, cross])
     mine = lax.all_to_all(heads, "x", 0, 0, tiled=True)
-    term = weight_term(place, grads, far, mine, swap(mine))
+    other = swap(mine)
+    term = weight_term(core.reshape(1), grads, mine, other)
     terms = lax.all_to_all(term.reshape(N_REST, ROWS, HD), REST, 0, 0, tiled=True)
     parts = lax.all_to_all(total(terms), REP, 0, 0, tiled=True)
     return attention, assemble(parts)

time: 109 us -> 109 us (level)
  blocking collectives: 44.6 us -> 58.3 us
  starting transfers between devices: 38.3 us -> 24.8 us
    all_to_all x0 -> x1, blocking collectives: none -> 14.2 us  [step(): mine = lax.all_to_all(heads, 'x', 0, 0, tiled=True)]
    all_to_all x1, waiting for transfers between devices: 0.01 us -> 13.5 us  [step(): grads = lax.all_to_all(grad_t, GROUP, 0, 0, tiled=True)]
    ppermute x3 -> x0, waiting for transfers between devices: 11.3 us -> none  [step(): grads.append(lax.ppermute(grad_t, 'x', around))]
    ppermute x3 -> x0, starting transfers between devices: 10.7 us -> none  [step(): grads.append(lax.ppermute(grad_t, 'x', around))]
    ppermute x3 -> x2, starting transfers between devices: 6.96 us -> 4.94 us  [swap(): return lax.ppermute(value, 'core', [(0, 1), (1, 0)])]
    ppermute x3 -> x2, waiting for transfers between devices: 1.51 us -> 0.01 us  [swap(): return lax.ppermute(value, 'core', [(0, 1), (1, 0)])]
  transfers between devices with their start and end apart: 10 -> 6, of which waited for: 6 -> 3; matrix products, arithmetic and copies ran while one was open for 0% -> 0% of each run, Pallas kernels for 1% -> 0%
where the time goes in v5:
time: 109 us; the launch traced here: 108 us
  blocking collectives  58.3 us (53%)
  starting transfers between devices  24.8 us (23%)
  waiting for transfers between devices  15.3 us (14%)
  Pallas kernels  7.01 us (6%)
  local copies, waits for them, and re-layouts  1.95 us (2%)
    all_to_all x1, blocking collectives, step(): lax.all_to_all(term.reshape(N_REST, ROWS, HD), REST, 0, 0, tiled=True)  31.4 us
    all_to_all x1, blocking collectives, step(): mine = lax.all_to_all(heads, 'x', 0, 0, tiled=True)  14.2 us
    all_to_all x1, waiting for transfers between devices, step(): grads = lax.all_to_all(grad_t, GROUP, 0, 0, tiled=True)  13.5 us
    all_to_all x1, blocking collectives, step(): parts = lax.all_to_all(total(terms), REP, 0, 0, tiled=True)  12.7 us
    ppermute x1, starting transfers between devices, step(): two = lax.ppermute(pay, SHARD, back(lambda s: 2))  10.9 us
    ppermute x2, starting transfers between devices, swap(): return lax.ppermute(value, 'core', [(0, 1), (1, 0)])  4.94 us
    all_to_all x1, starting transfers between devices, step(): grads = lax.all_to_all(grad_t, GROUP, 0, 0, tiled=True)  3.56 us
    ppermute x1, starting transfers between devices, step(): four = lax.ppermute(pay, SHARD, back(lambda s: 4))  3.48 us
  transfers between devices with their start and end apart: 6, of which 3 were waited for; matrix products, arithmetic and copies ran while one was open for 0% of the time, Pallas kernels for 0%

profile of v5, /device:TPU:8, one launch (start us, length us, event | category | flops | bytes accessed | tf_op | source)
XLA Modules:
  0.0 108.1 jit_solution(7770334805177298373)
XLA Ops:
  0.6 2.2 %pack.1 = (bf16[136,512]{1,0:T(8,128)(2,1)}, bf16[8,512,128]{2,1,0:T(8,128)(2,1)}) custom-call(bf16[1,128,256]{2,1,0:T(8,128)(2,1)} %key_ref.1, bf16[1,128,256]{2,1,0:T(8,128)(2,1)} %value_ref.1, s32[1,128]{1,0:T(1,128)} %seg_ref.1, bf16[1,128,1024]{2,1,0:T(8,128)(2,1)} %grad_ref.1), custom_call_target="tpu_custom_call" | custom-call | bytes 1048576 | tf_op jit(solution)/shard_map/pack/pallas_call | solution.py:63
  2.8 10.9 %collective-permute-start = (bf16[136,512]{1,0:T(8,128)(2,1)}, bf16[136,512]{1,0:T(8,128)(2,1)S(1)}, u32[]{:S(2)}, u32[]{:S(2)}) collective-permute-start(bf16[136,512]{1,0:T(8,128)(2,1)} %get-tuple-element.6.refs_0_), channel_id=1, source_target_pairs={{0,2},{1,3},{2,4},{3,5},{4,6},{5,7},{6,8},{7,9},{8,10},{9,11},{10,... | collective-permute-start | bytes 417800 | tf_op jit(solution)/shard_map/ppermute | solution.py:209
  13.7 1.9 %collective-permute-start.2 = (bf16[136,512]{1,0:T(8,128)(2,1)}, bf16[136,512]{1,0:T(8,128)(2,1)S(1)}, u32[]{:S(2)}, u32[]{:S(2)}) collective-permute-start(bf16[136,512]{1,0:T(8,128)(2,1)} %get-tuple-element.6.refs_0_), channel_id=1, source_target_pairs={{0,1},{1,4},{2,3},{3,6},{4,5},{5,8},{6,7},{7,10},{8,9},{9,12},{10,... | collective-permute-start | bytes 417800 | tf_op jit(solution)/shard_map/ppermute | solution.py:211
  15.7 3.5 %collective-permute-start.1 = (bf16[136,512]{1,0:T(8,128)(2,1)}, bf16[136,512]{1,0:T(8,128)(2,1)S(1)}, u32[]{:S(2)}, u32[]{:S(2)}) collective-permute-start(bf16[136,512]{1,0:T(8,128)(2,1)} %get-tuple-element.6.refs_0_), channel_id=1, source_target_pairs={{0,4},{1,5},{2,6},{3,7},{4,8},{5,9},{6,10},{7,11},{8,12},{9,13},{1... | collective-permute-start | bytes 417800 | tf_op jit(solution)/shard_map/ppermute | solution.py:212
  19.2 0.7 collective-permute-done.refs_1_
  19.8 2.6 %collective-permute-start.3 = (bf16[136,512]{1,0:T(8,128)(2,1)S(1)}, bf16[136,512]{1,0:T(8,128)(2,1)S(1)}, u32[]{:S(2)}, u32[]{:S(2)}) collective-permute-start(bf16[136,512]{1,0:T(8,128)(2,1)S(1)} %collective-permute-done.refs_1_), channel_id=1, source_target_pairs={{0,1},{1,0},{2,3},{3,2},{4,5},{5,4},{6,7},{7,6},{8,9},{9,8},{10,11... | collective-permute-start | bytes 417800 | tf_op jit(solution)/shard_map/ppermute | solution.py:207
  22.5 0.0 collective-permute-done.2.refs_3_
  22.5 1.1 %collective-permute-done.1.refs_2_ = bf16[136,512]{1,0:T(8,128)(2,1)S(1)} collective-permute-done((bf16[136,512]{1,0:T(8,128)(2,1)}, bf16[136,512]{1,0:T(8,128)(2,1)S(1)}, u32[]{:S(2)}, u32[]{:S(2)}) %collective-permute-start.1) | collective-permute-done | bytes 139296 | tf_op jit(solution)/shard_map/ppermute | solution.py:212
  23.6 0.0 collective-permute-done.3.refs_4_
  23.6 0.0 copy-start
  23.6 1.0 copy-done
  24.7 0.0 copy-start.1
  24.7 0.9 copy-done.1
  25.6 3.3 %attend.1 = (bf16[1,128,2048]{2,1,0:T(8,128)(2,1)}, bf16[4,128,512]{2,1,0:T(8,128)(2,1)S(1)}) custom-call(s32[1]{0:T(128)} %bitcast.index_ref, bf16[1,128,2048]{2,1,0:T(8,128)(2,1)S(1)} %copy-done, bf16[136,512]{1,0:T(8,128)(2,1)S(1)} %copy-done.1, bf16[136,512]{1,0:T(8,128)(2,1)S(1)} %collective-permute-done.refs_1_, ...), custom_call_target="tpu_custom_call" | custom-call | flops 700000000 | bytes 3145728 | tf_op jit(solution)/shard_map/attend/pallas_call | solution.py:123
  28.9 14.2 %all_to_all.20.mine_ref = bf16[4,128,512]{2,1,0:T(8,128)(2,1)S(1)} all-to-all(bf16[4,128,512]{2,1,0:T(8,128)(2,1)S(1)} %get-tuple-element.9), channel_id=1, replica_groups=mesh['x'=4,'zl'=4,'yz'=16,'core'=2] {'x'}, dimensions={0} | all-to-all | bytes 1048576 | tf_op jit(solution)/shard_map/all_to_all | solution.py:215
  43.1 3.6 %all-to-all-start = ((bf16[8,512,128]{2,1,0:T(8,128)(2,1)}), bf16[8,512,128]{2,1,0:T(8,128)(2,1)S(1)}, u32[]{:S(2)}, u32[]{:S(2)}) async-start(bf16[8,512,128]{2,1,0:T(8,128)(2,1)} %get-tuple-element.8), calls=%async_computation | async-start | bytes 2097152 | tf_op jit(solution)/shard_map/all_to_all | solution.py:210
  46.7 2.3 %collective-permute-start.4 = (bf16[4,128,512]{2,1,0:T(8,128)(2,1)S(1)}, bf16[4,128,512]{2,1,0:T(8,128)(2,1)S(1)}, u32[]{:S(2)}, u32[]{:S(2)}) collective-permute-start(bf16[4,128,512]{2,1,0:T(8,128)(2,1)S(1)} %all_to_all.20.mine_ref), channel_id=1, source_target_pairs={{0,1},{1,0},{2,3},{3,2},{4,5},{5,4},{6,7},{7,6},{8,9},{9,8},{10,11... | collective-permute-start | bytes 1572872 | tf_op jit(solution)/shard_map/ppermute | solution.py:207
  49.0 13.5 %all-to-all-done.grads_ref = bf16[8,512,128]{2,1,0:T(8,128)(2,1)S(1)} async-done(((bf16[8,512,128]{2,1,0:T(8,128)(2,1)}), bf16[8,512,128]{2,1,0:T(8,128)(2,1)S(1)}, u32[]{:S(2)}, u32[]{:S(2)}) %all-to-all-start) | async-done | bytes 1048608 | tf_op jit(solution)/shard_map/all_to_all | solution.py:210
  62.5 0.0 collective-permute-done.4.other_ref
  62.5 0.7 weight_term.1
  63.2 31.4 %all_to_all.21.terms_ref = bf16[64,32,128]{2,1,0:T(8,128)(2,1)S(1)} all-to-all(bf16[64,32,128]{2,1,0:T(8,128)(2,1)S(1)} %bitcast.3), channel_id=1, replica_groups=mesh['x'=4,'zl'=4,'yz'=16,'core'=2] {'yz','zl'}, dimensions={0} | all-to-all | bytes 1048576 | tf_op jit(solution)/shard_map/all_to_all | solution.py:218
  94.6 0.1 total.1
  94.7 12.7 %all_to_all.22.parts_ref = bf16[16,32,128]{2,1,0:T(8,128)(2,1)S(1)} all-to-all(bf16[16,32,128]{2,1,0:T(8,128)(2,1)S(1)} %total.1), channel_id=1, replica_groups=mesh['x'=4,'zl'=4,'yz'=16,'core'=2] {'x','zl'}, dimensions={0} | all-to-all | bytes 262144 | tf_op jit(solution)/shard_map/all_to_all | solution.py:219
  107.4 0.7 assemble.1
Async XLA Ops:
  2.8 17.0 %collective-permute-start = (bf16[136,512]{1,0:T(8,128)(2,1)}, bf16[136,512]{1,0:T(8,128)(2,1)S(1)}, u32[]{:S(2)}, u32[]{:S(2)}) collective-permute-start(bf16[136,512]{1,0:T(8,128)(2,1)} %get-tuple-element.6.refs_0_), channel_id=1, source_target_pairs={{0,2},{1,3},{2,4},{3,5},{4,6},{5,7},{6,8},{7,9},{8,10},{9,11},{10,... | collective-permute-start | bytes 417800 | tf_op jit(solution)/shard_map/ppermute | solution.py:209
  13.7 8.8 %collective-permute-start.2 = (bf16[136,512]{1,0:T(8,128)(2,1)}, bf16[136,512]{1,0:T(8,128)(2,1)S(1)}, u32[]{:S(2)}, u32[]{:S(2)}) collective-permute-start(bf16[136,512]{1,0:T(8,128)(2,1)} %get-tuple-element.6.refs_0_), channel_id=1, source_target_pairs={{0,1},{1,4},{2,3},{3,6},{4,5},{5,8},{6,7},{7,10},{8,9},{9,12},{10,... | collective-permute-start | bytes 417800 | tf_op jit(solution)/shard_map/ppermute | solution.py:211
  15.7 7.9 %collective-permute-start.1 = (bf16[136,512]{1,0:T(8,128)(2,1)}, bf16[136,512]{1,0:T(8,128)(2,1)S(1)}, u32[]{:S(2)}, u32[]{:S(2)}) collective-permute-start(bf16[136,512]{1,0:T(8,128)(2,1)} %get-tuple-element.6.refs_0_), channel_id=1, source_target_pairs={{0,4},{1,5},{2,6},{3,7},{4,8},{5,9},{6,10},{7,11},{8,12},{9,13},{1... | collective-permute-start | bytes 417800 | tf_op jit(solution)/shard_map/ppermute | solution.py:212
  19.8 3.8 %collective-permute-start.3 = (bf16[136,512]{1,0:T(8,128)(2,1)S(1)}, bf16[136,512]{1,0:T(8,128)(2,1)S(1)}, u32[]{:S(2)}, u32[]{:S(2)}) collective-permute-start(bf16[136,512]{1,0:T(8,128)(2,1)S(1)} %collective-permute-done.refs_1_), channel_id=1, source_target_pairs={{0,1},{1,0},{2,3},{3,2},{4,5},{5,4},{6,7},{7,6},{8,9},{9,8},{10,11... | collective-permute-start | bytes 417800 | tf_op jit(solution)/shard_map/ppermute | solution.py:207
  23.6 1.0 copy-start
  24.7 0.9 copy-start.1
  43.1 19.4 %all-to-all-start = ((bf16[8,512,128]{2,1,0:T(8,128)(2,1)}), bf16[8,512,128]{2,1,0:T(8,128)(2,1)S(1)}, u32[]{:S(2)}, u32[]{:S(2)}) async-start(bf16[8,512,128]{2,1,0:T(8,128)(2,1)} %get-tuple-element.8), calls=%async_computation | async-start | bytes 2097152 | tf_op jit(solution)/shard_map/all_to_all | solution.py:210
  46.7 15.9 %collective-permute-start.4 = (bf16[4,128,512]{2,1,0:T(8,128)(2,1)S(1)}, bf16[4,128,512]{2,1,0:T(8,128)(2,1)S(1)}, u32[]{:S(2)}, u32[]{:S(2)}) collective-permute-start(bf16[4,128,512]{2,1,0:T(8,128)(2,1)S(1)} %all_to_all.20.mine_ref), channel_id=1, source_target_pairs={{0,1},{1,0},{2,3},{3,2},{4,5},{5,4},{6,7},{7,6},{8,9},{9,8},{10,11... | collective-permute-start | bytes 1572872 | tf_op jit(solution)/shard_map/ppermute | solution.py:207

commit v6 on v5

--- a/solution.py
+++ b/solution.py
@@ -21,15 +21,17 @@
 NEG = -1e30
 EXP2_SCALE = (HD**-0.5) * 1.4426950408889634
 
-AXES = ("x", "zl", "yz", "core")
-SIZES = (4, 4, 16, 2)
+AXES = ("x", "zl", "y", "zh", "core")
+SIZES = (4, 4, 8, 2, 2)
 REP = ("x", "zl")
-SHARD = ("yz", "core")
+SHARD = ("y", "zh", "core")
 GROUP = ("x", "core")
-REST = ("yz", "zl")
+REST = ("zl", "zh", "y")
 N_X = 4
 N_ZL = 4
-N_YZ = 16
+N_Y = 8
+N_ZH = 2
+N_YZ = N_Y * N_ZH
 N_GROUP = 8
 N_REST = 64
 ROWS = D_WIN // N_SHARD
@@ -46,12 +48,26 @@
     return [pl.BlockSpec(memory_space=pltpu.VMEM)] * count
 
 
-def pack_kernel(key_ref, value_ref, seg_ref, grad_ref, pay_ref, grad_t_ref):
+def pack_kernel(key_ref, value_ref, seg_ref, pay_ref):
     pay_ref[:TOK, :KV] = key_ref[0]
     pay_ref[:TOK, KV:] = value_ref[0]
     seg = jnp.broadcast_to(seg_ref[...].astype(jnp.float32), (8, TOK))
     pay_ref[TOK:, :TOK] = seg.astype(jnp.bfloat16)
     pay_ref[TOK:, TOK:] = jnp.zeros((8, 2 * KV - TOK), jnp.bfloat16)
+
+
+def pack(keys, values, segments):
+    return pl.pallas_call(
+        pack_kernel,
+        out_shape=jax.ShapeDtypeStruct((PAY_ROWS, 2 * KV), jnp.bfloat16),
+        in_specs=vmem_specs(3),
+        out_specs=vmem_specs(1)[0],
+        name="pack",
+        cost_estimate=pl.CostEstimate(flops=0, bytes_accessed=1 << 18, transcendentals=0),
+    )(keys, values, segments)
+
+
+def turn_kernel(grad_ref, grad_t_ref):
     grad_t = jnp.transpose(grad_ref[0].astype(jnp.float32)).reshape(N_YZ, 2, ROWS, TOK)
     for core in range(2):
         rows = grad_t[:, core].reshape(HALF, TOK).astype(jnp.bfloat16)
@@ -59,18 +75,15 @@
             grad_t_ref[2 * x + core] = rows
 
 
-def pack(keys, values, segments, grad_output):
-    return pl.pallas_call(
-        pack_kernel,
-        out_shape=(
-            jax.ShapeDtypeStruct((PAY_ROWS, 2 * KV), jnp.bfloat16),
-            jax.ShapeDtypeStruct((N_GROUP, HALF, TOK), jnp.bfloat16),
-        ),
-        in_specs=vmem_specs(4),
-        out_specs=tuple(vmem_specs(2)),
-        name="pack",
+def turn(grad_output):
+    return pl.pallas_call(
+        turn_kernel,
+        out_shape=jax.ShapeDtypeStruct((N_GROUP, HALF, TOK), jnp.bfloat16),
+        in_specs=vmem_specs(1),
+        out_specs=vmem_specs(1)[0],
+        name="turn",
         cost_estimate=pl.CostEstimate(flops=0, bytes_accessed=1 << 20, transcendentals=0),
-    )(keys, values, segments, grad_output)
+    )(grad_output)
 
 
 def attend_kernel(index_ref, query_ref, *refs):
@@ -144,15 +157,16 @@
         grad = jnp.concatenate([grads_ref[2 * x + core], grads_ref[2 * x + 1 - core]], axis=1)
         mixed = jnp.concatenate([mine_ref[x], other_ref[x]], axis=0)
         term = term + jnp.dot(grad, mixed, preferred_element_type=jnp.float32)
-    term = term.astype(jnp.bfloat16).reshape(N_YZ, ROWS, WIDE)
+    term = term.astype(jnp.bfloat16).reshape(N_Y, N_ZH, ROWS, WIDE)
     for head in range(N_ZL):
-        out_ref[:, head] = term[:, :, head * HD : (head + 1) * HD]
+        for zh in range(N_ZH):
+            out_ref[head, zh] = term[:, zh, :, head * HD : (head + 1) * HD]
 
 
 def weight_term(core, grads, mine, other):
     return pl.pallas_call(
         term_kernel,
-        out_shape=jax.ShapeDtypeStruct((N_YZ, N_ZL, ROWS, HD), jnp.bfloat16),
+        out_shape=jax.ShapeDtypeStruct((N_ZL, N_ZH, N_Y, ROWS, HD), jnp.bfloat16),
         in_specs=[pl.BlockSpec(memory_space=pltpu.SMEM)] + vmem_specs(3),
         out_specs=vmem_specs(1)[0],
         name="weight_term",
@@ -197,8 +211,8 @@
 
 def step(queries, keys, values, segments, grad_output):
     core = lax.axis_index("core").astype(jnp.int32)
-    index = lax.axis_index("yz").astype(jnp.int32) * 2 + core
-    pay, grad_t = pack(keys, values, segments, grad_output)
+    index = lax.axis_index(SHARD).astype(jnp.int32)
+    pay = pack(keys, values, segments)
 
     def back(steps):
         return [(s, s + steps(s)) for s in range(N_SHARD) if s + steps(s) < N_SHARD]
@@ -207,7 +221,7 @@
         return lax.ppermute(value, "core", [(0, 1), (1, 0)])
 
     two = lax.ppermute(pay, SHARD, back(lambda s: 2))
-    grads = lax.all_to_all(grad_t, GROUP, 0, 0, tiled=True)
+    grads = lax.all_to_all(turn(grad_output), GROUP, 0, 0, tiled=True)
     near = lax.ppermute(pay, SHARD, back(lambda s: 3 if s % 2 else 1))
     four = lax.ppermute(pay, SHARD, back(lambda s: 4))
     cross = swap(two)

time: 109 us -> 108 us (level)
  blocking collectives: 58.3 us -> 43.7 us
  waiting for transfers between devices: 15.3 us -> 23.1 us
  starting transfers between devices: 24.8 us -> 29.4 us
  Pallas kernels: 7.01 us -> 8.63 us
    all_to_all x1 -> x0, blocking collectives: 14.2 us -> none  [step(): mine = lax.all_to_all(heads, 'x', 0, 0, tiled=True)]
    all_to_all x1 -> x2, waiting for transfers between devices: 13.5 us -> 21.4 us  [the longest x1 13.5 us: step(): grads = lax.all_to_all(turn(grad_output), GROUP, 0, 0, tiled=True)]
    all_to_all x1 -> x2, starting transfers between devices: 3.56 us -> 7.86 us  [the longest x1 4.31 us: step(): mine = lax.all_to_all(heads, 'x', 0, 0, tiled=True)]
    pallas_call x2 -> x3, Pallas kernels: 2.9 us -> 4.34 us  [the longest x1 2.09 us: turn(): pl.pallas_call(turn_kernel, out_shape=jax.ShapeDtypeStruct((N_GROUP, HALF...]
    ppermute x1, waiting for transfers between devices: 1.1 us -> 0.01 us  [step(): four = lax.ppermute(pay, SHARD, back(lambda s: 4))]
  transfers between devices with their start and end apart: 6 -> 7, of which waited for: 3 -> 4; matrix products, arithmetic and copies ran while one was open for 0% -> 0% of each run, Pallas kernels for 0% -> 2%
where the time goes in v6:
time: 108 us
  blocking collectives  43.7 us (40%)
  starting transfers between devices  29.4 us (27%)
  waiting for transfers between devices  23.1 us (21%)
  Pallas kernels  8.63 us (8%)
  local copies, waits for them, and re-layouts  1.95 us (2%)
    all_to_all x1, blocking collectives, step(): lax.all_to_all(term.reshape(N_REST, ROWS, HD), REST, 0, 0, tiled=True)  31.6 us
    all_to_all x1, waiting for transfers between devices, step(): grads = lax.all_to_all(turn(grad_output), GROUP, 0, 0, tiled=True)  13.5 us
    all_to_all x1, blocking collectives, step(): parts = lax.all_to_all(total(terms), REP, 0, 0, tiled=True)  12.2 us
    ppermute x1, starting transfers between devices, step(): two = lax.ppermute(pay, SHARD, back(lambda s: 2))  10.9 us
    all_to_all x1, waiting for transfers between devices, step(): mine = lax.all_to_all(heads, 'x', 0, 0, tiled=True)  7.83 us
    ppermute x2, starting transfers between devices, swap(): return lax.ppermute(value, 'core', [(0, 1), (1, 0)])  5.22 us
    all_to_all x1, starting transfers between devices, step(): mine = lax.all_to_all(heads, 'x', 0, 0, tiled=True)  4.31 us
    all_to_all x1, starting transfers between devices, step(): grads = lax.all_to_all(turn(grad_output), GROUP, 0, 0, tiled=True)  3.56 us
  transfers between devices with their start and end apart: 7, of which 4 were waited for; matrix products, arithmetic and copies ran while one was open for 0% of the time, Pallas kernels for 2%

profile of v6, /device:TPU:8, one launch (start us, length us, event | category | flops | bytes accessed | tf_op | source)
XLA Modules:
  0.0 107.5 jit_solution(3697379852643516834)
XLA Ops:
  0.6 1.5 %pack.1.refs_0_ = bf16[136,512]{1,0:T(8,128)(2,1)} custom-call(bf16[1,128,256]{2,1,0:T(8,128)(2,1)} %key_ref.1, bf16[1,128,256]{2,1,0:T(8,128)(2,1)} %value_ref.1, s32[1,128]{1,0:T(1,128)} %seg_ref.1), custom_call_target="tpu_custom_call" | custom-call | bytes 262144 | tf_op jit(solution)/shard_map/pack/pallas_call | solution.py:60
  2.2 10.9 %collective-permute-start = (bf16[136,512]{1,0:T(8,128)(2,1)}, bf16[136,512]{1,0:T(8,128)(2,1)S(1)}, u32[]{:S(2)}, u32[]{:S(2)}) collective-permute-start(bf16[136,512]{1,0:T(8,128)(2,1)} %pack.1.refs_0_), channel_id=1, source_target_pairs={{0,2},{1,3},{2,4},{3,5},{4,6},{5,7},{6,8},{7,9},{8,10},{9,11},{10,... | collective-permute-start | bytes 417800 | tf_op jit(solution)/shard_map/ppermute | solution.py:223
  13.1 3.5 %collective-permute-start.1 = (bf16[136,512]{1,0:T(8,128)(2,1)}, bf16[136,512]{1,0:T(8,128)(2,1)S(1)}, u32[]{:S(2)}, u32[]{:S(2)}) collective-permute-start(bf16[136,512]{1,0:T(8,128)(2,1)} %pack.1.refs_0_), channel_id=1, source_target_pairs={{0,4},{1,5},{2,6},{3,7},{4,8},{5,9},{6,10},{7,11},{8,12},{9,13},{1... | collective-permute-start | bytes 417800 | tf_op jit(solution)/shard_map/ppermute | solution.py:226
  16.6 1.9 %collective-permute-start.2 = (bf16[136,512]{1,0:T(8,128)(2,1)}, bf16[136,512]{1,0:T(8,128)(2,1)S(1)}, u32[]{:S(2)}, u32[]{:S(2)}) collective-permute-start(bf16[136,512]{1,0:T(8,128)(2,1)} %pack.1.refs_0_), channel_id=1, source_target_pairs={{0,1},{1,4},{2,3},{3,6},{4,5},{5,8},{6,7},{7,10},{8,9},{9,12},{10,... | collective-permute-start | bytes 417800 | tf_op jit(solution)/shard_map/ppermute | solution.py:225
  18.5 0.7 collective-permute-done.refs_1_
  19.2 2.9 %collective-permute-start.3 = (bf16[136,512]{1,0:T(8,128)(2,1)S(1)}, bf16[136,512]{1,0:T(8,128)(2,1)S(1)}, u32[]{:S(2)}, u32[]{:S(2)}) collective-permute-start(bf16[136,512]{1,0:T(8,128)(2,1)S(1)} %collective-permute-done.refs_1_), channel_id=1, source_target_pairs={{0,1},{1,0},{2,3},{3,2},{4,5},{5,4},{6,7},{7,6},{8,9},{9,8},{10,11... | collective-permute-start | bytes 417800 | tf_op jit(solution)/shard_map/ppermute | solution.py:221
  22.1 0.0 collective-permute-done.1.refs_2_
  22.1 1.0 collective-permute-done.2.refs_3_
  23.2 0.0 collective-permute-done.3.refs_4_
  23.2 0.0 copy-start
  23.2 0.9 copy-done
  24.1 0.0 copy-start.1
  24.1 1.0 copy-done.1
  25.1 3.5 %attend.1 = (bf16[1,128,2048]{2,1,0:T(8,128)(2,1)}, bf16[4,128,512]{2,1,0:T(8,128)(2,1)}) custom-call(s32[1]{0:T(128)} %bitcast.index_ref, bf16[1,128,2048]{2,1,0:T(8,128)(2,1)S(1)} %copy-done.1, bf16[136,512]{1,0:T(8,128)(2,1)S(1)} %copy-done, bf16[136,512]{1,0:T(8,128)(2,1)S(1)} %collective-permute-done.refs_1_, ...), custom_call_target="tpu_custom_call" | custom-call | flops 700000000 | bytes 3145728 | tf_op jit(solution)/shard_map/attend/pallas_call | solution.py:136
  28.6 4.3 %all-to-all-start.1 = ((bf16[4,128,512]{2,1,0:T(8,128)(2,1)}), bf16[4,128,512]{2,1,0:T(8,128)(2,1)S(1)}, u32[]{:S(2)}, u32[]{:S(2)}) async-start(bf16[4,128,512]{2,1,0:T(8,128)(2,1)} %get-tuple-element.5), calls=%async_computation.1 | async-start | bytes 1048576 | tf_op jit(solution)/shard_map/all_to_all | solution.py:229
  32.9 2.1 %turn.1 = bf16[8,512,128]{2,1,0:T(8,128)(2,1)} custom-call(bf16[1,128,1024]{2,1,0:T(8,128)(2,1)} %grad_ref.1), custom_call_target="tpu_custom_call" | custom-call | bytes 1048576 | tf_op jit(solution)/shard_map/turn/pallas_call | solution.py:79
  35.0 7.8 %all-to-all-done.1.mine_ref = bf16[4,128,512]{2,1,0:T(8,128)(2,1)S(1)} async-done(((bf16[4,128,512]{2,1,0:T(8,128)(2,1)}), bf16[4,128,512]{2,1,0:T(8,128)(2,1)S(1)}, u32[]{:S(2)}, u32[]{:S(2)}) %all-to-all-start.1) | async-done | bytes 524320 | tf_op jit(solution)/shard_map/all_to_all | solution.py:229
  42.8 3.6 %all-to-all-start = ((bf16[8,512,128]{2,1,0:T(8,128)(2,1)}), bf16[8,512,128]{2,1,0:T(8,128)(2,1)S(1)}, u32[]{:S(2)}, u32[]{:S(2)}) async-start(bf16[8,512,128]{2,1,0:T(8,128)(2,1)} %turn.1), calls=%async_computation | async-start | bytes 2097152 | tf_op jit(solution)/shard_map/all_to_all | solution.py:224
  46.4 2.3 %collective-permute-start.4 = (bf16[4,128,512]{2,1,0:T(8,128)(2,1)S(1)}, bf16[4,128,512]{2,1,0:T(8,128)(2,1)S(1)}, u32[]{:S(2)}, u32[]{:S(2)}) collective-permute-start(bf16[4,128,512]{2,1,0:T(8,128)(2,1)S(1)} %all-to-all-done.1.mine_ref), channel_id=1, source_target_pairs={{0,1},{1,0},{2,3},{3,2},{4,5},{5,4},{6,7},{7,6},{8,9},{9,8},{10,11... | collective-permute-start | bytes 1572872 | tf_op jit(solution)/shard_map/ppermute | solution.py:221
  48.7 13.5 %all-to-all-done.grads_ref = bf16[8,512,128]{2,1,0:T(8,128)(2,1)S(1)} async-done(((bf16[8,512,128]{2,1,0:T(8,128)(2,1)}), bf16[8,512,128]{2,1,0:T(8,128)(2,1)S(1)}, u32[]{:S(2)}, u32[]{:S(2)}) %all-to-all-start) | async-done | bytes 1048608 | tf_op jit(solution)/shard_map/all_to_all | solution.py:224
  62.3 0.0 collective-permute-done.4.other_ref
  62.3 0.7 weight_term.1
  63.0 31.6 %all_to_all.20.terms_ref = bf16[64,32,128]{2,1,0:T(8,128)(2,1)S(1)} all-to-all(bf16[64,32,128]{2,1,0:T(8,128)(2,1)S(1)} %bitcast.3), channel_id=1, replica_groups=mesh['x'=4,'zl'=4,'y'=8,'zh'=2,'core'=2] {'zl','zh','y'}, dimensions={0} | all-to-all | bytes 1048576 | tf_op jit(solution)/shard_map/all_to_all | solution.py:232
  94.5 0.1 total.1
  94.6 12.2 %all_to_all.21.parts_ref = bf16[16,32,128]{2,1,0:T(8,128)(2,1)S(1)} all-to-all(bf16[16,32,128]{2,1,0:T(8,128)(2,1)S(1)} %total.1), channel_id=1, replica_groups=mesh['x'=4,'zl'=4,'y'=8,'zh'=2,'core'=2] {'x','zl'}, dimensions={0} | all-to-all | bytes 262144 | tf_op jit(solution)/shard_map/all_to_all | solution.py:233
  106.8 0.7 assemble.1
Async XLA Ops:
  2.2 17.0 %collective-permute-start = (bf16[136,512]{1,0:T(8,128)(2,1)}, bf16[136,512]{1,0:T(8,128)(2,1)S(1)}, u32[]{:S(2)}, u32[]{:S(2)}) collective-permute-start(bf16[136,512]{1,0:T(8,128)(2,1)} %pack.1.refs_0_), channel_id=1, source_target_pairs={{0,2},{1,3},{2,4},{3,5},{4,6},{5,7},{6,8},{7,9},{8,10},{9,11},{10,... | collective-permute-start | bytes 417800 | tf_op jit(solution)/shard_map/ppermute | solution.py:223
  13.1 9.0 %collective-permute-start.1 = (bf16[136,512]{1,0:T(8,128)(2,1)}, bf16[136,512]{1,0:T(8,128)(2,1)S(1)}, u32[]{:S(2)}, u32[]{:S(2)}) collective-permute-start(bf16[136,512]{1,0:T(8,128)(2,1)} %pack.1.refs_0_), channel_id=1, source_target_pairs={{0,4},{1,5},{2,6},{3,7},{4,8},{5,9},{6,10},{7,11},{8,12},{9,13},{1... | collective-permute-start | bytes 417800 | tf_op jit(solution)/shard_map/ppermute | solution.py:226
  16.6 6.6 %collective-permute-start.2 = (bf16[136,512]{1,0:T(8,128)(2,1)}, bf16[136,512]{1,0:T(8,128)(2,1)S(1)}, u32[]{:S(2)}, u32[]{:S(2)}) collective-permute-start(bf16[136,512]{1,0:T(8,128)(2,1)} %pack.1.refs_0_), channel_id=1, source_target_pairs={{0,1},{1,4},{2,3},{3,6},{4,5},{5,8},{6,7},{7,10},{8,9},{9,12},{10,... | collective-permute-start | bytes 417800 | tf_op jit(solution)/shard_map/ppermute | solution.py:225
  19.2 4.0 %collective-permute-start.3 = (bf16[136,512]{1,0:T(8,128)(2,1)S(1)}, bf16[136,512]{1,0:T(8,128)(2,1)S(1)}, u32[]{:S(2)}, u32[]{:S(2)}) collective-permute-start(bf16[136,512]{1,0:T(8,128)(2,1)S(1)} %collective-permute-done.refs_1_), channel_id=1, source_target_pairs={{0,1},{1,0},{2,3},{3,2},{4,5},{5,4},{6,7},{7,6},{8,9},{9,8},{10,11... | collective-permute-start | bytes 417800 | tf_op jit(solution)/shard_map/ppermute | solution.py:221
  23.2 0.9 copy-start
  24.1 1.0 copy-start.1
  28.6 14.2 %all-to-all-start.1 = ((bf16[4,128,512]{2,1,0:T(8,128)(2,1)}), bf16[4,128,512]{2,1,0:T(8,128)(2,1)S(1)}, u32[]{:S(2)}, u32[]{:S(2)}) async-start(bf16[4,128,512]{2,1,0:T(8,128)(2,1)} %get-tuple-element.5), calls=%async_computation.1 | async-start | bytes 1048576 | tf_op jit(solution)/shard_map/all_to_all | solution.py:229
  42.8 19.4 %all-to-all-start = ((bf16[8,512,128]{2,1,0:T(8,128)(2,1)}), bf16[8,512,128]{2,1,0:T(8,128)(2,1)S(1)}, u32[]{:S(2)}, u32[]{:S(2)}) async-start(bf16[8,512,128]{2,1,0:T(8,128)(2,1)} %turn.1), calls=%async_computation | async-start | bytes 2097152 | tf_op jit(solution)/shard_map/all_to_all | solution.py:224
  46.4 15.9 %collective-permute-start.4 = (bf16[4,128,512]{2,1,0:T(8,128)(2,1)S(1)}, bf16[4,128,512]{2,1,0:T(8,128)(2,1)S(1)}, u32[]{:S(2)}, u32[]{:S(2)}) collective-permute-start(bf16[4,128,512]{2,1,0:T(8,128)(2,1)S(1)} %all-to-all-done.1.mine_ref), channel_id=1, source_target_pairs={{0,1},{1,0},{2,3},{3,2},{4,5},{5,4},{6,7},{7,6},{8,9},{9,8},{10,11... | collective-permute-start | bytes 1572872 | tf_op jit(solution)/shard_map/ppermute | solution.py:221

commit v7 on v4

--- a/solution.py
+++ b/solution.py
@@ -21,15 +21,17 @@
 NEG = -1e30
 EXP2_SCALE = (HD**-0.5) * 1.4426950408889634
 
-AXES = ("x", "zl", "yz", "core")
-SIZES = (4, 4, 16, 2)
+AXES = ("x", "zl", "y", "zh", "core")
+SIZES = (4, 4, 8, 2, 2)
 REP = ("x", "zl")
-SHARD = ("yz", "core")
+SHARD = ("y", "zh", "core")
 GROUP = ("x", "core")
-REST = ("yz", "core", "zl")
+REST = ("zl", "core", "zh", "y")
 N_X = 4
 N_ZL = 4
-N_YZ = 16
+N_Y = 8
+N_ZH = 2
+N_YZ = N_Y * N_ZH
 N_GROUP = 8
 ROWS = D_WIN // N_SHARD
 PART = ROWS // 2
@@ -141,16 +143,19 @@
         grad = jnp.concatenate([near_ref[x], far_ref[x]], axis=1)
         mixed = jnp.concatenate([mixed_ref[2 * x + core], mixed_ref[2 * x + 1 - core]], axis=0)
         term = term + jnp.dot(grad, mixed, preferred_element_type=jnp.float32)
-    term = term.astype(jnp.bfloat16).reshape(N_SHARD, 2, PART, WIDE)
+    term = term.astype(jnp.bfloat16).reshape(N_Y, N_ZH, 2, 2, PART, WIDE)
     for part in range(2):
         for head in range(2):
-            out_ref[:, 2 * part + head] = term[:, part, :, head * HD : (head + 1) * HD]
+            columns = slice(head * HD, (head + 1) * HD)
+            for to_core in range(2):
+                for zh in range(N_ZH):
+                    out_ref[2 * part + head, to_core, zh] = term[:, zh, to_core, part, :, columns]
 
 
 def weight_term(core, near, far, mixed):
     return pl.pallas_call(
         term_kernel,
-        out_shape=jax.ShapeDtypeStruct((N_SHARD, N_ZL, PART, HD), jnp.bfloat16),
+        out_shape=jax.ShapeDtypeStruct((N_ZL, 2, N_ZH, N_Y, PART, HD), jnp.bfloat16),
         in_specs=[pl.BlockSpec(memory_space=pltpu.SMEM)] + vmem_specs(3),
         out_specs=vmem_specs(1)[0],
         name="weight_term",
@@ -162,9 +167,9 @@
 
 
 def total_kernel(terms_ref, out_ref):
-    terms = terms_ref[...].reshape(N_YZ, 2, N_ZL, PART, HD)
+    terms = terms_ref[...].reshape(N_ZL, 2, N_YZ, PART, HD)
     for core in range(2):
-        own = terms[:, core].reshape(N_YZ * N_ZL, PART, HD).astype(jnp.float32)
+        own = terms[:, core].reshape(N_ZL * N_YZ, PART, HD).astype(jnp.float32)
         total = jnp.sum(own, axis=0).astype(jnp.bfloat16)
         out_ref[:, core] = jnp.broadcast_to(total[None], (N_REP, PART, HD))
 
@@ -204,7 +209,7 @@
 
 def step(queries, keys, values, segments, grad_output):
     core = lax.axis_index("core").astype(jnp.int32)
-    index = lax.axis_index("yz").astype(jnp.int32) * 2 + core
+    index = lax.axis_index(SHARD).astype(jnp.int32)
     pay, grad_t = pack(keys, values, segments, grad_output)
 
     def back(steps):

time: 109 us -> 111 us (1.018)
  the two profiles are of different devices: /device:TPU:8 before, /device:TPU:1 now
where the time goes in v7:
time: 111 us; the launch traced here: 110 us
  blocking collectives  73.8 us (66%)
  starting transfers between devices  27.4 us (25%)
  Pallas kernels  7 us (6%)
  waiting for transfers between devices  1.31 us (1%)
    all_to_all x1, blocking collectives, step(): lax.all_to_all(term.reshape(N_SHARD * N_ZL, PART, HD), REST, 0, 0, tiled=...  37.2 us
    all_to_all x1, blocking collectives, step(): near_grads = lax.all_to_all(grad_t, 'x', 0, 0, tiled=True)  14.7 us
    all_to_all x1, blocking collectives, step(): mixed = lax.all_to_all(heads, GROUP, 0, 0, tiled=True)  11.8 us
    ppermute x2, starting transfers between devices, swap(): return lax.ppermute(value, 'core', [(0, 1), (1, 0)])  10.5 us
    ppermute x1, starting transfers between devices, step(): two = lax.ppermute(pay, SHARD, back(lambda s: 2))  10.3 us
    all_to_all x1, blocking collectives, step(): parts = lax.all_to_all(total(terms), REP, 0, 0, tiled=True)  10 us
    ppermute x1, starting transfers between devices, step(): near = lax.ppermute(pay, SHARD, back(lambda s: 3 if s % 2 else 1))  3.38 us
    pallas_call x1, Pallas kernels, attend(): pl.pallas_call(attend_kernel, out_shape=(jax.ShapeDtypeStruct((1, TOK, HE...  3.29 us
  transfers between devices with their start and end apart: 5, of which 2 were waited for; matrix products, arithmetic and copies ran while one was open for 0% of the time, Pallas kernels for 3%

profile of v7, /device:TPU:1, one launch (start us, length us, event | category | flops | bytes accessed | tf_op | source)
XLA Modules:
  0.0 110.2 jit_solution(10942164043828024856)
XLA Ops:
  0.6 2.2 %pack.1 = (bf16[136,512]{1,0:T(8,128)(2,1)}, bf16[4,1024,128]{2,1,0:T(8,128)(2,1)}) custom-call(bf16[1,128,256]{2,1,0:T(8,128)(2,1)} %key_ref.1, bf16[1,128,256]{2,1,0:T(8,128)(2,1)} %value_ref.1, s32[1,128]{1,0:T(1,128)} %seg_ref.1, bf16[1,128,1024]{2,1,0:T(8,128)(2,1)} %grad_ref.1), custom_call_target="tpu_custom_call" | custom-call | bytes 1048576 | tf_op jit(solution)/shard_map/pack/pallas_call | solution.py:62
  2.8 0.0 copy-start.1
  2.8 0.0 copy-start
  2.8 14.7 %all_to_all.20.near_ref = bf16[4,1024,128]{2,1,0:T(8,128)(2,1)S(1)} all-to-all(bf16[4,1024,128]{2,1,0:T(8,128)(2,1)} %get-tuple-element.8), channel_id=1, replica_groups=mesh['x'=4,'zl'=4,'y'=8,'zh'=2,'core'=2] {'x'}, dimensions={0} | all-to-all | bytes 2097152 | tf_op jit(solution)/shard_map/all_to_all | solution.py:222
  17.5 8.5 %collective-permute-start.4 = (bf16[4,1024,128]{2,1,0:T(8,128)(2,1)S(1)}, bf16[4,1024,128]{2,1,0:T(8,128)(2,1)S(1)}, u32[]{:S(2)}, u32[]{:S(2)}) collective-permute-start(bf16[4,1024,128]{2,1,0:T(8,128)(2,1)S(1)} %all_to_all.20.near_ref), channel_id=1, source_target_pairs={{0,1},{1,0},{2,3},{3,2},{4,5},{5,4},{6,7},{7,6},{8,9},{9,8},{10,11... | collective-permute-start | bytes 3145736 | tf_op jit(solution)/shard_map/ppermute | solution.py:219
  26.1 0.0 copy-done.1
  26.1 10.3 %collective-permute-start = (bf16[136,512]{1,0:T(8,128)(2,1)S(1)}, bf16[136,512]{1,0:T(8,128)(2,1)S(1)}, u32[]{:S(2)}, u32[]{:S(2)}) collective-permute-start(bf16[136,512]{1,0:T(8,128)(2,1)S(1)} %copy-done.1), channel_id=1, source_target_pairs={{0,2},{1,3},{2,4},{3,5},{4,6},{5,7},{6,8},{7,9},{8,10},{9,11},{10,... | collective-permute-start | bytes 417800 | tf_op jit(solution)/shard_map/ppermute | solution.py:221
  36.4 3.4 %collective-permute-start.2 = (bf16[136,512]{1,0:T(8,128)(2,1)S(1)}, bf16[136,512]{1,0:T(8,128)(2,1)S(1)}, u32[]{:S(2)}, u32[]{:S(2)}) collective-permute-start(bf16[136,512]{1,0:T(8,128)(2,1)S(1)} %copy-done.1), channel_id=1, source_target_pairs={{0,1},{1,4},{2,3},{3,6},{4,5},{5,8},{6,7},{7,10},{8,9},{9,12},{10,... | collective-permute-start | bytes 417800 | tf_op jit(solution)/shard_map/ppermute | solution.py:223
  39.8 3.2 %collective-permute-start.1 = (bf16[136,512]{1,0:T(8,128)(2,1)S(1)}, bf16[136,512]{1,0:T(8,128)(2,1)S(1)}, u32[]{:S(2)}, u32[]{:S(2)}) collective-permute-start(bf16[136,512]{1,0:T(8,128)(2,1)S(1)} %copy-done.1), channel_id=1, source_target_pairs={{0,4},{1,5},{2,6},{3,7},{4,8},{5,9},{6,10},{7,11},{8,12},{9,13},{1... | collective-permute-start | bytes 417800 | tf_op jit(solution)/shard_map/ppermute | solution.py:224
  43.0 0.0 collective-permute-done.refs_1_
  43.0 1.9 %collective-permute-start.3 = (bf16[136,512]{1,0:T(8,128)(2,1)S(1)}, bf16[136,512]{1,0:T(8,128)(2,1)S(1)}, u32[]{:S(2)}, u32[]{:S(2)}) collective-permute-start(bf16[136,512]{1,0:T(8,128)(2,1)S(1)} %collective-permute-done.refs_1_), channel_id=1, source_target_pairs={{0,1},{1,0},{2,3},{3,2},{4,5},{5,4},{6,7},{7,6},{8,9},{9,8},{10,11... | collective-permute-start | bytes 417800 | tf_op jit(solution)/shard_map/ppermute | solution.py:219
  44.9 0.0 collective-permute-done.2.refs_3_
  45.0 1.0 collective-permute-done.1.refs_2_
  46.0 0.3 collective-permute-done.3.refs_4_
  46.3 0.0 copy-done
  46.3 3.3 %attend.1 = (bf16[1,128,2048]{2,1,0:T(8,128)(2,1)}, bf16[8,128,256]{2,1,0:T(8,128)(2,1)S(1)}) custom-call(s32[1]{0:T(128)} %bitcast.index_ref, bf16[1,128,2048]{2,1,0:T(8,128)(2,1)S(1)} %copy-done, bf16[136,512]{1,0:T(8,128)(2,1)S(1)} %copy-done.1, bf16[136,512]{1,0:T(8,128)(2,1)S(1)} %collective-permute-done.refs_1_, ...), custom_call_target="tpu_custom_call" | custom-call | flops 700000000 | bytes 3145728 | tf_op jit(solution)/shard_map/attend/pallas_call | solution.py:122
  49.6 11.8 %all_to_all.21.mixed_ref = bf16[8,128,256]{2,1,0:T(8,128)(2,1)S(1)} all-to-all(bf16[8,128,256]{2,1,0:T(8,128)(2,1)S(1)} %get-tuple-element.9), channel_id=1, replica_groups=mesh['x'=4,'zl'=4,'y'=8,'zh'=2,'core'=2] {'x','core'}, dimensions={0} | all-to-all | bytes 1048576 | tf_op jit(solution)/shard_map/all_to_all | solution.py:228
  61.4 0.0 collective-permute-done.4.far_ref
  61.4 0.7 weight_term.1
  62.1 37.2 %all_to_all.22.terms_ref = bf16[128,16,128]{2,1,0:T(8,128)(2,1)S(1)} all-to-all(bf16[128,16,128]{2,1,0:T(8,128)(2,1)S(1)} %bitcast.3), channel_id=1, replica_groups=mesh['x'=4,'zl'=4,'y'=8,'zh'=2,'core'=2] {'zl','core','zh','y'}, dimensions={0} | all-to-all | bytes 1048576 | tf_op jit(solution)/shard_map/all_to_all | solution.py:230
  99.4 0.1 total.1
  99.5 10.0 %all_to_all.23.parts_ref = bf16[16,2,16,128]{3,2,1,0:T(8,128)(2,1)S(1)} all-to-all(bf16[16,2,16,128]{3,2,1,0:T(8,128)(2,1)S(1)} %total.1), channel_id=1, replica_groups=mesh['x'=4,'zl'=4,'y'=8,'zh'=2,'core'=2] {'x','zl'}, dimensions={0} | all-to-all | bytes 262144 | tf_op jit(solution)/shard_map/all_to_all | solution.py:233
  109.5 0.7 assemble.1
Async XLA Ops:
  2.8 23.3 %copy-start.1 = (bf16[136,512]{1,0:T(8,128)(2,1)S(1)}, bf16[136,512]{1,0:T(8,128)(2,1)}, u32[]{:S(2)}) copy-start(bf16[136,512]{1,0:T(8,128)(2,1)} %get-tuple-element.6.refs_0_) | copy-start | bytes 417796
  2.8 43.4 %copy-start = (bf16[1,128,2048]{2,1,0:T(8,128)(2,1)S(1)}, bf16[1,128,2048]{2,1,0:T(8,128)(2,1)}, u32[]{:S(2)}) copy-start(bf16[1,128,2048]{2,1,0:T(8,128)(2,1)} %query_ref.1) | copy-start | bytes 1572868
  17.5 43.9 %collective-permute-start.4 = (bf16[4,1024,128]{2,1,0:T(8,128)(2,1)S(1)}, bf16[4,1024,128]{2,1,0:T(8,128)(2,1)S(1)}, u32[]{:S(2)}, u32[]{:S(2)}) collective-permute-start(bf16[4,1024,128]{2,1,0:T(8,128)(2,1)S(1)} %all_to_all.20.near_ref), channel_id=1, source_target_pairs={{0,1},{1,0},{2,3},{3,2},{4,5},{5,4},{6,7},{7,6},{8,9},{9,8},{10,11... | collective-permute-start | bytes 3145736 | tf_op jit(solution)/shard_map/ppermute | solution.py:219
  26.1 16.9 %collective-permute-start = (bf16[136,512]{1,0:T(8,128)(2,1)S(1)}, bf16[136,512]{1,0:T(8,128)(2,1)S(1)}, u32[]{:S(2)}, u32[]{:S(2)}) collective-permute-start(bf16[136,512]{1,0:T(8,128)(2,1)S(1)} %copy-done.1), channel_id=1, source_target_pairs={{0,2},{1,3},{2,4},{3,5},{4,6},{5,7},{6,8},{7,9},{8,10},{9,11},{10,... | collective-permute-start | bytes 417800 | tf_op jit(solution)/shard_map/ppermute | solution.py:221
  36.4 8.6 %collective-permute-start.2 = (bf16[136,512]{1,0:T(8,128)(2,1)S(1)}, bf16[136,512]{1,0:T(8,128)(2,1)S(1)}, u32[]{:S(2)}, u32[]{:S(2)}) collective-permute-start(bf16[136,512]{1,0:T(8,128)(2,1)S(1)} %copy-done.1), channel_id=1, source_target_pairs={{0,1},{1,4},{2,3},{3,6},{4,5},{5,8},{6,7},{7,10},{8,9},{9,12},{10,... | collective-permute-start | bytes 417800 | tf_op jit(solution)/shard_map/ppermute | solution.py:223
  39.8 6.2 %collective-permute-start.1 = (bf16[136,512]{1,0:T(8,128)(2,1)S(1)}, bf16[136,512]{1,0:T(8,128)(2,1)S(1)}, u32[]{:S(2)}, u32[]{:S(2)}) collective-permute-start(bf16[136,512]{1,0:T(8,128)(2,1)S(1)} %copy-done.1), channel_id=1, source_target_pairs={{0,4},{1,5},{2,6},{3,7},{4,8},{5,9},{6,10},{7,11},{8,12},{9,13},{1... | collective-permute-start | bytes 417800 | tf_op jit(solution)/shard_map/ppermute | solution.py:224
  43.0 3.3 %collective-permute-start.3 = (bf16[136,512]{1,0:T(8,128)(2,1)S(1)}, bf16[136,512]{1,0:T(8,128)(2,1)S(1)}, u32[]{:S(2)}, u32[]{:S(2)}) collective-permute-start(bf16[136,512]{1,0:T(8,128)(2,1)S(1)} %collective-permute-done.refs_1_), channel_id=1, source_target_pairs={{0,1},{1,0},{2,3},{3,2},{4,5},{5,4},{6,7},{7,6},{8,9},{9,8},{10,11... | collective-permute-start | bytes 417800 | tf_op jit(solution)/shard_map/ppermute | solution.py:219

commit v8 on v7

--- a/solution.py
+++ b/solution.py
@@ -36,7 +36,7 @@
 ROWS = D_WIN // N_SHARD
 PART = ROWS // 2
 WIDE = HEADS * HD // N_GROUP
-STACK = 4
+STACK = 8
 
 
 def params(mib):
@@ -47,29 +47,54 @@
     return [pl.BlockSpec(memory_space=pltpu.VMEM)] * count
 
 
-def pack_kernel(key_ref, value_ref, seg_ref, grad_ref, pay_ref, grad_t_ref):
+def pack_kernel(*refs):
+    sources, (pay_out, grad_t_out), held = refs[:4], refs[4:6], refs[6:10]
+    pay_ref, grad_t_ref, sems = refs[10:]
+    copies = [
+        pltpu.make_async_copy(source, here, sems.at[i])
+        for i, (source, here) in enumerate(zip(sources, held))
+    ]
+    for copy in copies:
+        copy.start()
+    key_ref, value_ref, seg_ref, grad_ref = held
+    pay_ref[TOK:, TOK:] = jnp.zeros((8, 2 * KV - TOK), jnp.bfloat16)
+    for copy in copies[:3]:
+        copy.wait()
     pay_ref[:TOK, :KV] = key_ref[0]
     pay_ref[:TOK, KV:] = value_ref[0]
     seg = jnp.broadcast_to(seg_ref[...].astype(jnp.float32), (8, TOK))
     pay_ref[TOK:, :TOK] = seg.astype(jnp.bfloat16)
-    pay_ref[TOK:, TOK:] = jnp.zeros((8, 2 * KV - TOK), jnp.bfloat16)
-    grad_t = jnp.transpose(grad_ref[0].astype(jnp.float32)).astype(jnp.bfloat16)
+    results = [pltpu.make_async_copy(pay_ref, pay_out, sems.at[4])]
+    results[0].start()
+    copies[3].wait()
+    grad_t_ref[...] = jnp.transpose(grad_ref[0].astype(jnp.float32)).astype(jnp.bfloat16)
     for x in range(N_X):
-        grad_t_ref[x] = grad_t
+        results.append(pltpu.make_async_copy(grad_t_ref, grad_t_out.at[x], sems.at[5 + x]))
+        results[-1].start()
+    for result in results:
+        result.wait()
 
 
 def pack(keys, values, segments, grad_output):
+    sources = (keys, values, segments, grad_output)
+    anywhere = pl.BlockSpec(memory_space=pl.ANY)
     return pl.pallas_call(
         pack_kernel,
         out_shape=(
             jax.ShapeDtypeStruct((PAY_ROWS, 2 * KV), jnp.bfloat16),
             jax.ShapeDtypeStruct((N_X, D_WIN, TOK), jnp.bfloat16),
         ),
-        in_specs=vmem_specs(4),
-        out_specs=tuple(vmem_specs(2)),
+        in_specs=[anywhere] * 4,
+        out_specs=(anywhere, anywhere),
+        scratch_shapes=[pltpu.VMEM(source.shape, source.dtype) for source in sources]
+        + [
+            pltpu.VMEM((PAY_ROWS, 2 * KV), jnp.bfloat16),
+            pltpu.VMEM((D_WIN, TOK), jnp.bfloat16),
+            pltpu.SemaphoreType.DMA((5 + N_X,)),
+        ],
         name="pack",
         cost_estimate=pl.CostEstimate(flops=0, bytes_accessed=1 << 20, transcendentals=0),
-    )(keys, values, segments, grad_output)
+    )(*sources)
 
 
 def attend_kernel(index_ref, query_ref, *refs):
@@ -129,7 +154,7 @@
         out_specs=tuple(vmem_specs(2)),
         scratch_shapes=[pltpu.VMEM((TOK, (SPAN + 1) * TOK), jnp.float32)],
         name="attend",
-        compiler_params=params(32),
+        compiler_params=pltpu.CompilerParams(vmem_limit_bytes=32 << 20),
         cost_estimate=pl.CostEstimate(
             flops=700_000_000, bytes_accessed=3 << 20, transcendentals=1_310_720
         ),

time: 111 us -> 110 us (level)
  no operation moved by 1% of the time
where the time goes in v8:
time: 110 us
  blocking collectives  73.8 us (67%)
  starting transfers between devices  27.4 us (25%)
  Pallas kernels  6.67 us (6%)
  waiting for transfers between devices  1.31 us (1%)
    all_to_all x1, blocking collectives, step(): lax.all_to_all(term.reshape(N_SHARD * N_ZL, PART, HD), REST, 0, 0, tiled=...  37.2 us
    all_to_all x1, blocking collectives, step(): near_grads = lax.all_to_all(grad_t, 'x', 0, 0, tiled=True)  14.7 us
    all_to_all x1, blocking collectives, step(): mixed = lax.all_to_all(heads, GROUP, 0, 0, tiled=True)  11.9 us
    ppermute x2, starting transfers between devices, swap(): return lax.ppermute(value, 'core', [(0, 1), (1, 0)])  10.5 us
    ppermute x1, starting transfers between devices, step(): two = lax.ppermute(pay, SHARD, back(lambda s: 2))  10.3 us
    all_to_all x1, blocking collectives, step(): parts = lax.all_to_all(total(terms), REP, 0, 0, tiled=True)  10 us
    ppermute x1, starting transfers between devices, step(): near = lax.ppermute(pay, SHARD, back(lambda s: 3 if s % 2 else 1))  3.38 us
    ppermute x1, starting transfers between devices, step(): four = lax.ppermute(pay, SHARD, back(lambda s: 4))  3.21 us
  transfers between devices with their start and end apart: 5, of which 2 were waited for; matrix products, arithmetic and copies ran while one was open for 0% of the time, Pallas kernels for 3%

profile of v8, /device:TPU:1, one launch (start us, length us, event | category | flops | bytes accessed | tf_op | source)
XLA Modules:
  0.0 109.9 jit_solution(1593487274377238620)
XLA Ops:
  0.6 2.2 %pack.1 = (bf16[136,512]{1,0:T(8,128)(2,1)}, bf16[4,1024,128]{2,1,0:T(8,128)(2,1)}) custom-call(bf16[1,128,256]{2,1,0:T(8,128)(2,1)} %refs_0_.1, bf16[1,128,256]{2,1,0:T(8,128)(2,1)} %refs_1_.1, s32[1,128]{1,0:T(1,128)} %refs_2_.1, bf16[1,128,1024]{2,1,0:T(8,128)(2,1)} %refs_3_.1), custom_call_target="tpu_custom_call" | custom-call | bytes 1048576 | tf_op jit(solution)/shard_map/pack/pallas_call | solution.py:81
  2.9 0.0 copy-start.1
  2.9 0.0 copy-start
  2.9 14.7 %all_to_all.20.near_ref = bf16[4,1024,128]{2,1,0:T(8,128)(2,1)S(1)} all-to-all(bf16[4,1024,128]{2,1,0:T(8,128)(2,1)} %get-tuple-element.8), channel_id=1, replica_groups=mesh['x'=4,'zl'=4,'y'=8,'zh'=2,'core'=2] {'x'}, dimensions={0} | all-to-all | bytes 2097152 | tf_op jit(solution)/shard_map/all_to_all | solution.py:247
  17.6 8.5 %collective-permute-start.4 = (bf16[4,1024,128]{2,1,0:T(8,128)(2,1)S(1)}, bf16[4,1024,128]{2,1,0:T(8,128)(2,1)S(1)}, u32[]{:S(2)}, u32[]{:S(2)}) collective-permute-start(bf16[4,1024,128]{2,1,0:T(8,128)(2,1)S(1)} %all_to_all.20.near_ref), channel_id=1, source_target_pairs={{0,1},{1,0},{2,3},{3,2},{4,5},{5,4},{6,7},{7,6},{8,9},{9,8},{10,11... | collective-permute-start | bytes 3145736 | tf_op jit(solution)/shard_map/ppermute | solution.py:244
  26.1 0.0 copy-done.1
  26.2 10.3 %collective-permute-start = (bf16[136,512]{1,0:T(8,128)(2,1)S(1)}, bf16[136,512]{1,0:T(8,128)(2,1)S(1)}, u32[]{:S(2)}, u32[]{:S(2)}) collective-permute-start(bf16[136,512]{1,0:T(8,128)(2,1)S(1)} %copy-done.1), channel_id=1, source_target_pairs={{0,2},{1,3},{2,4},{3,5},{4,6},{5,7},{6,8},{7,9},{8,10},{9,11},{10,... | collective-permute-start | bytes 417800 | tf_op jit(solution)/shard_map/ppermute | solution.py:246
  36.5 3.4 %collective-permute-start.2 = (bf16[136,512]{1,0:T(8,128)(2,1)S(1)}, bf16[136,512]{1,0:T(8,128)(2,1)S(1)}, u32[]{:S(2)}, u32[]{:S(2)}) collective-permute-start(bf16[136,512]{1,0:T(8,128)(2,1)S(1)} %copy-done.1), channel_id=1, source_target_pairs={{0,1},{1,4},{2,3},{3,6},{4,5},{5,8},{6,7},{7,10},{8,9},{9,12},{10,... | collective-permute-start | bytes 417800 | tf_op jit(solution)/shard_map/ppermute | solution.py:248
  39.9 3.2 %collective-permute-start.1 = (bf16[136,512]{1,0:T(8,128)(2,1)S(1)}, bf16[136,512]{1,0:T(8,128)(2,1)S(1)}, u32[]{:S(2)}, u32[]{:S(2)}) collective-permute-start(bf16[136,512]{1,0:T(8,128)(2,1)S(1)} %copy-done.1), channel_id=1, source_target_pairs={{0,4},{1,5},{2,6},{3,7},{4,8},{5,9},{6,10},{7,11},{8,12},{9,13},{1... | collective-permute-start | bytes 417800 | tf_op jit(solution)/shard_map/ppermute | solution.py:249
  43.1 0.0 collective-permute-done.refs_1_
  43.1 1.9 %collective-permute-start.3 = (bf16[136,512]{1,0:T(8,128)(2,1)S(1)}, bf16[136,512]{1,0:T(8,128)(2,1)S(1)}, u32[]{:S(2)}, u32[]{:S(2)}) collective-permute-start(bf16[136,512]{1,0:T(8,128)(2,1)S(1)} %collective-permute-done.refs_1_), channel_id=1, source_target_pairs={{0,1},{1,0},{2,3},{3,2},{4,5},{5,4},{6,7},{7,6},{8,9},{9,8},{10,11... | collective-permute-start | bytes 417800 | tf_op jit(solution)/shard_map/ppermute | solution.py:244
  45.0 0.0 collective-permute-done.2.refs_3_
  45.0 1.0 collective-permute-done.1.refs_2_
  46.0 0.3 collective-permute-done.3.refs_4_
  46.3 0.0 copy-done
  46.3 2.9 %attend.1 = (bf16[1,128,2048]{2,1,0:T(8,128)(2,1)}, bf16[8,128,256]{2,1,0:T(8,128)(2,1)S(1)}) custom-call(s32[1]{0:T(128)} %bitcast.index_ref, bf16[1,128,2048]{2,1,0:T(8,128)(2,1)S(1)} %copy-done, bf16[136,512]{1,0:T(8,128)(2,1)S(1)} %copy-done.1, bf16[136,512]{1,0:T(8,128)(2,1)S(1)} %collective-permute-done.refs_1_, ...), custom_call_target="tpu_custom_call" | custom-call | flops 700000000 | bytes 3145728 | tf_op jit(solution)/shard_map/attend/pallas_call | solution.py:147
  49.3 11.9 %all_to_all.21.mixed_ref = bf16[8,128,256]{2,1,0:T(8,128)(2,1)S(1)} all-to-all(bf16[8,128,256]{2,1,0:T(8,128)(2,1)S(1)} %get-tuple-element.9), channel_id=1, replica_groups=mesh['x'=4,'zl'=4,'y'=8,'zh'=2,'core'=2] {'x','core'}, dimensions={0} | all-to-all | bytes 1048576 | tf_op jit(solution)/shard_map/all_to_all | solution.py:253
  61.1 0.0 collective-permute-done.4.far_ref
  61.1 0.7 weight_term.1
  61.9 37.2 %all_to_all.22.terms_ref = bf16[128,16,128]{2,1,0:T(8,128)(2,1)S(1)} all-to-all(bf16[128,16,128]{2,1,0:T(8,128)(2,1)S(1)} %bitcast.3), channel_id=1, replica_groups=mesh['x'=4,'zl'=4,'y'=8,'zh'=2,'core'=2] {'zl','core','zh','y'}, dimensions={0} | all-to-all | bytes 1048576 | tf_op jit(solution)/shard_map/all_to_all | solution.py:255
  99.1 0.1 total.1
  99.2 10.0 %all_to_all.23.parts_ref = bf16[16,2,16,128]{3,2,1,0:T(8,128)(2,1)S(1)} all-to-all(bf16[16,2,16,128]{3,2,1,0:T(8,128)(2,1)S(1)} %total.1), channel_id=1, replica_groups=mesh['x'=4,'zl'=4,'y'=8,'zh'=2,'core'=2] {'x','zl'}, dimensions={0} | all-to-all | bytes 262144 | tf_op jit(solution)/shard_map/all_to_all | solution.py:258
  109.2 0.7 assemble.1
Async XLA Ops:
  2.9 23.3 %copy-start.1 = (bf16[136,512]{1,0:T(8,128)(2,1)S(1)}, bf16[136,512]{1,0:T(8,128)(2,1)}, u32[]{:S(2)}) copy-start(bf16[136,512]{1,0:T(8,128)(2,1)} %get-tuple-element.6.refs_0_) | copy-start | bytes 417796
  2.9 43.5 %copy-start = (bf16[1,128,2048]{2,1,0:T(8,128)(2,1)S(1)}, bf16[1,128,2048]{2,1,0:T(8,128)(2,1)}, u32[]{:S(2)}) copy-start(bf16[1,128,2048]{2,1,0:T(8,128)(2,1)} %query_ref.1) | copy-start | bytes 1572868
  17.6 43.5 %collective-permute-start.4 = (bf16[4,1024,128]{2,1,0:T(8,128)(2,1)S(1)}, bf16[4,1024,128]{2,1,0:T(8,128)(2,1)S(1)}, u32[]{:S(2)}, u32[]{:S(2)}) collective-permute-start(bf16[4,1024,128]{2,1,0:T(8,128)(2,1)S(1)} %all_to_all.20.near_ref), channel_id=1, source_target_pairs={{0,1},{1,0},{2,3},{3,2},{4,5},{5,4},{6,7},{7,6},{8,9},{9,8},{10,11... | collective-permute-start | bytes 3145736 | tf_op jit(solution)/shard_map/ppermute | solution.py:244
  26.2 16.9 %collective-permute-start = (bf16[136,512]{1,0:T(8,128)(2,1)S(1)}, bf16[136,512]{1,0:T(8,128)(2,1)S(1)}, u32[]{:S(2)}, u32[]{:S(2)}) collective-permute-start(bf16[136,512]{1,0:T(8,128)(2,1)S(1)} %copy-done.1), channel_id=1, source_target_pairs={{0,2},{1,3},{2,4},{3,5},{4,6},{5,7},{6,8},{7,9},{8,10},{9,11},{10,... | collective-permute-start | bytes 417800 | tf_op jit(solution)/shard_map/ppermute | solution.py:246
  36.5 8.6 %collective-permute-start.2 = (bf16[136,512]{1,0:T(8,128)(2,1)S(1)}, bf16[136,512]{1,0:T(8,128)(2,1)S(1)}, u32[]{:S(2)}, u32[]{:S(2)}) collective-permute-start(bf16[136,512]{1,0:T(8,128)(2,1)S(1)} %copy-done.1), channel_id=1, source_target_pairs={{0,1},{1,4},{2,3},{3,6},{4,5},{5,8},{6,7},{7,10},{8,9},{9,12},{10,... | collective-permute-start | bytes 417800 | tf_op jit(solution)/shard_map/ppermute | solution.py:248
  39.9 6.2 %collective-permute-start.1 = (bf16[136,512]{1,0:T(8,128)(2,1)S(1)}, bf16[136,512]{1,0:T(8,128)(2,1)S(1)}, u32[]{:S(2)}, u32[]{:S(2)}) collective-permute-start(bf16[136,512]{1,0:T(8,128)(2,1)S(1)} %copy-done.1), channel_id=1, source_target_pairs={{0,4},{1,5},{2,6},{3,7},{4,8},{5,9},{6,10},{7,11},{8,12},{9,13},{1... | collective-permute-start | bytes 417800 | tf_op jit(solution)/shard_map/ppermute | solution.py:249
  43.1 3.3 %collective-permute-start.3 = (bf16[136,512]{1,0:T(8,128)(2,1)S(1)}, bf16[136,512]{1,0:T(8,128)(2,1)S(1)}, u32[]{:S(2)}, u32[]{:S(2)}) collective-permute-start(bf16[136,512]{1,0:T(8,128)(2,1)S(1)} %collective-permute-done.refs_1_), channel_id=1, source_target_pairs={{0,1},{1,0},{2,3},{3,2},{4,5},{5,4},{6,7},{7,6},{8,9},{9,8},{10,11... | collective-permute-start | bytes 417800 | tf_op jit(solution)/shard_map/ppermute | solution.py:244

commit v9 on v8

--- a/solution.py
+++ b/solution.py
@@ -24,9 +24,10 @@
 AXES = ("x", "zl", "y", "zh", "core")
 SIZES = (4, 4, 8, 2, 2)
 REP = ("x", "zl")
+COPIES = ("zl", "x")
 SHARD = ("y", "zh", "core")
 GROUP = ("x", "core")
-REST = ("zl", "core", "zh", "y")
+REST = ("core", "zl", "zh", "y")
 N_X = 4
 N_ZL = 4
 N_Y = 8
@@ -174,13 +175,13 @@
             columns = slice(head * HD, (head + 1) * HD)
             for to_core in range(2):
                 for zh in range(N_ZH):
-                    out_ref[2 * part + head, to_core, zh] = term[:, zh, to_core, part, :, columns]
+                    out_ref[to_core, 2 * part + head, zh] = term[:, zh, to_core, part, :, columns]
 
 
 def weight_term(core, near, far, mixed):
     return pl.pallas_call(
         term_kernel,
-        out_shape=jax.ShapeDtypeStruct((N_ZL, 2, N_ZH, N_Y, PART, HD), jnp.bfloat16),
+        out_shape=jax.ShapeDtypeStruct((2, N_ZL, N_ZH, N_Y, PART, HD), jnp.bfloat16),
         in_specs=[pl.BlockSpec(memory_space=pltpu.SMEM)] + vmem_specs(3),
         out_specs=vmem_specs(1)[0],
         name="weight_term",
@@ -192,9 +193,9 @@
 
 
 def total_kernel(terms_ref, out_ref):
-    terms = terms_ref[...].reshape(N_ZL, 2, N_YZ, PART, HD)
+    terms = terms_ref[...].reshape(2, N_ZL * N_YZ, PART, HD)
     for core in range(2):
-        own = terms[:, core].reshape(N_ZL * N_YZ, PART, HD).astype(jnp.float32)
+        own = terms[core].astype(jnp.float32)
         total = jnp.sum(own, axis=0).astype(jnp.bfloat16)
         out_ref[:, core] = jnp.broadcast_to(total[None], (N_REP, PART, HD))
 
@@ -216,7 +217,7 @@
             for half in range(2):
                 for core in range(2):
                     head = 4 * x + 2 * core + half
-                    piece = parts_ref[4 * x + 2 * part + half, core].astype(jnp.float32)
+                    piece = parts_ref[(2 * part + half) * N_X + x, core].astype(jnp.float32)
                     rows = slice(part * PART, (part + 1) * PART)
                     out_ref[rows, head * HD : (head + 1) * HD] = piece
 
@@ -255,7 +256,7 @@
     terms = lax.all_to_all(
         term.reshape(N_SHARD * N_ZL, PART, HD), REST, 0, 0, tiled=True
     )
-    parts = lax.all_to_all(total(terms), REP, 0, 0, tiled=True)
+    parts = lax.all_to_all(total(terms), COPIES, 0, 0, tiled=True)
     return attention, assemble(parts)
 
 

time: 110 us -> 110 us (level)
  the two profiles are of different devices: /device:TPU:1 before, /device:TPU:2 now
where the time goes in v9:
time: 110 us
  blocking collectives  80.4 us (73%)
  starting transfers between devices  21.2 us (19%)
  Pallas kernels  6.68 us (6%)
    all_to_all x1, blocking collectives, step(): lax.all_to_all(term.reshape(N_SHARD * N_ZL, PART, HD), REST, 0, 0, tiled=...  35.3 us
    all_to_all x1, blocking collectives, step(): near_grads = lax.all_to_all(grad_t, 'x', 0, 0, tiled=True)  18.9 us
    all_to_all x1, blocking collectives, step(): parts = lax.all_to_all(total(terms), COPIES, 0, 0, tiled=True)  13.4 us
    all_to_all x1, blocking collectives, step(): mixed = lax.all_to_all(heads, GROUP, 0, 0, tiled=True)  12.8 us
    ppermute x1, starting transfers between devices, step(): two = lax.ppermute(pay, SHARD, back(lambda s: 2))  10.6 us
    ppermute x2, starting transfers between devices, swap(): return lax.ppermute(value, 'core', [(0, 1), (1, 0)])  5.01 us
    ppermute x1, starting transfers between devices, step(): four = lax.ppermute(pay, SHARD, back(lambda s: 4))  3.48 us
    pallas_call x1, Pallas kernels, attend(): pl.pallas_call(attend_kernel, out_shape=(jax.ShapeDtypeStruct((1, TOK, HE...  2.94 us
  transfers between devices with their start and end apart: 5, of which 2 were waited for; matrix products, arithmetic and copies ran while one was open for 0% of the time, Pallas kernels for 3%

profile of v9, /device:TPU:2, one launch (start us, length us, event | category | flops | bytes accessed | tf_op | source)
XLA Modules:
  0.0 110.0 jit_solution(9516116953812784467)
XLA Ops:
  0.6 2.2 %pack.1 = (bf16[136,512]{1,0:T(8,128)(2,1)}, bf16[4,1024,128]{2,1,0:T(8,128)(2,1)}) custom-call(bf16[1,128,256]{2,1,0:T(8,128)(2,1)} %refs_0_.1, bf16[1,128,256]{2,1,0:T(8,128)(2,1)} %refs_1_.1, s32[1,128]{1,0:T(1,128)} %refs_2_.1, bf16[1,128,1024]{2,1,0:T(8,128)(2,1)} %refs_3_.1), custom_call_target="tpu_custom_call" | custom-call | bytes 1048576 | tf_op jit(solution)/shard_map/pack/pallas_call | solution.py:82
  2.9 0.0 copy-start.1
  2.9 0.0 copy-start
  2.9 18.9 %all_to_all.20.near_ref = bf16[4,1024,128]{2,1,0:T(8,128)(2,1)S(1)} all-to-all(bf16[4,1024,128]{2,1,0:T(8,128)(2,1)} %get-tuple-element.8), channel_id=1, replica_groups=mesh['x'=4,'zl'=4,'y'=8,'zh'=2,'core'=2] {'x'}, dimensions={0} | all-to-all | bytes 2097152 | tf_op jit(solution)/shard_map/all_to_all | solution.py:248
  21.8 1.9 %collective-permute-start.4 = (bf16[4,1024,128]{2,1,0:T(8,128)(2,1)S(1)}, bf16[4,1024,128]{2,1,0:T(8,128)(2,1)S(1)}, u32[]{:S(2)}, u32[]{:S(2)}) collective-permute-start(bf16[4,1024,128]{2,1,0:T(8,128)(2,1)S(1)} %all_to_all.20.near_ref), channel_id=1, source_target_pairs={{0,1},{1,0},{2,3},{3,2},{4,5},{5,4},{6,7},{7,6},{8,9},{9,8},{10,11... | collective-permute-start | bytes 3145736 | tf_op jit(solution)/shard_map/ppermute | solution.py:245
  23.7 0.0 copy-done.1
  23.7 10.6 %collective-permute-start = (bf16[136,512]{1,0:T(8,128)(2,1)S(1)}, bf16[136,512]{1,0:T(8,128)(2,1)S(1)}, u32[]{:S(2)}, u32[]{:S(2)}) collective-permute-start(bf16[136,512]{1,0:T(8,128)(2,1)S(1)} %copy-done.1), channel_id=1, source_target_pairs={{0,2},{1,3},{2,4},{3,5},{4,6},{5,7},{6,8},{7,9},{8,10},{9,11},{10,... | collective-permute-start | bytes 417800 | tf_op jit(solution)/shard_map/ppermute | solution.py:247
  34.3 2.1 %collective-permute-start.2 = (bf16[136,512]{1,0:T(8,128)(2,1)S(1)}, bf16[136,512]{1,0:T(8,128)(2,1)S(1)}, u32[]{:S(2)}, u32[]{:S(2)}) collective-permute-start(bf16[136,512]{1,0:T(8,128)(2,1)S(1)} %copy-done.1), channel_id=1, source_target_pairs={{0,1},{1,4},{2,3},{3,6},{4,5},{5,8},{6,7},{7,10},{8,9},{9,12},{10,... | collective-permute-start | bytes 417800 | tf_op jit(solution)/shard_map/ppermute | solution.py:249
  36.5 3.5 %collective-permute-start.1 = (bf16[136,512]{1,0:T(8,128)(2,1)S(1)}, bf16[136,512]{1,0:T(8,128)(2,1)S(1)}, u32[]{:S(2)}, u32[]{:S(2)}) collective-permute-start(bf16[136,512]{1,0:T(8,128)(2,1)S(1)} %copy-done.1), channel_id=1, source_target_pairs={{0,4},{1,5},{2,6},{3,7},{4,8},{5,9},{6,10},{7,11},{8,12},{9,13},{1... | collective-permute-start | bytes 417800 | tf_op jit(solution)/shard_map/ppermute | solution.py:250
  40.0 0.0 collective-permute-done.refs_1_
  40.0 3.1 %collective-permute-start.3 = (bf16[136,512]{1,0:T(8,128)(2,1)S(1)}, bf16[136,512]{1,0:T(8,128)(2,1)S(1)}, u32[]{:S(2)}, u32[]{:S(2)}) collective-permute-start(bf16[136,512]{1,0:T(8,128)(2,1)S(1)} %collective-permute-done.refs_1_), channel_id=1, source_target_pairs={{0,1},{1,0},{2,3},{3,2},{4,5},{5,4},{6,7},{7,6},{8,9},{9,8},{10,11... | collective-permute-start | bytes 417800 | tf_op jit(solution)/shard_map/ppermute | solution.py:245
  43.1 0.0 collective-permute-done.2.refs_3_
  43.1 0.4 collective-permute-done.1.refs_2_
  43.5 0.6 collective-permute-done.3.refs_4_
  44.1 0.0 copy-done
  44.1 2.9 %attend.1 = (bf16[1,128,2048]{2,1,0:T(8,128)(2,1)}, bf16[8,128,256]{2,1,0:T(8,128)(2,1)S(1)}) custom-call(s32[1]{0:T(128)} %bitcast.index_ref, bf16[1,128,2048]{2,1,0:T(8,128)(2,1)S(1)} %copy-done, bf16[136,512]{1,0:T(8,128)(2,1)S(1)} %copy-done.1, bf16[136,512]{1,0:T(8,128)(2,1)S(1)} %collective-permute-done.refs_1_, ...), custom_call_target="tpu_custom_call" | custom-call | flops 700000000 | bytes 3145728 | tf_op jit(solution)/shard_map/attend/pallas_call | solution.py:148
  47.0 12.8 %all_to_all.21.mixed_ref = bf16[8,128,256]{2,1,0:T(8,128)(2,1)S(1)} all-to-all(bf16[8,128,256]{2,1,0:T(8,128)(2,1)S(1)} %get-tuple-element.9), channel_id=1, replica_groups=mesh['x'=4,'zl'=4,'y'=8,'zh'=2,'core'=2] {'x','core'}, dimensions={0} | all-to-all | bytes 1048576 | tf_op jit(solution)/shard_map/all_to_all | solution.py:254
  59.8 0.0 collective-permute-done.4.far_ref
  59.8 0.7 weight_term.1
  60.5 35.3 %all_to_all.22.terms_ref = bf16[128,16,128]{2,1,0:T(8,128)(2,1)S(1)} all-to-all(bf16[128,16,128]{2,1,0:T(8,128)(2,1)S(1)} %bitcast.3), channel_id=1, replica_groups=mesh['x'=4,'zl'=4,'y'=8,'zh'=2,'core'=2] {'core','zl','zh','y'}, dimensions={0} | all-to-all | bytes 1048576 | tf_op jit(solution)/shard_map/all_to_all | solution.py:256
  95.8 0.1 total.1
  95.9 13.4 %all_to_all.23.parts_ref = bf16[16,2,16,128]{3,2,1,0:T(8,128)(2,1)S(1)} all-to-all(bf16[16,2,16,128]{3,2,1,0:T(8,128)(2,1)S(1)} %total.1), channel_id=1, replica_groups=mesh['x'=4,'zl'=4,'y'=8,'zh'=2,'core'=2] {'zl','x'}, dimensions={0} | all-to-all | bytes 262144 | tf_op jit(solution)/shard_map/all_to_all | solution.py:259
  109.3 0.7 assemble.1
Async XLA Ops:
  2.9 20.9 %copy-start.1 = (bf16[136,512]{1,0:T(8,128)(2,1)S(1)}, bf16[136,512]{1,0:T(8,128)(2,1)}, u32[]{:S(2)}) copy-start(bf16[136,512]{1,0:T(8,128)(2,1)} %get-tuple-element.6.refs_0_) | copy-start | bytes 417796
  2.9 41.2 %copy-start = (bf16[1,128,2048]{2,1,0:T(8,128)(2,1)S(1)}, bf16[1,128,2048]{2,1,0:T(8,128)(2,1)}, u32[]{:S(2)}) copy-start(bf16[1,128,2048]{2,1,0:T(8,128)(2,1)} %query_ref.1) | copy-start | bytes 1572868
  21.8 38.0 %collective-permute-start.4 = (bf16[4,1024,128]{2,1,0:T(8,128)(2,1)S(1)}, bf16[4,1024,128]{2,1,0:T(8,128)(2,1)S(1)}, u32[]{:S(2)}, u32[]{:S(2)}) collective-permute-start(bf16[4,1024,128]{2,1,0:T(8,128)(2,1)S(1)} %all_to_all.20.near_ref), channel_id=1, source_target_pairs={{0,1},{1,0},{2,3},{3,2},{4,5},{5,4},{6,7},{7,6},{8,9},{9,8},{10,11... | collective-permute-start | bytes 3145736 | tf_op jit(solution)/shard_map/ppermute | solution.py:245
  23.7 16.2 %collective-permute-start = (bf16[136,512]{1,0:T(8,128)(2,1)S(1)}, bf16[136,512]{1,0:T(8,128)(2,1)S(1)}, u32[]{:S(2)}, u32[]{:S(2)}) collective-permute-start(bf16[136,512]{1,0:T(8,128)(2,1)S(1)} %copy-done.1), channel_id=1, source_target_pairs={{0,2},{1,3},{2,4},{3,5},{4,6},{5,7},{6,8},{7,9},{8,10},{9,11},{10,... | collective-permute-start | bytes 417800 | tf_op jit(solution)/shard_map/ppermute | solution.py:247
  34.3 8.8 %collective-permute-start.2 = (bf16[136,512]{1,0:T(8,128)(2,1)S(1)}, bf16[136,512]{1,0:T(8,128)(2,1)S(1)}, u32[]{:S(2)}, u32[]{:S(2)}) collective-permute-start(bf16[136,512]{1,0:T(8,128)(2,1)S(1)} %copy-done.1), channel_id=1, source_target_pairs={{0,1},{1,4},{2,3},{3,6},{4,5},{5,8},{6,7},{7,10},{8,9},{9,12},{10,... | collective-permute-start | bytes 417800 | tf_op jit(solution)/shard_map/ppermute | solution.py:249
  36.5 7.0 %collective-permute-start.1 = (bf16[136,512]{1,0:T(8,128)(2,1)S(1)}, bf16[136,512]{1,0:T(8,128)(2,1)S(1)}, u32[]{:S(2)}, u32[]{:S(2)}) collective-permute-start(bf16[136,512]{1,0:T(8,128)(2,1)S(1)} %copy-done.1), channel_id=1, source_target_pairs={{0,4},{1,5},{2,6},{3,7},{4,8},{5,9},{6,10},{7,11},{8,12},{9,13},{1... | collective-permute-start | bytes 417800 | tf_op jit(solution)/shard_map/ppermute | solution.py:250
  40.0 4.1 %collective-permute-start.3 = (bf16[136,512]{1,0:T(8,128)(2,1)S(1)}, bf16[136,512]{1,0:T(8,128)(2,1)S(1)}, u32[]{:S(2)}, u32[]{:S(2)}) collective-permute-start(bf16[136,512]{1,0:T(8,128)(2,1)S(1)} %collective-permute-done.refs_1_), channel_id=1, source_target_pairs={{0,1},{1,0},{2,3},{3,2},{4,5},{5,4},{6,7},{7,6},{8,9},{9,8},{10,11... | collective-permute-start | bytes 417800 | tf_op jit(solution)/shard_map/ppermute | solution.py:245

commit v10 on v9

--- a/solution.py
+++ b/solution.py
@@ -24,7 +24,7 @@
 AXES = ("x", "zl", "y", "zh", "core")
 SIZES = (4, 4, 8, 2, 2)
 REP = ("x", "zl")
-COPIES = ("zl", "x")
+
 SHARD = ("y", "zh", "core")
 GROUP = ("x", "core")
 REST = ("core", "zl", "zh", "y")
@@ -217,7 +217,7 @@
             for half in range(2):
                 for core in range(2):
                     head = 4 * x + 2 * core + half
-                    piece = parts_ref[(2 * part + half) * N_X + x, core].astype(jnp.float32)
+                    piece = parts_ref[4 * x + 2 * part + half, core].astype(jnp.float32)
                     rows = slice(part * PART, (part + 1) * PART)
                     out_ref[rows, head * HD : (head + 1) * HD] = piece
 
@@ -256,7 +256,7 @@
     terms = lax.all_to_all(
         term.reshape(N_SHARD * N_ZL, PART, HD), REST, 0, 0, tiled=True
     )
-    parts = lax.all_to_all(total(terms), COPIES, 0, 0, tiled=True)
+    parts = lax.all_to_all(total(terms), REP, 0, 0, tiled=True)
     return attention, assemble(parts)
 
 

time: 110 us -> 110 us (level)
  no operation moved by 1% of the time
where the time goes in v10:
time: 110 us; the launch traced here: 109 us
  blocking collectives  79.9 us (73%)
  starting transfers between devices  21.2 us (19%)
  Pallas kernels  6.68 us (6%)
    all_to_all x1, blocking collectives, step(): lax.all_to_all(term.reshape(N_SHARD * N_ZL, PART, HD), REST, 0, 0, tiled=...  35.3 us
    all_to_all x1, blocking collectives, step(): near_grads = lax.all_to_all(grad_t, 'x', 0, 0, tiled=True)  18.9 us
    all_to_all x1, blocking collectives, step(): parts = lax.all_to_all(total(terms), REP, 0, 0, tiled=True)  12.9 us
    all_to_all x1, blocking collectives, step(): mixed = lax.all_to_all(heads, GROUP, 0, 0, tiled=True)  12.8 us
    ppermute x1, starting transfers between devices, step(): two = lax.ppermute(pay, SHARD, back(lambda s: 2))  10.6 us
    ppermute x2, starting transfers between devices, swap(): return lax.ppermute(value, 'core', [(0, 1), (1, 0)])  5.01 us
    ppermute x1, starting transfers between devices, step(): four = lax.ppermute(pay, SHARD, back(lambda s: 4))  3.48 us
    pallas_call x1, Pallas kernels, attend(): pl.pallas_call(attend_kernel, out_shape=(jax.ShapeDtypeStruct((1, TOK, HE...  2.94 us
  transfers between devices with their start and end apart: 5, of which 2 were waited for; matrix products, arithmetic and copies ran while one was open for 0% of the time, Pallas kernels for 3%

profile of v10, /device:TPU:2, one launch (start us, length us, event | category | flops | bytes accessed | tf_op | source)
XLA Modules:
  0.0 109.5 jit_solution(5909170110570135185)
XLA Ops:
  0.6 2.2 %pack.1 = (bf16[136,512]{1,0:T(8,128)(2,1)}, bf16[4,1024,128]{2,1,0:T(8,128)(2,1)}) custom-call(bf16[1,128,256]{2,1,0:T(8,128)(2,1)} %refs_0_.1, bf16[1,128,256]{2,1,0:T(8,128)(2,1)} %refs_1_.1, s32[1,128]{1,0:T(1,128)} %refs_2_.1, bf16[1,128,1024]{2,1,0:T(8,128)(2,1)} %refs_3_.1), custom_call_target="tpu_custom_call" | custom-call | bytes 1048576 | tf_op jit(solution)/shard_map/pack/pallas_call | solution.py:82
  2.9 0.0 copy-start.1
  2.9 0.0 copy-start
  2.9 18.9 %all_to_all.20.near_ref = bf16[4,1024,128]{2,1,0:T(8,128)(2,1)S(1)} all-to-all(bf16[4,1024,128]{2,1,0:T(8,128)(2,1)} %get-tuple-element.8), channel_id=1, replica_groups=mesh['x'=4,'zl'=4,'y'=8,'zh'=2,'core'=2] {'x'}, dimensions={0} | all-to-all | bytes 2097152 | tf_op jit(solution)/shard_map/all_to_all | solution.py:248
  21.8 1.9 %collective-permute-start.4 = (bf16[4,1024,128]{2,1,0:T(8,128)(2,1)S(1)}, bf16[4,1024,128]{2,1,0:T(8,128)(2,1)S(1)}, u32[]{:S(2)}, u32[]{:S(2)}) collective-permute-start(bf16[4,1024,128]{2,1,0:T(8,128)(2,1)S(1)} %all_to_all.20.near_ref), channel_id=1, source_target_pairs={{0,1},{1,0},{2,3},{3,2},{4,5},{5,4},{6,7},{7,6},{8,9},{9,8},{10,11... | collective-permute-start | bytes 3145736 | tf_op jit(solution)/shard_map/ppermute | solution.py:245
  23.7 0.0 copy-done.1
  23.7 10.6 %collective-permute-start = (bf16[136,512]{1,0:T(8,128)(2,1)S(1)}, bf16[136,512]{1,0:T(8,128)(2,1)S(1)}, u32[]{:S(2)}, u32[]{:S(2)}) collective-permute-start(bf16[136,512]{1,0:T(8,128)(2,1)S(1)} %copy-done.1), channel_id=1, source_target_pairs={{0,2},{1,3},{2,4},{3,5},{4,6},{5,7},{6,8},{7,9},{8,10},{9,11},{10,... | collective-permute-start | bytes 417800 | tf_op jit(solution)/shard_map/ppermute | solution.py:247
  34.3 2.1 %collective-permute-start.2 = (bf16[136,512]{1,0:T(8,128)(2,1)S(1)}, bf16[136,512]{1,0:T(8,128)(2,1)S(1)}, u32[]{:S(2)}, u32[]{:S(2)}) collective-permute-start(bf16[136,512]{1,0:T(8,128)(2,1)S(1)} %copy-done.1), channel_id=1, source_target_pairs={{0,1},{1,4},{2,3},{3,6},{4,5},{5,8},{6,7},{7,10},{8,9},{9,12},{10,... | collective-permute-start | bytes 417800 | tf_op jit(solution)/shard_map/ppermute | solution.py:249
  36.5 3.5 %collective-permute-start.1 = (bf16[136,512]{1,0:T(8,128)(2,1)S(1)}, bf16[136,512]{1,0:T(8,128)(2,1)S(1)}, u32[]{:S(2)}, u32[]{:S(2)}) collective-permute-start(bf16[136,512]{1,0:T(8,128)(2,1)S(1)} %copy-done.1), channel_id=1, source_target_pairs={{0,4},{1,5},{2,6},{3,7},{4,8},{5,9},{6,10},{7,11},{8,12},{9,13},{1... | collective-permute-start | bytes 417800 | tf_op jit(solution)/shard_map/ppermute | solution.py:250
  40.0 0.0 collective-permute-done.refs_1_
  40.0 3.1 %collective-permute-start.3 = (bf16[136,512]{1,0:T(8,128)(2,1)S(1)}, bf16[136,512]{1,0:T(8,128)(2,1)S(1)}, u32[]{:S(2)}, u32[]{:S(2)}) collective-permute-start(bf16[136,512]{1,0:T(8,128)(2,1)S(1)} %collective-permute-done.refs_1_), channel_id=1, source_target_pairs={{0,1},{1,0},{2,3},{3,2},{4,5},{5,4},{6,7},{7,6},{8,9},{9,8},{10,11... | collective-permute-start | bytes 417800 | tf_op jit(solution)/shard_map/ppermute | solution.py:245
  43.1 0.0 collective-permute-done.2.refs_3_
  43.1 0.4 collective-permute-done.1.refs_2_
  43.5 0.6 collective-permute-done.3.refs_4_
  44.1 0.0 copy-done
  44.1 2.9 %attend.1 = (bf16[1,128,2048]{2,1,0:T(8,128)(2,1)}, bf16[8,128,256]{2,1,0:T(8,128)(2,1)S(1)}) custom-call(s32[1]{0:T(128)} %bitcast.index_ref, bf16[1,128,2048]{2,1,0:T(8,128)(2,1)S(1)} %copy-done, bf16[136,512]{1,0:T(8,128)(2,1)S(1)} %copy-done.1, bf16[136,512]{1,0:T(8,128)(2,1)S(1)} %collective-permute-done.refs_1_, ...), custom_call_target="tpu_custom_call" | custom-call | flops 700000000 | bytes 3145728 | tf_op jit(solution)/shard_map/attend/pallas_call | solution.py:148
  47.0 12.8 %all_to_all.21.mixed_ref = bf16[8,128,256]{2,1,0:T(8,128)(2,1)S(1)} all-to-all(bf16[8,128,256]{2,1,0:T(8,128)(2,1)S(1)} %get-tuple-element.9), channel_id=1, replica_groups=mesh['x'=4,'zl'=4,'y'=8,'zh'=2,'core'=2] {'x','core'}, dimensions={0} | all-to-all | bytes 1048576 | tf_op jit(solution)/shard_map/all_to_all | solution.py:254
  59.8 0.0 collective-permute-done.4.far_ref
  59.8 0.7 weight_term.1
  60.5 35.3 %all_to_all.22.terms_ref = bf16[128,16,128]{2,1,0:T(8,128)(2,1)S(1)} all-to-all(bf16[128,16,128]{2,1,0:T(8,128)(2,1)S(1)} %bitcast.3), channel_id=1, replica_groups=mesh['x'=4,'zl'=4,'y'=8,'zh'=2,'core'=2] {'core','zl','zh','y'}, dimensions={0} | all-to-all | bytes 1048576 | tf_op jit(solution)/shard_map/all_to_all | solution.py:256
  95.8 0.1 total.1
  95.9 12.9 %all_to_all.23.parts_ref = bf16[16,2,16,128]{3,2,1,0:T(8,128)(2,1)S(1)} all-to-all(bf16[16,2,16,128]{3,2,1,0:T(8,128)(2,1)S(1)} %total.1), channel_id=1, replica_groups=mesh['x'=4,'zl'=4,'y'=8,'zh'=2,'core'=2] {'x','zl'}, dimensions={0} | all-to-all | bytes 262144 | tf_op jit(solution)/shard_map/all_to_all | solution.py:259
  108.7 0.7 assemble.1
Async XLA Ops:
  2.9 20.9 %copy-start.1 = (bf16[136,512]{1,0:T(8,128)(2,1)S(1)}, bf16[136,512]{1,0:T(8,128)(2,1)}, u32[]{:S(2)}) copy-start(bf16[136,512]{1,0:T(8,128)(2,1)} %get-tuple-element.6.refs_0_) | copy-start | bytes 417796
  2.9 41.2 %copy-start = (bf16[1,128,2048]{2,1,0:T(8,128)(2,1)S(1)}, bf16[1,128,2048]{2,1,0:T(8,128)(2,1)}, u32[]{:S(2)}) copy-start(bf16[1,128,2048]{2,1,0:T(8,128)(2,1)} %query_ref.1) | copy-start | bytes 1572868
  21.8 38.0 %collective-permute-start.4 = (bf16[4,1024,128]{2,1,0:T(8,128)(2,1)S(1)}, bf16[4,1024,128]{2,1,0:T(8,128)(2,1)S(1)}, u32[]{:S(2)}, u32[]{:S(2)}) collective-permute-start(bf16[4,1024,128]{2,1,0:T(8,128)(2,1)S(1)} %all_to_all.20.near_ref), channel_id=1, source_target_pairs={{0,1},{1,0},{2,3},{3,2},{4,5},{5,4},{6,7},{7,6},{8,9},{9,8},{10,11... | collective-permute-start | bytes 3145736 | tf_op jit(solution)/shard_map/ppermute | solution.py:245
  23.7 16.2 %collective-permute-start = (bf16[136,512]{1,0:T(8,128)(2,1)S(1)}, bf16[136,512]{1,0:T(8,128)(2,1)S(1)}, u32[]{:S(2)}, u32[]{:S(2)}) collective-permute-start(bf16[136,512]{1,0:T(8,128)(2,1)S(1)} %copy-done.1), channel_id=1, source_target_pairs={{0,2},{1,3},{2,4},{3,5},{4,6},{5,7},{6,8},{7,9},{8,10},{9,11},{10,... | collective-permute-start | bytes 417800 | tf_op jit(solution)/shard_map/ppermute | solution.py:247
  34.3 8.8 %collective-permute-start.2 = (bf16[136,512]{1,0:T(8,128)(2,1)S(1)}, bf16[136,512]{1,0:T(8,128)(2,1)S(1)}, u32[]{:S(2)}, u32[]{:S(2)}) collective-permute-start(bf16[136,512]{1,0:T(8,128)(2,1)S(1)} %copy-done.1), channel_id=1, source_target_pairs={{0,1},{1,4},{2,3},{3,6},{4,5},{5,8},{6,7},{7,10},{8,9},{9,12},{10,... | collective-permute-start | bytes 417800 | tf_op jit(solution)/shard_map/ppermute | solution.py:249
  36.5 7.0 %collective-permute-start.1 = (bf16[136,512]{1,0:T(8,128)(2,1)S(1)}, bf16[136,512]{1,0:T(8,128)(2,1)S(1)}, u32[]{:S(2)}, u32[]{:S(2)}) collective-permute-start(bf16[136,512]{1,0:T(8,128)(2,1)S(1)} %copy-done.1), channel_id=1, source_target_pairs={{0,4},{1,5},{2,6},{3,7},{4,8},{5,9},{6,10},{7,11},{8,12},{9,13},{1... | collective-permute-start | bytes 417800 | tf_op jit(solution)/shard_map/ppermute | solution.py:250
  40.0 4.1 %collective-permute-start.3 = (bf16[136,512]{1,0:T(8,128)(2,1)S(1)}, bf16[136,512]{1,0:T(8,128)(2,1)S(1)}, u32[]{:S(2)}, u32[]{:S(2)}) collective-permute-start(bf16[136,512]{1,0:T(8,128)(2,1)S(1)} %collective-permute-done.refs_1_), channel_id=1, source_target_pairs={{0,1},{1,0},{2,3},{3,2},{4,5},{5,4},{6,7},{7,6},{8,9},{9,8},{10,11... | collective-permute-start | bytes 417800 | tf_op jit(solution)/shard_map/ppermute | solution.py:245
